TPU v7x, 512 devices: a whole 4x8x8 slice. The times are simulated.
512 devices in a mesh: lat: 16 (over y, core), lon: 32 (over x, z).
Axes of the slice: x: 4, y: 8, z: 8, core: 2. Of those that a mesh axis runs over, the one named last changes fastest.
Arguments:
- background_expectation: float32 [3, 128, 4096], P(None, 'lat', 'lon'), may hold values from -6 to 6
- factor: float32 [32, 3, 128, 4096], P(None, None, 'lat', 'lon'), may hold values from -6 to 6
- average_thickness: float32 [128, 4096], P('lat', 'lon'), may hold values from 1 to 2
- obs_cells: int32 [131072], P(('lat', 'lon')), may hold values from 0 to 1023
- obs_count: int32 [512], P(('lat', 'lon')), may hold values from 64 to 256, as said below
- obs_values: float32 [131072], P(('lat', 'lon')), may hold values from -384 to 384
- obs_error: float32 [131072], P(('lat', 'lon')), may hold values from 20 to 200
Outputs:
- updated_expectation: float32 [3, 128, 4096], P(None, 'lat', 'lon')
- analysis_factor: float32 [32, 3, 128, 4096], P(None, None, 'lat', 'lon')
Inputs may be any that keep to these rules, and one draw needn't show every extreme that they name: `obs_cells`: each entry is a cell of the block of the device that holds the slot, row-major over its 8 x 128 cells. Device d uses its first obs_count[d] slots; some device uses all 256.
All inputs are finite; a program needn't handle non-finite values.
Results may differ from a plain program's by a relative error of at most 0.00027.
Values sent between devices are 32-bit elements; how exact they have to be, the bound alone decides.
No kernel may reach another device: no remote copies, remote signals or barrier semaphores. Data moves between devices by JAX's collectives and lax.ppermute only.
A program may use at most 64 MiB of HBM per device.

v0:
```python
import jax
import jax.numpy as jnp
from jax import lax
from jax.sharding import PartitionSpec as P

STEPS = 4


TIME_STEP = 0.9
ROTATION = 0.25


def with_halo(block, sides, width, periodic):
    for axis, dim in sides:
        count = lax.axis_size(axis)
        forward = [(i, i + 1) for i in range(count - 1)]
        if periodic:
            forward.append((count - 1, 0))
        backward = [(target, source) for source, target in forward]
        low = lax.ppermute(
            lax.slice_in_dim(block, block.shape[dim] - width, None, axis=dim), axis, forward
        )
        high = lax.ppermute(lax.slice_in_dim(block, 0, width, axis=dim), axis, backward)
        block = jnp.concatenate([low, block, high], axis=dim)
    return block


def centred(field, axis):
    return 0.5 * (jnp.roll(field, -1, axis) - jnp.roll(field, 1, axis))


def advance(extended, row_mask):
    columns = (extended.shape[0] - 1) // 3
    state = extended[:-1].reshape(columns, 3, extended.shape[1], extended.shape[2])
    depth_plane = extended[-1]
    height, east_wind, north_wind = (state[:, 0], state[:, 1], state[:, 2])
    divergence = centred(east_wind, 2) + centred(north_wind, 1)
    height = (height - TIME_STEP * depth_plane * divergence) * row_mask
    new_east = (east_wind - TIME_STEP * centred(height, 2) + ROTATION * north_wind) * row_mask
    north_wind = (north_wind - TIME_STEP * centred(height, 1) - ROTATION * east_wind) * row_mask
    return jnp.stack([height, new_east, north_wind], 1)


def per_device(
    background_expectation, factor, average_thickness, obs_cells, obs_count, obs_values, obs_error
):
    band_rows = factor.shape[2]
    cycle_cols = factor.shape[3]
    columns = factor.shape[0] + 1
    joined_components = jnp.concatenate([background_expectation[None], factor], 0)
    depth_plane = average_thickness[None]
    for repeat in range(STEPS):
        extended = with_halo(
            jnp.concatenate(
                [joined_components.reshape(3 * columns, band_rows, cycle_cols), depth_plane], 0
            ),
            (("lat", 1),),
            2,
            False,
        )
        extended = with_halo(extended, (("lon", 2),), 2, True)
        global_row = lax.axis_index("lat") * band_rows - 2 + jnp.arange(band_rows + 2 * 2)
        inside = (global_row >= 0) & (global_row < band_rows * lax.axis_size("lat"))
        joined_components = advance(extended, inside.astype(jnp.float32)[:, None])[
            :, :, 2 : 2 + band_rows, 2 : 2 + cycle_cols
        ]
    surface_elevation = joined_components[:, 0].reshape(columns, band_rows * cycle_cols)
    picked = jnp.take(surface_elevation, obs_cells, axis=1)
    live = (jnp.arange(obs_cells.shape[0], dtype=jnp.int32) < obs_count[0]).astype(jnp.float32)
    weight = live / obs_error
    scaled = picked[1:] * weight
    innovation = (obs_values - picked[0]) * weight
    gram = jnp.dot(scaled, scaled.T, precision=lax.Precision.HIGHEST)
    drive = jnp.dot(scaled, innovation, precision=lax.Precision.HIGHEST)
    gram, drive = lax.psum((gram, drive), ("lat", "lon"))
    rank = columns - 1
    identity = jnp.eye(rank, dtype=jnp.float32)
    system = identity + gram
    lower = jnp.linalg.cholesky(system)
    inverse = lax.linalg.triangular_solve(
        lower, identity, left_side=True, lower=True, transpose_a=True
    )
    middle = lax.linalg.triangular_solve(lower, drive[:, None], left_side=True, lower=True)
    difference_coefficients = lax.linalg.triangular_solve(
        lower, middle, left_side=True, lower=True, transpose_a=True
    )[:, 0]
    sample_realisations = joined_components[1:].reshape(rank, -1)
    analysis_factor = jnp.dot(
        inverse.T, sample_realisations, precision=lax.Precision.HIGHEST
    ).reshape(factor.shape)
    updated_expectation = joined_components[0] + jnp.dot(
        difference_coefficients, sample_realisations, precision=lax.Precision.HIGHEST
    ).reshape(background_expectation.shape)
    return (updated_expectation, analysis_factor)


def solution(mesh):
    return jax.shard_map(
        per_device,
        mesh=mesh,
        in_specs=(
            P(None, "lat", "lon"),
            P(None, None, "lat", "lon"),
            P("lat", "lon"),
            P(("lat", "lon")),
            P(("lat", "lon")),
            P(("lat", "lon")),
            P(("lat", "lon")),
        ),
        out_specs=(P(None, "lat", "lon"), P(None, None, "lat", "lon")),
        check_vma=False,
    )
```

profile of v0, /device:TPU:1, one launch (start us, length us, event | category | flops | bytes accessed | tf_op | source)
XLA Modules:
  0.0 247.3 jit_solution(5355350248722977163)
XLA Ops:
  0.6 1.0 pad_maximum_fusion.16
  1.7 0.8 fusion.92
  2.5 4.6 %collective-permute-start = (f32[100,2,128]{2,1,0:T(2,128)S(1)}, f32[100,2,128]{2,1,0:T(2,128)S(1)}, u32[]{:S(2)}, u32[]{:S(2)}) collective-permute-start(f32[100,2,128]{2,1,0:T(2,128)S(1)} %get-tuple-element.146), channel_id=1, source_target_pairs={{0,32},{32,64},{64,96},{96,128},{128,160},{160,192},{192,224},{224... | collective-permute-start | bytes 307208 | tf_op jit(solution)/shard_map/ppermute | solution.py:20
  7.1 5.5 %collective-permute-start.1 = (f32[100,2,128]{2,1,0:T(2,128)S(1)}, f32[100,2,128]{2,1,0:T(2,128)S(1)}, u32[]{:S(2)}, u32[]{:S(2)}) collective-permute-start(f32[100,2,128]{2,1,0:T(2,128)S(1)} %get-tuple-element.147), channel_id=1, source_target_pairs={{32,0},{64,32},{96,64},{128,96},{160,128},{192,160},{224,192},{256... | collective-permute-start | bytes 307208 | tf_op jit(solution)/shard_map/ppermute | solution.py:23
  12.6 0.9 collective-permute-done.1
  13.5 0.8 fusion.17
  15.3 12.4 %collective-permute-start.3 = (f32[100,12,2]{0,2,1:T(2,128)S(1)}, f32[100,12,2]{0,2,1:T(2,128)S(1)}, u32[]{:S(2)}, u32[]{:S(2)}) collective-permute-start(f32[100,12,2]{0,2,1:T(2,128)S(1)} %copy.207), channel_id=1, source_target_pairs={{1,0},{2,1},{3,2},{4,3},{5,4},{6,5},{7,6},{8,7},{9,8},{10,9},{11,1... | collective-permute-start | bytes 28808 | tf_op jit(solution)/shard_map/ppermute | solution.py:23
  27.7 1.9 collective-permute-start.2
  29.6 5.8 %collective-permute-done.2 = f32[100,12,2]{0,2,1:T(2,128)S(1)} collective-permute-done((f32[100,12,2]{0,2,1:T(2,128)S(1)}, f32[100,12,2]{0,2,1:T(2,128)S(1)}, u32[]{:S(2)}, u32[]{:S(2)}) %collective-permute-start.2) | collective-permute-done | bytes 9632 | tf_op jit(solution)/shard_map/ppermute | solution.py:20
  35.9 0.5 copy.209
  36.4 1.1 fusion.3
  38.8 0.6 fusion.31
  39.8 1.2 fusion.35
  42.0 0.9 fusion.83
  42.9 0.9 pad_maximum_fusion.8
  44.0 3.2 %collective-permute-start.4 = (f32[100,2,128]{2,1,0:T(2,128)S(1)}, f32[100,2,128]{2,1,0:T(2,128)S(1)}, u32[]{:S(2)}, u32[]{:S(2)}) collective-permute-start(f32[100,2,128]{2,1,0:T(2,128)S(1)} %get-tuple-element.144), channel_id=1, source_target_pairs={{0,32},{32,64},{64,96},{96,128},{128,160},{160,192},{192,224},{224... | collective-permute-start | bytes 307208 | tf_op jit(solution)/shard_map/ppermute | solution.py:20
  47.2 1.9 collective-permute-start.5
  49.2 4.0 %collective-permute-done.5 = f32[100,2,128]{2,1,0:T(2,128)S(1)} collective-permute-done((f32[100,2,128]{2,1,0:T(2,128)S(1)}, f32[100,2,128]{2,1,0:T(2,128)S(1)}, u32[]{:S(2)}, u32[]{:S(2)}) %collective-permute-start.5) | collective-permute-done | bytes 102432 | tf_op jit(solution)/shard_map/ppermute | solution.py:23
  54.0 1.9 collective-permute-start.6
  56.2 6.9 %collective-permute-start.7 = (f32[100,12,2]{0,2,1:T(2,128)S(1)}, f32[100,12,2]{0,2,1:T(2,128)S(1)}, u32[]{:S(2)}, u32[]{:S(2)}) collective-permute-start(f32[100,12,2]{0,2,1:T(2,128)S(1)} %copy.230), channel_id=1, source_target_pairs={{1,0},{2,1},{3,2},{4,3},{5,4},{6,5},{7,6},{8,7},{9,8},{10,9},{11,1... | collective-permute-start | bytes 28808 | tf_op jit(solution)/shard_map/ppermute | solution.py:23
  64.1 1.2 fusion.7
  65.6 0.5 copy_bitcast_fusion.5
  66.6 0.5 fusion.44
  67.5 0.5 fusion.40
  68.0 0.8 fusion.48
  69.1 3.0 %collective-permute-start.8 = (f32[100,2,128]{2,1,0:T(2,128)S(1)}, f32[100,2,128]{2,1,0:T(2,128)S(1)}, u32[]{:S(2)}, u32[]{:S(2)}) collective-permute-start(f32[100,2,128]{2,1,0:T(2,128)S(1)} %get-tuple-element.142), channel_id=1, source_target_pairs={{0,32},{32,64},{64,96},{96,128},{128,160},{160,192},{192,224},{224... | collective-permute-start | bytes 307208 | tf_op jit(solution)/shard_map/ppermute | solution.py:20
  72.1 1.9 collective-permute-start.9
  74.0 4.0 %collective-permute-done.9 = f32[100,2,128]{2,1,0:T(2,128)S(1)} collective-permute-done((f32[100,2,128]{2,1,0:T(2,128)S(1)}, f32[100,2,128]{2,1,0:T(2,128)S(1)}, u32[]{:S(2)}, u32[]{:S(2)}) %collective-permute-start.9) | collective-permute-done | bytes 102432 | tf_op jit(solution)/shard_map/ppermute | solution.py:23
  79.2 7.2 %collective-permute-start.11 = (f32[100,12,2]{0,2,1:T(2,128)S(1)}, f32[100,12,2]{0,2,1:T(2,128)S(1)}, u32[]{:S(2)}, u32[]{:S(2)}) collective-permute-start(f32[100,12,2]{0,2,1:T(2,128)S(1)} %copy.250), channel_id=1, source_target_pairs={{1,0},{2,1},{3,2},{4,3},{5,4},{6,5},{7,6},{8,7},{9,8},{10,9},{11,1... | collective-permute-start | bytes 28808 | tf_op jit(solution)/shard_map/ppermute | solution.py:23
  86.4 1.9 collective-permute-start.10
  88.3 5.8 %collective-permute-done.10 = f32[100,12,2]{0,2,1:T(2,128)S(1)} collective-permute-done((f32[100,12,2]{0,2,1:T(2,128)S(1)}, f32[100,12,2]{0,2,1:T(2,128)S(1)}, u32[]{:S(2)}, u32[]{:S(2)}) %collective-permute-start.10) | collective-permute-done | bytes 9632 | tf_op jit(solution)/shard_map/ppermute | solution.py:20
  95.1 1.2 fusion.11
  97.5 0.5 fusion.60
  98.4 0.5 fusion.56
  98.9 0.8 fusion.64
  100.1 3.2 %collective-permute-start.12 = (f32[100,2,128]{2,1,0:T(2,128)S(1)}, f32[100,2,128]{2,1,0:T(2,128)S(1)}, u32[]{:S(2)}, u32[]{:S(2)}) collective-permute-start(f32[100,2,128]{2,1,0:T(2,128)S(1)} %get-tuple-element.140), channel_id=1, source_target_pairs={{0,32},{32,64},{64,96},{96,128},{128,160},{160,192},{192,224},{224... | collective-permute-start | bytes 307208 | tf_op jit(solution)/shard_map/ppermute | solution.py:20
  103.3 2.1 collective-permute-start.13
  105.5 0.5 compare_and_fusion
  106.0 3.3 %collective-permute-done.13 = f32[100,2,128]{2,1,0:T(2,128)S(1)} collective-permute-done((f32[100,2,128]{2,1,0:T(2,128)S(1)}, f32[100,2,128]{2,1,0:T(2,128)S(1)}, u32[]{:S(2)}, u32[]{:S(2)}) %collective-permute-start.13) | collective-permute-done | bytes 102432 | tf_op jit(solution)/shard_map/ppermute | solution.py:23
  110.4 1.9 collective-permute-start.15
  112.3 3.4 %collective-permute-start.14 = (f32[100,12,2]{0,2,1:T(2,128)S(1)}, f32[100,12,2]{0,2,1:T(2,128)S(1)}, u32[]{:S(2)}, u32[]{:S(2)}) collective-permute-start(f32[100,12,2]{0,2,1:T(2,128)S(1)} %copy.269), channel_id=1, source_target_pairs={{0,1},{1,2},{2,3},{3,4},{4,5},{5,6},{6,7},{7,8},{8,9},{9,10},{10,1... | collective-permute-start | bytes 28808 | tf_op jit(solution)/shard_map/ppermute | solution.py:20
  116.3 3.7 %collective-permute-done.14 = f32[100,12,2]{0,2,1:T(2,128)S(1)} collective-permute-done((f32[100,12,2]{0,2,1:T(2,128)S(1)}, f32[100,12,2]{0,2,1:T(2,128)S(1)}, u32[]{:S(2)}, u32[]{:S(2)}) %collective-permute-start.14) | collective-permute-done | bytes 9632 | tf_op jit(solution)/shard_map/ppermute | solution.py:20
  121.0 1.2 fusion.15
  123.5 0.5 fusion.72
  124.0 0.8 slice.565
  125.2 0.5 fusion.76
  125.7 0.6 slice_bitcast_fusion.24
  126.3 0.8 slice_bitcast_fusion.16
  127.2 0.8 slice_bitcast_fusion.8
  128.2 1.9 copy.289
  130.1 1.8 gather_fusion
  132.1 0.7 subtract_multiply_fusion
  132.8 0.5 fusion.88
  133.7 99.6 %all-reduce = (f32[32,32]{1,0:T(8,128)S(1)}, f32[32]{0:T(128)S(1)}) all-reduce(f32[32,32]{1,0:T(8,128)S(1)} %fusion.88, f32[32]{0:T(128)S(1)} %convolution_bitcast_fusion.3), channel_id=1, replica_groups=mesh['lat'=16,'lon'=32] {'lat','lon'}, use_global_device_ids=true, to_apply=%region_0.1 | all-reduce | flops 1056 | bytes 8448 | tf_op jit(solution)/shard_map/psum | solution.py:75
  233.4 2.9 %cholesky.18 = f32[32,32]{1,0:T(8,128)S(1)} custom-call(f32[32,32]{1,0:T(8,128)S(1)} %fusion.104), custom_call_target="Cholesky" | custom-call | tf_op jit(solution)/shard_map/jit(cholesky)/cholesky | solution.py:79
  236.3 0.6 compare_reduce_fusion
  237.0 0.7 fusion.95
  237.6 2.4 custom-call.10
  240.6 1.1 fusion.78
  242.0 1.5 fusion.81
  243.5 0.9 pad_maximum_fusion.10
  245.2 0.5 fusion.86
  245.7 0.6 copy.294
  246.3 1.0 copy.295
  (119 shorter events, 17.7 us)
Async XLA Ops:
  2.5 10.1 %collective-permute-start = (f32[100,2,128]{2,1,0:T(2,128)S(1)}, f32[100,2,128]{2,1,0:T(2,128)S(1)}, u32[]{:S(2)}, u32[]{:S(2)}) collective-permute-start(f32[100,2,128]{2,1,0:T(2,128)S(1)} %get-tuple-element.146), channel_id=1, source_target_pairs={{0,32},{32,64},{64,96},{96,128},{128,160},{160,192},{192,224},{224... | collective-permute-start | bytes 307208 | tf_op jit(solution)/shard_map/ppermute | solution.py:20
  7.1 6.4 %collective-permute-start.1 = (f32[100,2,128]{2,1,0:T(2,128)S(1)}, f32[100,2,128]{2,1,0:T(2,128)S(1)}, u32[]{:S(2)}, u32[]{:S(2)}) collective-permute-start(f32[100,2,128]{2,1,0:T(2,128)S(1)} %get-tuple-element.147), channel_id=1, source_target_pairs={{32,0},{64,32},{96,64},{128,96},{160,128},{192,160},{224,192},{256... | collective-permute-start | bytes 307208 | tf_op jit(solution)/shard_map/ppermute | solution.py:23
  14.6 21.8 %copy-start.2 = (f32[8,128]{1,0:T(8,128)S(1)}, f32[8,128]{1,0:T(8,128)}, u32[]{:S(2)}) copy-start(f32[8,128]{1,0:T(8,128)} %param.9) | copy-start | bytes 12292
  15.3 20.7 %collective-permute-start.3 = (f32[100,12,2]{0,2,1:T(2,128)S(1)}, f32[100,12,2]{0,2,1:T(2,128)S(1)}, u32[]{:S(2)}, u32[]{:S(2)}) collective-permute-start(f32[100,12,2]{0,2,1:T(2,128)S(1)} %copy.207), channel_id=1, source_target_pairs={{1,0},{2,1},{3,2},{4,3},{5,4},{6,5},{7,6},{8,7},{9,8},{10,9},{11,1... | collective-permute-start | bytes 28808 | tf_op jit(solution)/shard_map/ppermute | solution.py:23
  27.7 7.8 %collective-permute-start.2 = (f32[100,12,2]{0,2,1:T(2,128)S(1)}, f32[100,12,2]{0,2,1:T(2,128)S(1)}, u32[]{:S(2)}, u32[]{:S(2)}) collective-permute-start(f32[100,12,2]{0,2,1:T(2,128)S(1)} %copy.206), channel_id=1, source_target_pairs={{0,1},{1,2},{2,3},{3,4},{4,5},{5,6},{6,7},{7,8},{8,9},{9,10},{10,1... | collective-permute-start | bytes 28808 | tf_op jit(solution)/shard_map/ppermute | solution.py:20
  44.0 5.2 %collective-permute-start.4 = (f32[100,2,128]{2,1,0:T(2,128)S(1)}, f32[100,2,128]{2,1,0:T(2,128)S(1)}, u32[]{:S(2)}, u32[]{:S(2)}) collective-permute-start(f32[100,2,128]{2,1,0:T(2,128)S(1)} %get-tuple-element.144), channel_id=1, source_target_pairs={{0,32},{32,64},{64,96},{96,128},{128,160},{160,192},{192,224},{224... | collective-permute-start | bytes 307208 | tf_op jit(solution)/shard_map/ppermute | solution.py:20
  47.2 6.0 %collective-permute-start.5 = (f32[100,2,128]{2,1,0:T(2,128)S(1)}, f32[100,2,128]{2,1,0:T(2,128)S(1)}, u32[]{:S(2)}, u32[]{:S(2)}) collective-permute-start(f32[100,2,128]{2,1,0:T(2,128)S(1)} %get-tuple-element.145), channel_id=1, source_target_pairs={{32,0},{64,32},{96,64},{128,96},{160,128},{192,160},{224,192},{256... | collective-permute-start | bytes 307208 | tf_op jit(solution)/shard_map/ppermute | solution.py:23
  54.0 9.1 %collective-permute-start.6 = (f32[100,12,2]{0,2,1:T(2,128)S(1)}, f32[100,12,2]{0,2,1:T(2,128)S(1)}, u32[]{:S(2)}, u32[]{:S(2)}) collective-permute-start(f32[100,12,2]{0,2,1:T(2,128)S(1)} %copy.229), channel_id=1, source_target_pairs={{0,1},{1,2},{2,3},{3,4},{4,5},{5,6},{6,7},{7,8},{8,9},{9,10},{10,1... | collective-permute-start | bytes 28808 | tf_op jit(solution)/shard_map/ppermute | solution.py:20
  56.2 7.5 %collective-permute-start.7 = (f32[100,12,2]{0,2,1:T(2,128)S(1)}, f32[100,12,2]{0,2,1:T(2,128)S(1)}, u32[]{:S(2)}, u32[]{:S(2)}) collective-permute-start(f32[100,12,2]{0,2,1:T(2,128)S(1)} %copy.230), channel_id=1, source_target_pairs={{1,0},{2,1},{3,2},{4,3},{5,4},{6,5},{7,6},{8,7},{9,8},{10,9},{11,1... | collective-permute-start | bytes 28808 | tf_op jit(solution)/shard_map/ppermute | solution.py:23
  69.1 4.9 %collective-permute-start.8 = (f32[100,2,128]{2,1,0:T(2,128)S(1)}, f32[100,2,128]{2,1,0:T(2,128)S(1)}, u32[]{:S(2)}, u32[]{:S(2)}) collective-permute-start(f32[100,2,128]{2,1,0:T(2,128)S(1)} %get-tuple-element.142), channel_id=1, source_target_pairs={{0,32},{32,64},{64,96},{96,128},{128,160},{160,192},{192,224},{224... | collective-permute-start | bytes 307208 | tf_op jit(solution)/shard_map/ppermute | solution.py:20
  72.1 6.0 %collective-permute-start.9 = (f32[100,2,128]{2,1,0:T(2,128)S(1)}, f32[100,2,128]{2,1,0:T(2,128)S(1)}, u32[]{:S(2)}, u32[]{:S(2)}) collective-permute-start(f32[100,2,128]{2,1,0:T(2,128)S(1)} %get-tuple-element.143), channel_id=1, source_target_pairs={{32,0},{64,32},{96,64},{128,96},{160,128},{192,160},{224,192},{256... | collective-permute-start | bytes 307208 | tf_op jit(solution)/shard_map/ppermute | solution.py:23
  78.5 9.8 %copy-start.3 = (s32[256]{0:T(256)S(1)}, s32[256]{0:T(256)}, u32[]{:S(2)}) copy-start(s32[256]{0:T(256)} %param.10) | copy-start | bytes 3076
  79.2 15.5 %collective-permute-start.11 = (f32[100,12,2]{0,2,1:T(2,128)S(1)}, f32[100,12,2]{0,2,1:T(2,128)S(1)}, u32[]{:S(2)}, u32[]{:S(2)}) collective-permute-start(f32[100,12,2]{0,2,1:T(2,128)S(1)} %copy.250), channel_id=1, source_target_pairs={{1,0},{2,1},{3,2},{4,3},{5,4},{6,5},{7,6},{8,7},{9,8},{10,9},{11,1... | collective-permute-start | bytes 28808 | tf_op jit(solution)/shard_map/ppermute | solution.py:23
  86.4 7.8 %collective-permute-start.10 = (f32[100,12,2]{0,2,1:T(2,128)S(1)}, f32[100,12,2]{0,2,1:T(2,128)S(1)}, u32[]{:S(2)}, u32[]{:S(2)}) collective-permute-start(f32[100,12,2]{0,2,1:T(2,128)S(1)} %copy.249), channel_id=1, source_target_pairs={{0,1},{1,2},{2,3},{3,4},{4,5},{5,6},{6,7},{7,8},{8,9},{9,10},{10,1... | collective-permute-start | bytes 28808 | tf_op jit(solution)/shard_map/ppermute | solution.py:20
  100.1 5.9 %collective-permute-start.12 = (f32[100,2,128]{2,1,0:T(2,128)S(1)}, f32[100,2,128]{2,1,0:T(2,128)S(1)}, u32[]{:S(2)}, u32[]{:S(2)}) collective-permute-start(f32[100,2,128]{2,1,0:T(2,128)S(1)} %get-tuple-element.140), channel_id=1, source_target_pairs={{0,32},{32,64},{64,96},{96,128},{128,160},{160,192},{192,224},{224... | collective-permute-start | bytes 307208 | tf_op jit(solution)/shard_map/ppermute | solution.py:20
  103.3 6.0 %collective-permute-start.13 = (f32[100,2,128]{2,1,0:T(2,128)S(1)}, f32[100,2,128]{2,1,0:T(2,128)S(1)}, u32[]{:S(2)}, u32[]{:S(2)}) collective-permute-start(f32[100,2,128]{2,1,0:T(2,128)S(1)} %get-tuple-element.141), channel_id=1, source_target_pairs={{32,0},{64,32},{96,64},{128,96},{160,128},{192,160},{224,192},{256... | collective-permute-start | bytes 307208 | tf_op jit(solution)/shard_map/ppermute | solution.py:23
  110.4 10.1 %collective-permute-start.15 = (f32[100,12,2]{0,2,1:T(2,128)S(1)}, f32[100,12,2]{0,2,1:T(2,128)S(1)}, u32[]{:S(2)}, u32[]{:S(2)}) collective-permute-start(f32[100,12,2]{0,2,1:T(2,128)S(1)} %copy.270), channel_id=1, source_target_pairs={{1,0},{2,1},{3,2},{4,3},{5,4},{6,5},{7,6},{8,7},{9,8},{10,9},{11,1... | collective-permute-start | bytes 28808 | tf_op jit(solution)/shard_map/ppermute | solution.py:23
  112.3 7.8 %collective-permute-start.14 = (f32[100,12,2]{0,2,1:T(2,128)S(1)}, f32[100,12,2]{0,2,1:T(2,128)S(1)}, u32[]{:S(2)}, u32[]{:S(2)}) collective-permute-start(f32[100,12,2]{0,2,1:T(2,128)S(1)} %copy.269), channel_id=1, source_target_pairs={{0,1},{1,2},{2,3},{3,4},{4,5},{5,6},{6,7},{7,8},{8,9},{9,10},{10,1... | collective-permute-start | bytes 28808 | tf_op jit(solution)/shard_map/ppermute | solution.py:20
  128.0 3.9 %copy-start.4 = (pred[256]{0:T(512)(128)(4,1)S(1)}, pred[256]{0:T(512)(128)(4,1)}, u32[]{:S(2)}) copy-start(pred[256]{0:T(512)(128)(4,1)} %compare_and_fusion) | copy-start | bytes 772
  240.1 1.6 copy-start
  240.1 1.6 copy-start.1
where the time goes:
time: 249 us; the launch traced here: 247 us
  blocking collectives  99.6 us (40%)
  starting transfers between devices  63 us (25%)
  other arithmetic  28.8 us (12%)
  waiting for transfers between devices  27.8 us (11%)
  local copies, waits for them, and re-layouts  23.6 us (9%)
    psum x1, blocking collectives, per_device(): gram, drive = lax.psum((gram, drive), ('lat', 'lon'))  99.6 us
    ppermute x8, starting transfers between devices, with_halo(): lax.ppermute(lax.slice_in_dim(block, 0, width, axis=dim), axis, backward)  39.9 us
    ppermute x8, starting transfers between devices, with_halo(): lax.ppermute(lax.slice_in_dim(block, block.shape[dim] - width, None, axis...  23.2 us
    ppermute x8, waiting for transfers between devices, with_halo(): lax.ppermute(lax.slice_in_dim(block, block.shape[dim] - width, None, axis...  15.4 us
    ppermute x8, waiting for transfers between devices, with_halo(): lax.ppermute(lax.slice_in_dim(block, 0, width, axis=dim), axis, backward)  12.5 us
    concatenate x8, other arithmetic, with_halo(): block = jnp.concatenate([low, block, high], axis=dim)  5.93 us
    concatenate x32, local copies, waits for them, and re-layouts, centred(): return 0.5 * (jnp.roll(field, -1, axis) - jnp.roll(field, 1, axis))  5.54 us
  transfers between devices with their start and end apart: 16, of which 8 were waited for; matrix products, arithmetic and copies ran while one was open for 1% of the time, Pallas kernels for 0%

commit v1 on v0

v1 whole, which is shorter than its diff:
```python
import functools

import jax
import jax.numpy as jnp
from jax import lax
from jax.experimental import pallas as pl
from jax.experimental.pallas import tpu as pltpu
from jax.sharding import PartitionSpec as P

STEPS = 4
TIME_STEP = 0.9
ROTATION = 0.25

RANK = 32
ROWS = 8
LANES = 128
HALO = 2 * STEPS
TILES = RANK // 8
PLANES = 3 * ROWS
PACK = 3 * RANK + 8
HIGHEST = lax.Precision.HIGHEST
NT = (((1,), (1,)), ((), ()))


def lane_iota():
    return lax.broadcasted_iota(jnp.int32, (8, LANES), 1)


def member_rows(field, row, tile):
    return pl.ds(8 * tile * PLANES + field * ROWS + row, 8, stride=PLANES)


def small_tile(mean_ref, depth_ref, row):
    return jnp.concatenate(
        [mean_ref[f * ROWS + row : f * ROWS + row + 1, :] for f in range(3)]
        + [depth_ref[row : row + 1, :]] * 5,
        0,
    )


def pack_kernel(factor_ref, mean_ref, depth_ref, out_ref):
    group = lane_iota() // 16

    def packed(row_value):
        acc = None
        for row in range(ROWS):
            moved = pltpu.roll(row_value(row), (HALO + 16 * row) % LANES, 1)
            acc = moved if acc is None else jnp.where(group == row, moved, acc)
        return acc

    for field in range(3):
        for tile in range(TILES):
            out_ref[field * RANK + 8 * tile : field * RANK + 8 * tile + 8, :] = packed(
                lambda row: factor_ref[member_rows(field, row, tile), :]
            )
    out_ref[3 * RANK : PACK, :] = packed(lambda row: small_tile(mean_ref, depth_ref, row))


def obs_kernel(count_ref, cells_ref, values_ref, error_ref, out_ref):
    slots = cells_ref.shape[1]
    live = lax.broadcasted_iota(jnp.int32, (1, slots), 1) < count_ref[0]
    weight = jnp.where(live, 1.0, 0.0) / error_ref[...]
    square = weight * weight
    cells = cells_ref[...]
    row_of = cells // LANES
    lane_of = cells - row_of * LANES
    in_row = lax.broadcasted_iota(jnp.int32, (ROWS, slots), 0) == row_of
    spread = jnp.concatenate(
        [jnp.where(in_row, square, 0.0), jnp.where(in_row, square * values_ref[...], 0.0)], 0
    )
    in_lane = lax.broadcasted_iota(jnp.int32, (LANES, slots), 0) == lane_of
    out_ref[...] = lax.dot_general(
        spread, jnp.where(in_lane, 1.0, 0.0), NT, precision=HIGHEST, preferred_element_type=jnp.float32
    )


def forecast_kernel(
    own_ref, north_ref, south_ref, mean_ref, depth_ref, edge_ref, north_edge_ref, south_edge_ref,
    weight_ref, split_ref, mean_out_ref, gram_ref, state, depth, heights, scaled,
):
    lane = lane_iota()
    left, right = lane >= LANES - HALO, lane < HALO
    band = lax.axis_index("lat")
    bands = lax.axis_size("lat")

    def windows(value, edge, row):
        moved = pltpu.roll(edge, (LANES - HALO - 16 * row) % LANES, 1)
        return jnp.where(left, moved, value), jnp.where(right, moved, value)

    blocks = (
        (north_ref, north_edge_ref, lambda r: north_edge_ref[PACK + 8 * r : PACK + 8 * r + 8, :]),
        (own_ref, edge_ref, lambda r: small_tile(mean_ref, depth_ref, r)),
        (south_ref, south_edge_ref, lambda r: south_edge_ref[PACK + 8 * r : PACK + 8 * r + 8, :]),
    )
    for block, (main, edges, small) in enumerate(blocks):
        for field in range(3):
            for tile in range(TILES):
                edge = edges[field * RANK + 8 * tile : field * RANK + 8 * tile + 8, :]
                for row in range(ROWS):
                    west, east = windows(main[member_rows(field, row, tile), :], edge, row)
                    state[2 * tile, field, ROWS * block + row] = west
                    state[2 * tile + 1, field, ROWS * block + row] = east
        edge = edges[3 * RANK : PACK, :]
        for row in range(ROWS):
            at = ROWS * block + row
            west, east = windows(small(row), edge, row)
            for field in range(3):
                state[2 * TILES, field, at, 0:1, :] = west[field : field + 1, :]
                state[2 * TILES, field, at, 1:2, :] = east[field : field + 1, :]
                state[2 * TILES, field, at, 2:8, :] = west[2:8, :]
            scaled_west = (0.5 * TIME_STEP) * west[3:4, :]
            scaled_east = (0.5 * TIME_STEP) * east[3:4, :]
            depth[0, at] = jnp.broadcast_to(scaled_west, (8, LANES))
            depth[1, at] = jnp.broadcast_to(scaled_east, (8, LANES))
            depth[2, at] = jnp.where(
                lax.broadcasted_iota(jnp.int32, (8, LANES), 0) == 0, depth[0, at], depth[1, at]
            )

    pull = 0.5 * TIME_STEP
    north_pull = jnp.where(band > 0, pull, 0.0)
    south_pull = jnp.where(band < bands - 1, pull, 0.0)

    def lon_difference(value):
        return pltpu.roll(value, LANES - 1, 1) - pltpu.roll(value, 1, 1)

    def advance(which, carry):
        plane = jnp.where(which == 2 * TILES, 2, which & 1)
        h, e, n = (state.at[which, field] for field in range(3))
        for step in range(STEPS):
            first, last = 1 + 2 * step, 3 * ROWS - 2 - 2 * step
            for row in range(first, last + 1):
                divergence = lon_difference(e[row]) + (n[row + 1] - n[row - 1])
                h[row] = h[row] - depth[plane, row] * divergence
            for row in range(first + 1, last):
                row_pull = north_pull if row < ROWS else south_pull if row >= 2 * ROWS else pull
                east, north = e[row], n[row]
                e[row] = east - pull * lon_difference(h[row]) + ROTATION * north
                n[row] = north - row_pull * (h[row + 1] - h[row - 1]) - ROTATION * east
        return carry

    lax.fori_loop(0, 2 * TILES + 1, advance, 0)

    half = lane < LANES // 2
    half_row = lax.broadcasted_iota(jnp.int32, (1, LANES), 1) < LANES // 2
    for field in range(3):
        for row in range(ROWS):
            cols = slice((field * ROWS + row) * LANES, (field * ROWS + row + 1) * LANES)
            full = jnp.concatenate(
                [
                    jnp.where(half, state[2 * t, field, ROWS + row], state[2 * t + 1, field, ROWS + row])
                    for t in range(TILES)
                ],
                0,
            )
            high = full.astype(jnp.bfloat16)
            rest = full - high.astype(jnp.float32)
            middle = rest.astype(jnp.bfloat16)
            split_ref[0:RANK, cols] = high
            split_ref[RANK : 2 * RANK, cols] = middle
            split_ref[2 * RANK : 3 * RANK, cols] = (rest - middle.astype(jnp.float32)).astype(jnp.bfloat16)
            both = state[2 * TILES, field, ROWS + row]
            mean = jnp.where(half_row, both[0:1, :], both[1:2, :])
            mean_out_ref[field * ROWS + row : field * ROWS + row + 1, :] = mean
            if field == 0:
                square = weight_ref[row : row + 1, :]
                heights[:, cols] = full
                scaled[0:RANK, cols] = full * square
                pulled = weight_ref[ROWS + row : ROWS + row + 1, :] - square * mean
                scaled[RANK : RANK + 8, cols] = jnp.broadcast_to(pulled, (8, LANES))
    gram = lax.dot_general(
        heights[...], scaled[...], NT, precision=HIGHEST, preferred_element_type=jnp.float32
    )
    gram = jnp.concatenate([gram, jnp.zeros((RANK, LANES - RANK - 8), jnp.float32)], 1)
    acc = None
    for tile in range(TILES):
        part = gram[8 * tile : 8 * tile + 8, :]
        if tile < 2:
            far = gram[8 * tile + 16 : 8 * tile + 24, :]
            part = jnp.where(lane == 31, pltpu.roll(part, LANES - 1, 1), part)
            part = jnp.where(lane == 30, pltpu.roll(far, LANES - 2, 1), part)
        moved = pltpu.roll(part, 32 * tile, 1) if tile else part
        acc = moved if acc is None else jnp.where(lane // 32 == tile, moved, acc)
    gram_ref[...] = acc


def analysis_kernel(parts_ref, split_ref, mean_ref, update_ref, factor_ref):
    lane = lane_iota()
    total = jnp.sum(parts_ref[...], 0)
    tiles, drives = [], [None] * TILES
    for tile in range(TILES):
        part = pltpu.roll(total, LANES - 32 * tile, 1) if tile else total
        if tile < 2:
            drives[tile] = pltpu.roll(part, 2 * RANK - 31, 1)
            drives[tile + 2] = pltpu.roll(part, 2 * RANK - 30, 1)
        tiles.append(part)
    lower = jnp.concatenate(tiles, 0)
    wide = lax.broadcasted_iota(jnp.int32, (RANK, LANES), 1)
    deep = lax.broadcasted_iota(jnp.int32, (RANK, LANES), 0)
    mirrored = jnp.concatenate([lower, jnp.zeros((LANES - RANK, LANES), jnp.float32)], 0).T[0:RANK, :]
    work = jnp.where(wide > deep, mirrored, lower)
    work = jnp.where(wide < RANK, work, 0.0) + jnp.where((wide == deep) | (wide == deep + RANK), 1.0, 0.0)
    work = jnp.where(wide == 2 * RANK, jnp.concatenate(drives, 0), work)
    for k in range(RANK - 1):
        row = work[k : k + 1, :] * (1.0 / work[k : k + 1, k : k + 1])
        column = jnp.where(deep[:, 0:1] > k, work[:, k : k + 1], 0.0)
        work = work - column * row
    pivots = jnp.sum(jnp.where(wide == deep, work, 0.0), 1, keepdims=True)
    work = work * lax.rsqrt(pivots)
    shift = jnp.sum(work * work[:, 2 * RANK : 2 * RANK + 1], 0, keepdims=True)
    mixed = jnp.concatenate([work, jnp.broadcast_to(shift, (8, LANES))], 0)[:, RANK : 2 * RANK]
    high = mixed.astype(jnp.bfloat16)
    rest = mixed - high.astype(jnp.float32)
    middle = rest.astype(jnp.bfloat16)
    low = (rest - middle.astype(jnp.float32)).astype(jnp.bfloat16)
    left = jnp.concatenate([high, high, high, middle, middle, low], 1)
    split = split_ref[...]
    fine = jnp.concatenate([split, split[0 : 2 * RANK], split[0:RANK]], 0)
    out = jnp.dot(left, fine, preferred_element_type=jnp.float32)
    for plane in range(PLANES):
        cols = slice(plane * LANES, (plane + 1) * LANES)
        for tile in range(TILES):
            factor_ref[pl.ds(8 * tile * PLANES + plane, 8, stride=PLANES), :] = out[8 * tile : 8 * tile + 8, cols]
        update_ref[plane : plane + 1, :] = mean_ref[plane : plane + 1, :] + out[RANK : RANK + 1, cols]


VMEM = pl.BlockSpec(memory_space=pltpu.VMEM)
SMEM = pl.BlockSpec(memory_space=pltpu.SMEM)


def f32(*shape):
    return jax.ShapeDtypeStruct(shape, jnp.float32)


def shift_by(value, axis, step, periodic):
    count = lax.axis_size(axis)
    pairs = [(i, (i + step) % count) for i in range(count) if periodic or 0 <= i + step < count]
    return lax.ppermute(value, axis, pairs)


def sum_over(value, axis):
    count = lax.axis_size(axis)
    sent = jnp.broadcast_to(value[None], (count, *value.shape))
    return lax.all_to_all(sent, axis, 0, 0)


def per_device(
    background_expectation, factor, average_thickness, obs_cells, obs_count, obs_values, obs_error
):
    assert factor.shape == (RANK, 3, ROWS, LANES)
    own = factor.reshape(RANK * PLANES, LANES)
    mean = background_expectation.reshape(PLANES, LANES)
    edges = pl.pallas_call(
        pack_kernel, out_shape=f32(PACK, LANES), in_specs=[VMEM] * 3, out_specs=VMEM, name="pack"
    )(own, mean, average_thickness)
    from_west = shift_by(edges, "lon", 1, True)
    from_east = shift_by(edges, "lon", -1, True)
    from_north = shift_by(own, "lat", 1, False)
    from_south = shift_by(own, "lat", -1, False)
    east_lane = (lax.broadcasted_iota(jnp.int32, (PACK, LANES), 1) & 8) != 0
    halo = jnp.where(east_lane, from_east, from_west)
    small = jnp.concatenate([mean.reshape(3, ROWS, LANES), average_thickness[None]], 0)
    small = jnp.concatenate([small, jnp.zeros_like(small)], 0).transpose(1, 0, 2).reshape(8 * ROWS, LANES)
    corner = jnp.concatenate([halo, small], 0)
    north_corner = shift_by(corner, "lat", 1, False)
    south_corner = shift_by(corner, "lat", -1, False)
    slots = obs_cells.shape[0]
    weights = pl.pallas_call(
        obs_kernel, out_shape=f32(2 * ROWS, LANES), in_specs=[SMEM] + [VMEM] * 3, out_specs=VMEM, name="obs"
    )(obs_count, obs_cells.reshape(1, slots), obs_values.reshape(1, slots), obs_error.reshape(1, slots))
    split, mean, gram = pl.pallas_call(
        forecast_kernel,
        out_shape=(
            jax.ShapeDtypeStruct((3 * RANK, PLANES * LANES), jnp.bfloat16),
            f32(PLANES, LANES),
            f32(8, LANES),
        ),
        in_specs=[VMEM] * 9,
        out_specs=(VMEM,) * 3,
        scratch_shapes=[
            pltpu.VMEM((2 * TILES + 1, 3, 3 * ROWS, 8, LANES), jnp.float32),
            pltpu.VMEM((3, 3 * ROWS, 8, LANES), jnp.float32),
            pltpu.VMEM((RANK, ROWS * LANES), jnp.float32),
            pltpu.VMEM((RANK + 8, ROWS * LANES), jnp.float32),
        ],
        name="forecast",
    )(own, from_north, from_south, mean, average_thickness, halo, north_corner, south_corner, weights)
    gram = jnp.sum(sum_over(gram, "lat"), 0)
    parts = sum_over(gram, "lon")
    update, analysis = pl.pallas_call(
        analysis_kernel,
        out_shape=(f32(PLANES, LANES), f32(RANK * PLANES, LANES)),
        in_specs=[VMEM] * 3,
        out_specs=(VMEM, VMEM),
        name="analysis",
    )(parts, split, mean)
    return update.reshape(background_expectation.shape), analysis.reshape(factor.shape)


def solution(mesh):
    return jax.shard_map(
        per_device,
        mesh=mesh,
        in_specs=(
            P(None, "lat", "lon"),
            P(None, None, "lat", "lon"),
            P("lat", "lon"),
            P(("lat", "lon")),
            P(("lat", "lon")),
            P(("lat", "lon")),
            P(("lat", "lon")),
        ),
        out_specs=(P(None, "lat", "lon"), P(None, None, "lat", "lon")),
        check_vma=False,
    )
```

time: 249 us -> 80.9 us (0.32)
  blocking collectives: 99.6 us -> 31.5 us
  starting transfers between devices: 63 us -> 27.1 us
  other arithmetic: 28.8 us -> 0.12 us
  waiting for transfers between devices: 27.8 us -> 0.02 us
  local copies, waits for them, and re-layouts: 23.6 us -> 3.48 us
  Pallas kernels: 0 us -> 16.8 us
    psum x1 -> x0, blocking collectives: 99.6 us -> none  [per_device(): gram, drive = lax.psum((gram, drive), ('lat', 'lon'))]
    ppermute x16 -> x6, starting transfers between devices: 63 us -> 27.1 us  [shift_by(): return lax.ppermute(value, axis, pairs)]
    all_to_all x0 -> x2, blocking collectives: none -> 31.5 us  [sum_over(): return lax.all_to_all(sent, axis, 0, 0)]
    ppermute x16 -> x6, waiting for transfers between devices: 27.8 us -> 0.02 us  [shift_by(): return lax.ppermute(value, axis, pairs)]
    pallas_call x0 -> x4, Pallas kernels: none -> 16.8 us  [the longest x1 8.34 us: per_device(): pl.pallas_call(forecast_kernel, out_shape=(jax.ShapeDtypeStruct((3 * RANK...]
    mul x21 -> x0, other arithmetic: 11.2 us -> none  [the longest x4 4.29 us: advance(): (east_wind - TIME_STEP * centred(height, 2) + ROTATION * north_wind) * ro...]
    another operation x9 -> x0, other arithmetic: 8.86 us -> none  [the longest x3 3.59 us: per_device(): lower = jnp.linalg.cholesky(system)]
    concatenate x13 -> x1, other arithmetic: 7.97 us -> 0.01 us  [per_device(): corner = jnp.concatenate([halo, small], 0)]
  transfers between devices with their start and end apart: 16 -> 6, of which waited for: 8 -> 0; matrix products, arithmetic and copies ran while one was open for 1% -> 0% of each run, Pallas kernels for 0% -> 2%
where the time goes in v1:
time: 80.9 us; the launch traced here: 80.4 us
  blocking collectives  31.5 us (39%)
  starting transfers between devices  27.1 us (33%)
  Pallas kernels  16.8 us (21%)
  local copies, waits for them, and re-layouts  3.48 us (4%)
  between operations  1.46 us (2%)
    all_to_all x2, blocking collectives, sum_over(): return lax.all_to_all(sent, axis, 0, 0)  31.5 us
    ppermute x6, starting transfers between devices, shift_by(): return lax.ppermute(value, axis, pairs)  27.1 us
    pallas_call x1, Pallas kernels, per_device(): pl.pallas_call(forecast_kernel, out_shape=(jax.ShapeDtypeStruct((3 * RANK...  8.34 us
    pallas_call x1, Pallas kernels, per_device(): pl.pallas_call(analysis_kernel, out_shape=(f32(PLANES, LANES), f32(RANK *...  5.03 us
    unnamed x17, local copies, waits for them, and re-layouts  2.71 us
    pallas_call x1, Pallas kernels, per_device(): pl.pallas_call(pack_kernel, out_shape=f32(PACK, LANES), in_specs=[VMEM] *...  1.86 us
  transfers between devices with their start and end apart: 6, of which 0 were waited for; matrix products, arithmetic and copies ran while one was open for 0% of the time, Pallas kernels for 2%

profile of v1, /device:TPU:1, one launch (start us, length us, event | category | flops | bytes accessed | tf_op | source)
XLA Modules:
  0.0 80.4 jit_solution(16430253188727444522)
XLA Ops:
  0.6 0.0 copy-start
  0.6 0.0 copy-start.4
  0.7 1.9 %pack.1 = f32[104,128]{1,0:T(8,128)} custom-call(f32[768,128]{1,0:T(8,128)} %bitcast.14, f32[24,128]{1,0:T(8,128)} %bitcast.18, f32[8,128]{1,0:T(8,128)} %depth_ref.3), custom_call_target="tpu_custom_call" | custom-call | tf_op jit(solution)/shard_map/pack/pallas_call | solution.py:252
  2.5 4.8 %collective-permute-start.3 = (f32[104,128]{1,0:T(8,128)}, f32[104,128]{1,0:T(8,128)S(1)}, u32[]{:S(2)}, u32[]{:S(2)}) collective-permute-start(f32[104,128]{1,0:T(8,128)} %pack.1), channel_id=1, source_target_pairs={{0,1},{1,2},{2,3},{3,4},{4,5},{5,6},{6,7},{7,8},{8,9},{9,10},{10,1... | collective-permute-start | bytes 159752 | tf_op jit(solution)/shard_map/ppermute | solution.py:237
  7.3 10.8 %collective-permute-start.2 = (f32[104,128]{1,0:T(8,128)}, f32[104,128]{1,0:T(8,128)S(1)}, u32[]{:S(2)}, u32[]{:S(2)}) collective-permute-start(f32[104,128]{1,0:T(8,128)} %pack.1), channel_id=1, source_target_pairs={{0,31},{1,0},{2,1},{3,2},{4,3},{5,4},{6,5},{7,6},{8,7},{9,8},{10,9... | collective-permute-start | bytes 159752 | tf_op jit(solution)/shard_map/ppermute | solution.py:237
  18.1 0.0 copy-done
  18.1 2.9 %collective-permute-start.1 = (f32[768,128]{1,0:T(8,128)S(1)}, f32[768,128]{1,0:T(8,128)S(1)}, u32[]{:S(2)}, u32[]{:S(2)}) collective-permute-start(f32[768,128]{1,0:T(8,128)S(1)} %bitcast.16), channel_id=1, source_target_pairs={{32,0},{64,32},{96,64},{128,96},{160,128},{192,160},{224,192},{256... | collective-permute-start | bytes 1179656 | tf_op jit(solution)/shard_map/ppermute | solution.py:237
  21.0 3.1 %collective-permute-start = (f32[768,128]{1,0:T(8,128)S(1)}, f32[768,128]{1,0:T(8,128)S(1)}, u32[]{:S(2)}, u32[]{:S(2)}) collective-permute-start(f32[768,128]{1,0:T(8,128)S(1)} %bitcast.17), channel_id=1, source_target_pairs={{0,32},{32,64},{64,96},{96,128},{128,160},{160,192},{192,224},{224... | collective-permute-start | bytes 1179656 | tf_op jit(solution)/shard_map/ppermute | solution.py:237
  24.1 0.0 copy-done.4
  24.1 0.0 copy-start.7
  24.2 0.1 pad.4.clone
  24.2 0.6 copy-done.7
  24.8 0.1 maximum_bitcast_fusion
  24.9 0.0 collective-permute-done.3
  24.9 0.0 collective-permute-done.2
  24.9 0.0 copy-start.1
  25.0 0.6 copy-done.1
  25.6 1.9 %collective-permute-start.5 = (f32[168,128]{1,0:T(8,128)S(1)}, f32[168,128]{1,0:T(8,128)S(1)}, u32[]{:S(2)}, u32[]{:S(2)}) collective-permute-start(f32[168,128]{1,0:T(8,128)S(1)} %pad_maximum_fusion), channel_id=1, source_target_pairs={{32,0},{64,32},{96,64},{128,96},{160,128},{192,160},{224,192},{256... | collective-permute-start | bytes 258056 | tf_op jit(solution)/shard_map/ppermute | solution.py:237
  27.5 3.6 %collective-permute-start.4 = (f32[168,128]{1,0:T(8,128)S(1)}, f32[168,128]{1,0:T(8,128)S(1)}, u32[]{:S(2)}, u32[]{:S(2)}) collective-permute-start(f32[168,128]{1,0:T(8,128)S(1)} %pad_maximum_fusion), channel_id=1, source_target_pairs={{0,32},{32,64},{64,96},{96,128},{128,160},{160,192},{192,224},{224... | collective-permute-start | bytes 258056 | tf_op jit(solution)/shard_map/ppermute | solution.py:237
  31.8 1.5 %obs.1.weight_ref = f32[16,128]{1,0:T(8,128)} custom-call(s32[1]{0:T(128)S(6)} %copy.13.count_ref, s32[1,256]{1,0:T(1,128)} %bitcast.21, f32[1,256]{1,0:T(1,128)} %bitcast.22, f32[1,256]{1,0:T(1,128)} %bitcast.23), custom_call_target="tpu_custom_call" | custom-call | tf_op jit(solution)/shard_map/obs/pallas_call | solution.py:267
  33.3 0.0 collective-permute-done.5.south_edge_ref
  33.3 0.0 copy-start.5
  33.3 0.0 collective-permute-done.4.north_edge_ref
  33.3 0.0 copy-start.6
  33.3 0.0 collective-permute-done.1.south_ref
  33.3 0.0 copy-start.2
  33.3 0.0 collective-permute-done.north_ref
  33.4 0.6 copy-done.5
  33.9 0.0 copy-done.6
  34.0 0.1 copy-done.2
  34.1 0.0 copy-start.3
  34.1 0.7 copy-done.3
  34.9 8.3 %forecast.1 = (bf16[96,3072]{1,0:T(8,128)(2,1)}, f32[24,128]{1,0:T(8,128)}, f32[8,128]{1,0:T(8,128)}) custom-call(f32[768,128]{1,0:T(8,128)} %bitcast.15, f32[768,128]{1,0:T(8,128)} %copy-done.3, f32[768,128]{1,0:T(8,128)} %copy-done.2, f32[24,128]{1,0:T(8,128)} %bitcast.19, f32[8,128]{1,0:T(8,128)} %depth_ref.3, f32[104,128]{1,0:T(8,128)} %copy-done.1, ...), custom_call_target="tpu_custom_call" | custom-call | tf_op jit(solution)/shard_map/forecast/pallas_call | solution.py:270
  43.2 0.7 broadcast_in_dim.20
  43.9 17.6 %all_to_all.10 = f32[16,8,128]{2,1,0:T(8,128)S(1)} all-to-all(f32[16,8,128]{2,1,0:T(8,128)S(1)} %broadcast_in_dim.20), channel_id=1, replica_groups=mesh['lat'=16,'lon'=32] {'lat'}, dimensions={0} | all-to-all | bytes 131072 | tf_op jit(solution)/shard_map/all_to_all | solution.py:243
  61.5 13.9 %all_to_all.11.parts_ref = f32[32,8,128]{2,1,0:T(8,128)} all-to-all(f32[32,8,128]{2,1,0:T(8,128)S(1)} %broadcast_in_dim.21), channel_id=1, replica_groups=mesh['lat'=16,'lon'=32] {'lon'}, dimensions={0} | all-to-all | bytes 262144 | tf_op jit(solution)/shard_map/all_to_all | solution.py:243
  75.4 5.0 %analysis.1 = (f32[24,128]{1,0:T(8,128)}, f32[768,128]{1,0:T(8,128)}) custom-call(f32[32,8,128]{2,1,0:T(8,128)} %all_to_all.11.parts_ref, bf16[96,3072]{1,0:T(8,128)(2,1)} %get-tuple-element.8.split_ref, f32[24,128]{1,0:T(8,128)} %get-tuple-element.9.mean_ref), custom_call_target="tpu_custom_call" | custom-call | tf_op jit(solution)/shard_map/analysis/pallas_call | solution.py:289
  (7 shorter events, 0.1 us)
Async XLA Ops:
  0.6 17.5 %copy-start = (f32[32,3,8,128]{3,2,1,0:T(8,128)S(1)}, f32[32,3,8,128]{3,2,1,0:T(8,128)}, u32[]{:S(2)}) copy-start(f32[32,3,8,128]{3,2,1,0:T(8,128)} %param.8) | copy-start | bytes 1179652
  0.6 23.5 %copy-start.4 = (f32[3,8,128]{2,1,0:T(8,128)S(1)}, f32[3,8,128]{2,1,0:T(8,128)}, u32[]{:S(2)}) copy-start(f32[3,8,128]{2,1,0:T(8,128)} %param.7) | copy-start | bytes 36868
  2.5 22.4 %collective-permute-start.3 = (f32[104,128]{1,0:T(8,128)}, f32[104,128]{1,0:T(8,128)S(1)}, u32[]{:S(2)}, u32[]{:S(2)}) collective-permute-start(f32[104,128]{1,0:T(8,128)} %pack.1), channel_id=1, source_target_pairs={{0,1},{1,2},{2,3},{3,4},{4,5},{5,6},{6,7},{7,8},{8,9},{9,10},{10,1... | collective-permute-start | bytes 159752 | tf_op jit(solution)/shard_map/ppermute | solution.py:237
  7.3 17.6 %collective-permute-start.2 = (f32[104,128]{1,0:T(8,128)}, f32[104,128]{1,0:T(8,128)S(1)}, u32[]{:S(2)}, u32[]{:S(2)}) collective-permute-start(f32[104,128]{1,0:T(8,128)} %pack.1), channel_id=1, source_target_pairs={{0,31},{1,0},{2,1},{3,2},{4,3},{5,4},{6,5},{7,6},{8,7},{9,8},{10,9... | collective-permute-start | bytes 159752 | tf_op jit(solution)/shard_map/ppermute | solution.py:237
  18.1 15.2 %collective-permute-start.1 = (f32[768,128]{1,0:T(8,128)S(1)}, f32[768,128]{1,0:T(8,128)S(1)}, u32[]{:S(2)}, u32[]{:S(2)}) collective-permute-start(f32[768,128]{1,0:T(8,128)S(1)} %bitcast.16), channel_id=1, source_target_pairs={{32,0},{64,32},{96,64},{128,96},{160,128},{192,160},{224,192},{256... | collective-permute-start | bytes 1179656 | tf_op jit(solution)/shard_map/ppermute | solution.py:237
  21.0 12.3 %collective-permute-start = (f32[768,128]{1,0:T(8,128)S(1)}, f32[768,128]{1,0:T(8,128)S(1)}, u32[]{:S(2)}, u32[]{:S(2)}) collective-permute-start(f32[768,128]{1,0:T(8,128)S(1)} %bitcast.17), channel_id=1, source_target_pairs={{0,32},{32,64},{64,96},{96,128},{128,160},{160,192},{192,224},{224... | collective-permute-start | bytes 1179656 | tf_op jit(solution)/shard_map/ppermute | solution.py:237
  24.1 0.7 copy-start.7
  24.9 0.6 copy-start.1
  25.6 7.8 %collective-permute-start.5 = (f32[168,128]{1,0:T(8,128)S(1)}, f32[168,128]{1,0:T(8,128)S(1)}, u32[]{:S(2)}, u32[]{:S(2)}) collective-permute-start(f32[168,128]{1,0:T(8,128)S(1)} %pad_maximum_fusion), channel_id=1, source_target_pairs={{32,0},{64,32},{96,64},{128,96},{160,128},{192,160},{224,192},{256... | collective-permute-start | bytes 258056 | tf_op jit(solution)/shard_map/ppermute | solution.py:237
  27.5 5.8 %collective-permute-start.4 = (f32[168,128]{1,0:T(8,128)S(1)}, f32[168,128]{1,0:T(8,128)S(1)}, u32[]{:S(2)}, u32[]{:S(2)}) collective-permute-start(f32[168,128]{1,0:T(8,128)S(1)} %pad_maximum_fusion), channel_id=1, source_target_pairs={{0,32},{32,64},{64,96},{96,128},{128,160},{160,192},{192,224},{224... | collective-permute-start | bytes 258056 | tf_op jit(solution)/shard_map/ppermute | solution.py:237
  33.3 0.6 copy-start.5
  33.3 0.7 copy-start.6
  33.3 0.8 copy-start.2
  34.1 0.7 copy-start.3

commit v2 on v1

--- a/solution.py
+++ b/solution.py
@@ -231,6 +231,10 @@
     return jax.ShapeDtypeStruct(shape, jnp.float32)
 
 
+def on_chip(value):
+    return pltpu.with_memory_space_constraint(value, pltpu.VMEM)
+
+
 def shift_by(value, axis, step, periodic):
     count = lax.axis_size(axis)
     pairs = [(i, (i + step) % count) for i in range(count) if periodic or 0 <= i + step < count]
@@ -247,10 +251,10 @@
     background_expectation, factor, average_thickness, obs_cells, obs_count, obs_values, obs_error
 ):
     assert factor.shape == (RANK, 3, ROWS, LANES)
-    own = factor.reshape(RANK * PLANES, LANES)
+    own = on_chip(factor.reshape(RANK * PLANES, LANES))
     mean = background_expectation.reshape(PLANES, LANES)
     edges = pl.pallas_call(
-        pack_kernel, out_shape=f32(PACK, LANES), in_specs=[VMEM] * 3, out_specs=VMEM, name="pack"
+        pack_kernel, out_shape=pltpu.VMEM((PACK, LANES), jnp.float32), in_specs=[VMEM] * 3, out_specs=VMEM, name="pack"
     )(own, mean, average_thickness)
     from_west = shift_by(edges, "lon", 1, True)
     from_east = shift_by(edges, "lon", -1, True)
@@ -265,14 +269,14 @@
     south_corner = shift_by(corner, "lat", -1, False)
     slots = obs_cells.shape[0]
     weights = pl.pallas_call(
-        obs_kernel, out_shape=f32(2 * ROWS, LANES), in_specs=[SMEM] + [VMEM] * 3, out_specs=VMEM, name="obs"
+        obs_kernel, out_shape=pltpu.VMEM((2 * ROWS, LANES), jnp.float32), in_specs=[SMEM] + [VMEM] * 3, out_specs=VMEM, name="obs"
     )(obs_count, obs_cells.reshape(1, slots), obs_values.reshape(1, slots), obs_error.reshape(1, slots))
     split, mean, gram = pl.pallas_call(
         forecast_kernel,
         out_shape=(
-            jax.ShapeDtypeStruct((3 * RANK, PLANES * LANES), jnp.bfloat16),
-            f32(PLANES, LANES),
-            f32(8, LANES),
+            pltpu.VMEM((3 * RANK, PLANES * LANES), jnp.bfloat16),
+            pltpu.VMEM((PLANES, LANES), jnp.float32),
+            pltpu.VMEM((8, LANES), jnp.float32),
         ),
         in_specs=[VMEM] * 9,
         out_specs=(VMEM,) * 3,
@@ -283,7 +287,10 @@
             pltpu.VMEM((RANK + 8, ROWS * LANES), jnp.float32),
         ],
         name="forecast",
-    )(own, from_north, from_south, mean, average_thickness, halo, north_corner, south_corner, weights)
+    )(
+        own, on_chip(from_north), on_chip(from_south), mean, average_thickness,
+        on_chip(halo), on_chip(north_corner), on_chip(south_corner), weights,
+    )
     gram = jnp.sum(sum_over(gram, "lat"), 0)
     parts = sum_over(gram, "lon")
     update, analysis = pl.pallas_call(
@@ -292,7 +299,7 @@
         in_specs=[VMEM] * 3,
         out_specs=(VMEM, VMEM),
         name="analysis",
-    )(parts, split, mean)
+    )(on_chip(parts), split, mean)
     return update.reshape(background_expectation.shape), analysis.reshape(factor.shape)
 
 

time: 80.9 us -> 76.8 us (0.949)
  Pallas kernels: 16.8 us -> 14.4 us
  local copies, waits for them, and re-layouts: 3.48 us -> 1.94 us
    pallas_call x3, Pallas kernels: 11.7 us -> 9.37 us  [the longest x1 7.27 us: per_device(): pl.pallas_call(forecast_kernel, out_shape=(pltpu.VMEM((3 * RANK, PLANES *...]
    unnamed x17 -> x11, local copies, waits for them, and re-layouts: 2.71 us -> 1.84 us
  transfers between devices with their start and end apart: 6 -> 6, of which waited for: 0 -> 0; matrix products, arithmetic and copies ran while one was open for 0% -> 0% of each run, Pallas kernels for 2% -> 1%
where the time goes in v2:
time: 76.8 us; the launch traced here: 76.4 us
  blocking collectives  31.4 us (41%)
  starting transfers between devices  27.1 us (35%)
  Pallas kernels  14.4 us (19%)
  local copies, waits for them, and re-layouts  1.94 us (3%)
  between operations  1.41 us (2%)
    all_to_all x2, blocking collectives, sum_over(): return lax.all_to_all(sent, axis, 0, 0)  31.4 us
    ppermute x6, starting transfers between devices, shift_by(): return lax.ppermute(value, axis, pairs)  27.1 us
    pallas_call x1, Pallas kernels, per_device(): pl.pallas_call(forecast_kernel, out_shape=(pltpu.VMEM((3 * RANK, PLANES *...  7.27 us
    pallas_call x1, Pallas kernels, per_device(): pl.pallas_call(analysis_kernel, out_shape=(f32(PLANES, LANES), f32(RANK *...  5.01 us
    unnamed x11, local copies, waits for them, and re-layouts  1.84 us
  transfers between devices with their start and end apart: 6, of which 0 were waited for; matrix products, arithmetic and copies ran while one was open for 0% of the time, Pallas kernels for 1%

profile of v2, /device:TPU:1, one launch (start us, length us, event | category | flops | bytes accessed | tf_op | source)
XLA Modules:
  0.0 76.4 jit_solution(1568112422126112065)
XLA Ops:
  0.6 0.0 copy-start.3
  0.6 1.2 %pack.1 = f32[104,128]{1,0:T(8,128)S(1)} custom-call(f32[768,128]{1,0:T(8,128)} %bitcast.factor_ref.own_ref, f32[24,128]{1,0:T(8,128)} %bitcast.14, f32[8,128]{1,0:T(8,128)} %depth_ref.3), custom_call_target="tpu_custom_call" | custom-call | tf_op jit(solution)/shard_map/pack/pallas_call | solution.py:256
  1.8 4.8 %collective-permute-start.3 = (f32[104,128]{1,0:T(8,128)S(1)}, f32[104,128]{1,0:T(8,128)S(1)}, u32[]{:S(2)}, u32[]{:S(2)}) collective-permute-start(f32[104,128]{1,0:T(8,128)S(1)} %pack.1), channel_id=1, source_target_pairs={{0,1},{1,2},{2,3},{3,4},{4,5},{5,6},{6,7},{7,8},{8,9},{9,10},{10,1... | collective-permute-start | bytes 159752 | tf_op jit(solution)/shard_map/ppermute | solution.py:241
  6.7 10.8 %collective-permute-start.2 = (f32[104,128]{1,0:T(8,128)S(1)}, f32[104,128]{1,0:T(8,128)S(1)}, u32[]{:S(2)}, u32[]{:S(2)}) collective-permute-start(f32[104,128]{1,0:T(8,128)S(1)} %pack.1), channel_id=1, source_target_pairs={{0,31},{1,0},{2,1},{3,2},{4,3},{5,4},{6,5},{7,6},{8,7},{9,8},{10,9... | collective-permute-start | bytes 159752 | tf_op jit(solution)/shard_map/ppermute | solution.py:241
  17.5 2.9 %collective-permute-start.1 = (f32[768,128]{1,0:T(8,128)}, f32[768,128]{1,0:T(8,128)S(1)}, u32[]{:S(2)}, u32[]{:S(2)}) collective-permute-start(f32[768,128]{1,0:T(8,128)} %bitcast.factor_ref.own_ref), channel_id=1, source_target_pairs={{32,0},{64,32},{96,64},{128,96},{160,128},{192,160},{224,192},{256... | collective-permute-start | bytes 1179656 | tf_op jit(solution)/shard_map/ppermute | solution.py:241
  20.3 3.1 %collective-permute-start = (f32[768,128]{1,0:T(8,128)}, f32[768,128]{1,0:T(8,128)S(1)}, u32[]{:S(2)}, u32[]{:S(2)}) collective-permute-start(f32[768,128]{1,0:T(8,128)} %bitcast.factor_ref.own_ref), channel_id=1, source_target_pairs={{0,32},{32,64},{64,96},{96,128},{128,160},{160,192},{192,224},{224... | collective-permute-start | bytes 1179656 | tf_op jit(solution)/shard_map/ppermute | solution.py:241
  23.4 0.0 copy-done.3
  23.5 0.0 copy-start.4
  23.5 0.1 pad.4.clone
  23.6 0.6 copy-done.4
  24.2 0.1 maximum_bitcast_fusion
  24.2 0.0 collective-permute-done.3
  24.2 0.0 collective-permute-done.2
  24.3 1.9 %collective-permute-start.5 = (f32[168,128]{1,0:T(8,128)S(1)}, f32[168,128]{1,0:T(8,128)S(1)}, u32[]{:S(2)}, u32[]{:S(2)}) collective-permute-start(f32[168,128]{1,0:T(8,128)S(1)} %pad_maximum_fusion), channel_id=1, source_target_pairs={{32,0},{64,32},{96,64},{128,96},{160,128},{192,160},{224,192},{256... | collective-permute-start | bytes 258056 | tf_op jit(solution)/shard_map/ppermute | solution.py:241
  26.2 3.6 %collective-permute-start.4 = (f32[168,128]{1,0:T(8,128)S(1)}, f32[168,128]{1,0:T(8,128)S(1)}, u32[]{:S(2)}, u32[]{:S(2)}) collective-permute-start(f32[168,128]{1,0:T(8,128)S(1)} %pad_maximum_fusion), channel_id=1, source_target_pairs={{0,32},{32,64},{64,96},{96,128},{128,160},{160,192},{192,224},{224... | collective-permute-start | bytes 258056 | tf_op jit(solution)/shard_map/ppermute | solution.py:241
  30.5 0.9 %obs.1.weight_ref = f32[16,128]{1,0:T(8,128)S(1)} custom-call(s32[1]{0:T(128)S(6)} %copy.13.count_ref, s32[1,256]{1,0:T(1,128)} %bitcast.17, f32[1,256]{1,0:T(1,128)} %bitcast.18, f32[1,256]{1,0:T(1,128)} %bitcast.19), custom_call_target="tpu_custom_call" | custom-call | tf_op jit(solution)/shard_map/obs/pallas_call | solution.py:271
  31.4 0.0 copy-start.1
  31.4 0.6 copy-done.1
  32.1 0.0 collective-permute-done.5.south_edge_ref
  32.1 0.0 collective-permute-done.4.north_edge_ref
  32.1 0.0 collective-permute-done.1.south_ref
  32.1 0.0 collective-permute-done.north_ref
  32.1 7.3 %forecast.1 = (bf16[96,3072]{1,0:T(8,128)(2,1)S(1)}, f32[24,128]{1,0:T(8,128)S(1)}, f32[8,128]{1,0:T(8,128)S(1)}) custom-call(f32[768,128]{1,0:T(8,128)} %bitcast.factor_ref.own_ref, f32[768,128]{1,0:T(8,128)S(1)} %collective-permute-done.north_ref, f32[768,128]{1,0:T(8,128)S(1)} %collective-permute-done.1.south_ref, f32[24,128]{1,0:T(8,128)} %bitcast.15, ...), custom_call_target="tpu_custom_call" | custom-call | tf_op jit(solution)/shard_map/forecast/pallas_call | solution.py:274
  39.3 0.0 copy-start.2
  39.3 0.6 copy-done.2
  39.9 0.0 copy-start
  40.0 17.6 %all_to_all.10 = f32[16,8,128]{2,1,0:T(8,128)S(1)} all-to-all(f32[16,8,128]{2,1,0:T(8,128)S(1)} %broadcast_in_dim.20), channel_id=1, replica_groups=mesh['lat'=16,'lon'=32] {'lat'}, dimensions={0} | all-to-all | bytes 131072 | tf_op jit(solution)/shard_map/all_to_all | solution.py:247
  57.6 13.8 %all_to_all.11.parts_ref = f32[32,8,128]{2,1,0:T(8,128)S(1)} all-to-all(f32[32,8,128]{2,1,0:T(8,128)S(1)} %broadcast_in_dim.21), channel_id=1, replica_groups=mesh['lat'=16,'lon'=32] {'lon'}, dimensions={0} | all-to-all | bytes 262144 | tf_op jit(solution)/shard_map/all_to_all | solution.py:247
  71.4 0.0 copy-done
  71.4 5.0 %analysis.1 = (f32[24,128]{1,0:T(8,128)}, f32[768,128]{1,0:T(8,128)}) custom-call(f32[32,8,128]{2,1,0:T(8,128)S(1)} %all_to_all.11.parts_ref, bf16[96,3072]{1,0:T(8,128)(2,1)} %copy-done, f32[24,128]{1,0:T(8,128)} %copy-done.2), custom_call_target="tpu_custom_call" | custom-call | tf_op jit(solution)/shard_map/analysis/pallas_call | solution.py:296
  (8 shorter events, 0.1 us)
Async XLA Ops:
  0.6 22.8 %copy-start.3 = (f32[3,8,128]{2,1,0:T(8,128)S(1)}, f32[3,8,128]{2,1,0:T(8,128)}, u32[]{:S(2)}) copy-start(f32[3,8,128]{2,1,0:T(8,128)} %param.7) | copy-start | bytes 36868
  1.8 22.4 %collective-permute-start.3 = (f32[104,128]{1,0:T(8,128)S(1)}, f32[104,128]{1,0:T(8,128)S(1)}, u32[]{:S(2)}, u32[]{:S(2)}) collective-permute-start(f32[104,128]{1,0:T(8,128)S(1)} %pack.1), channel_id=1, source_target_pairs={{0,1},{1,2},{2,3},{3,4},{4,5},{5,6},{6,7},{7,8},{8,9},{9,10},{10,1... | collective-permute-start | bytes 159752 | tf_op jit(solution)/shard_map/ppermute | solution.py:241
  6.7 17.6 %collective-permute-start.2 = (f32[104,128]{1,0:T(8,128)S(1)}, f32[104,128]{1,0:T(8,128)S(1)}, u32[]{:S(2)}, u32[]{:S(2)}) collective-permute-start(f32[104,128]{1,0:T(8,128)S(1)} %pack.1), channel_id=1, source_target_pairs={{0,31},{1,0},{2,1},{3,2},{4,3},{5,4},{6,5},{7,6},{8,7},{9,8},{10,9... | collective-permute-start | bytes 159752 | tf_op jit(solution)/shard_map/ppermute | solution.py:241
  17.5 14.6 %collective-permute-start.1 = (f32[768,128]{1,0:T(8,128)}, f32[768,128]{1,0:T(8,128)S(1)}, u32[]{:S(2)}, u32[]{:S(2)}) collective-permute-start(f32[768,128]{1,0:T(8,128)} %bitcast.factor_ref.own_ref), channel_id=1, source_target_pairs={{32,0},{64,32},{96,64},{128,96},{160,128},{192,160},{224,192},{256... | collective-permute-start | bytes 1179656 | tf_op jit(solution)/shard_map/ppermute | solution.py:241
  20.3 11.7 %collective-permute-start = (f32[768,128]{1,0:T(8,128)}, f32[768,128]{1,0:T(8,128)S(1)}, u32[]{:S(2)}, u32[]{:S(2)}) collective-permute-start(f32[768,128]{1,0:T(8,128)} %bitcast.factor_ref.own_ref), channel_id=1, source_target_pairs={{0,32},{32,64},{64,96},{96,128},{128,160},{160,192},{192,224},{224... | collective-permute-start | bytes 1179656 | tf_op jit(solution)/shard_map/ppermute | solution.py:241
  23.5 0.7 copy-start.4
  24.3 7.8 %collective-permute-start.5 = (f32[168,128]{1,0:T(8,128)S(1)}, f32[168,128]{1,0:T(8,128)S(1)}, u32[]{:S(2)}, u32[]{:S(2)}) collective-permute-start(f32[168,128]{1,0:T(8,128)S(1)} %pad_maximum_fusion), channel_id=1, source_target_pairs={{32,0},{64,32},{96,64},{128,96},{160,128},{192,160},{224,192},{256... | collective-permute-start | bytes 258056 | tf_op jit(solution)/shard_map/ppermute | solution.py:241
  26.2 5.8 %collective-permute-start.4 = (f32[168,128]{1,0:T(8,128)S(1)}, f32[168,128]{1,0:T(8,128)S(1)}, u32[]{:S(2)}, u32[]{:S(2)}) collective-permute-start(f32[168,128]{1,0:T(8,128)S(1)} %pad_maximum_fusion), channel_id=1, source_target_pairs={{0,32},{32,64},{64,96},{96,128},{128,160},{160,192},{192,224},{224... | collective-permute-start | bytes 258056 | tf_op jit(solution)/shard_map/ppermute | solution.py:241
  31.4 0.6 copy-start.1
  39.3 0.6 copy-start.2
  39.9 31.4 %copy-start = (bf16[96,3072]{1,0:T(8,128)(2,1)}, bf16[96,3072]{1,0:T(8,128)(2,1)S(1)}, u32[]{:S(2)}) copy-start(bf16[96,3072]{1,0:T(8,128)(2,1)S(1)} %get-tuple-element.8.split_ref) | copy-start | bytes 1769476

commit v3 on v2

v3 whole, which is shorter than its diff:
```python
import functools

import jax
import jax.numpy as jnp
from jax import lax
from jax.experimental import pallas as pl
from jax.experimental.pallas import tpu as pltpu
from jax.sharding import PartitionSpec as P

STEPS = 4
TIME_STEP = 0.9
ROTATION = 0.25

RANK = 32
ROWS = 8
LANES = 128
HALO = 2 * STEPS
TILES = RANK // 8
PLANES = 3 * ROWS
GROUP = LANES // TILES
MAIN, SMALL, SIDE = 0, 12, 13
PER_ROW = 17
PULL = 0.5 * TIME_STEP
WIDTH = 4
HIGHEST = lax.Precision.HIGHEST
NT = (((1,), (1,)), ((), ()))


def lane_iota():
    return lax.broadcasted_iota(jnp.int32, (8, LANES), 1)


def member_rows(field, row, tile):
    return pl.ds(8 * tile * PLANES + field * ROWS + row, 8, stride=PLANES)


def block_at(row, tile):
    return pl.ds((row * PER_ROW + tile) * 8, 8)


def pack_kernel(factor_ref, mean_ref, depth_ref, block_ref, edge_ref):
    lane = lane_iota()
    part = lane // GROUP
    even = ((lane - 8) & 16) == 0
    kept = {}
    for row in range(ROWS):
        small = jnp.concatenate(
            [mean_ref[f * ROWS + row : f * ROWS + row + 1, :] for f in range(3)]
            + [depth_ref[row : row + 1, :]] * 5,
            0,
        )
        block_ref[block_at(row, SMALL), :] = small
        sides = []
        for field in range(3):
            side = None
            for tile in range(TILES):
                value = factor_ref[member_rows(field, row, tile), :]
                block_ref[block_at(row, MAIN + TILES * field + tile), :] = value
                moved = pltpu.roll(value, 16 + GROUP * tile, 1)
                side = moved if side is None else jnp.where(part == tile, moved, side)
            sides.append(side)
        side = pltpu.roll(small, 16, 1)
        side = jnp.where(part == 0, side, pltpu.roll(side, GROUP, 1))
        sides.append(jnp.where(part < 2, side, pltpu.roll(side, 2 * GROUP, 1)))
        for which, side in enumerate(sides):
            block_ref[block_at(row, SIDE + which), :] = side
            if row % 2 == 0:
                kept[which] = side
            else:
                at = pl.ds(((row // 2) * 4 + which) * 8, 8)
                edge_ref[at, :] = jnp.where(even, kept[which], pltpu.roll(side, 16, 1))


def pulls():
    band = lax.axis_index("lat")
    bands = lax.axis_size("lat")
    north = jnp.where(band > 0, PULL, 0.0)
    south = jnp.where(band < bands - 1, PULL, 0.0)
    return north, south


def lon_difference(value):
    return pltpu.roll(value, LANES - 1, 1) - pltpu.roll(value, 1, 1)


def advance(states, row_pulls):
    north_pull, south_pull = row_pulls
    for step in range(STEPS):
        first, last = 1 + 2 * step, 3 * ROWS - 2 - 2 * step
        for state, depth in states:
            h, e, n = (state.at[field] for field in range(3))
            for row in range(first, last + 1):
                divergence = lon_difference(e[row]) + (n[row + 1] - n[row - 1])
                h[row] = h[row] - depth[row] * divergence
        for state, depth in states:
            h, e, n = (state.at[field] for field in range(3))
            for row in range(first + 1, last):
                row_pull = north_pull if row < ROWS else south_pull if row >= 2 * ROWS else PULL
                east, north = e[row], n[row]
                e[row] = east - PULL * lon_difference(h[row]) + ROTATION * north
                n[row] = north - row_pull * (h[row + 1] - h[row - 1]) - ROTATION * east


def observed(count_ref, cells_ref, values_ref, error_ref):
    slots = cells_ref.shape[1]
    live = lax.broadcasted_iota(jnp.int32, (1, slots), 1) < count_ref[0]
    weight = jnp.where(live, 1.0, 0.0) / error_ref[...]
    square = weight * weight
    cells = cells_ref[...]
    row_of = cells // LANES
    lane_of = cells - row_of * LANES
    in_row = lax.broadcasted_iota(jnp.int32, (ROWS, slots), 0) == row_of
    spread = jnp.concatenate(
        [jnp.where(in_row, square, 0.0), jnp.where(in_row, square * values_ref[...], 0.0)], 0
    )
    in_lane = lax.broadcasted_iota(jnp.int32, (LANES, slots), 0) == lane_of
    return lax.dot_general(
        spread, jnp.where(in_lane, 1.0, 0.0), NT, precision=HIGHEST, preferred_element_type=jnp.float32
    )


def inner_kernel(
    count_ref, own_ref, north_ref, south_ref, cells_ref, values_ref, error_ref, out_ref, weight_ref, state, depth
):
    blocks = (north_ref, own_ref, south_ref)
    for block, ref in enumerate(blocks):
        for row in range(ROWS):
            depth[ROWS * block + row] = PULL * jnp.broadcast_to(
                ref[pl.ds((row * PER_ROW + SMALL) * 8 + 3, 1), :], (8, LANES)
            )
    weight_ref[...] = observed(count_ref, cells_ref, values_ref, error_ref)
    row_pulls = pulls()

    def pair(which, carry):
        for half in range(2):
            tile = 2 * which + half
            for block, ref in enumerate(blocks):
                for field in range(3):
                    for row in range(ROWS):
                        at = pl.multiple_of((row * PER_ROW + MAIN + TILES * field + tile) * 8, 8)
                        state[half, field, ROWS * block + row] = ref[pl.ds(at, 8), :]
        advance([(state.at[half], depth) for half in range(2)], row_pulls)
        for half in range(2):
            tile = 2 * which + half
            for field in range(3):
                for row in range(ROWS):
                    at = pl.multiple_of(((field * ROWS + row) * TILES + tile) * 8, 8)
                    out_ref[pl.ds(at, 8), :] = state[half, field, ROWS + row]
        return carry

    lax.fori_loop(0, TILES // 2, pair, 0)


def side_kernel(
    own_ref, north_ref, south_ref, halo_ref, north_halo_ref, south_halo_ref, inner_ref, weight_ref,
    split_ref, mean_out_ref, gram_ref, state, depth, heights, scaled,
):
    lane = lane_iota()
    low_lanes = (lane & 16) == 0
    sub = lax.broadcasted_iota(jnp.int32, (8, LANES), 0)
    blocks = ((north_ref, north_halo_ref), (own_ref, halo_ref), (south_ref, south_halo_ref))
    for block, (ref, halos) in enumerate(blocks):
        for row in range(ROWS):
            at = ROWS * block + row
            for which in range(4):
                side = ref[block_at(row, SIDE + which), :]
                halo = halos[pl.ds(((row // 2) * 4 + which) * 8, 8), :]
                if row % 2:
                    halo = pltpu.roll(halo, LANES - 16, 1)
                right = jnp.where(low_lanes, side, halo)
                left = jnp.where(low_lanes, halo, side)
                if which < 3:
                    state[0, which, at] = right
                    state[1, which, at] = left
                else:
                    small = ref[block_at(row, SMALL), :]
                    for field in range(3):
                        state[2, field, at] = jnp.where(
                            sub == 0,
                            jnp.broadcast_to(small[field : field + 1, :], (8, LANES)),
                            jnp.where(
                                sub == 1,
                                jnp.broadcast_to(right[field : field + 1, :], (8, LANES)),
                                jnp.broadcast_to(left[field : field + 1, :], (8, LANES)),
                            ),
                        )
                    depth[0, at] = PULL * jnp.broadcast_to(right[3:4, :], (8, LANES))
                    depth[1, at] = PULL * jnp.broadcast_to(left[3:4, :], (8, LANES))
                    whole = PULL * jnp.broadcast_to(small[3:4, :], (8, LANES))
                    depth[2, at] = jnp.where(sub == 0, whole, jnp.where(sub == 1, depth[0, at], depth[1, at]))
    advance([(state.at[which], depth.at[which]) for which in range(3)], pulls())

    from_right = (lane & 16) == 0
    edge = (lane < HALO) | (lane >= LANES - HALO)
    for field in range(3):
        for row in range(ROWS):
            plane = field * ROWS + row
            cols = slice(plane * LANES, (plane + 1) * LANES)
            sides = jnp.where(from_right, state[0, field, ROWS + row], state[1, field, ROWS + row])
            full = jnp.concatenate(
                [
                    jnp.where(
                        edge,
                        pltpu.roll(sides, (LANES - 16 - GROUP * tile) % LANES, 1),
                        inner_ref[pl.ds((plane * TILES + tile) * 8, 8), :],
                    )
                    for tile in range(TILES)
                ],
                0,
            )
            high = full.astype(jnp.bfloat16)
            rest = full - high.astype(jnp.float32)
            middle = rest.astype(jnp.bfloat16)
            split_ref[0:RANK, cols] = high
            split_ref[RANK : 2 * RANK, cols] = middle
            split_ref[2 * RANK : 3 * RANK, cols] = (rest - middle.astype(jnp.float32)).astype(jnp.bfloat16)
            mine = state[2, field, ROWS + row]
            both = jnp.where(from_right[0:1], mine[1:2, :], mine[2:3, :])
            mean = jnp.where(edge[0:1], pltpu.roll(both, LANES - 16, 1), mine[0:1, :])
            mean_out_ref[plane : plane + 1, :] = mean
            if field == 0:
                square = weight_ref[row : row + 1, :]
                heights[:, cols] = full
                scaled[0:RANK, cols] = full * square
                pulled = weight_ref[ROWS + row : ROWS + row + 1, :] - square * mean
                scaled[RANK : RANK + 8, cols] = jnp.broadcast_to(pulled, (8, LANES))
    gram = lax.dot_general(
        heights[...], scaled[...], NT, precision=HIGHEST, preferred_element_type=jnp.float32
    )
    gram = jnp.concatenate([gram, jnp.zeros((RANK, LANES - RANK - 8), jnp.float32)], 1)
    acc = None
    for tile in range(TILES):
        part = gram[8 * tile : 8 * tile + 8, :]
        if tile < 2:
            far = gram[8 * tile + 16 : 8 * tile + 24, :]
            part = jnp.where(lane == 31, pltpu.roll(part, LANES - 1, 1), part)
            part = jnp.where(lane == 30, pltpu.roll(far, LANES - 2, 1), part)
        moved = pltpu.roll(part, 32 * tile, 1) if tile else part
        acc = moved if acc is None else jnp.where(lane // 32 == tile, moved, acc)
    gram_ref[...] = acc


def analysis_kernel(parts_ref, split_ref, mean_ref, update_ref, factor_ref):
    lane = lane_iota()
    total = jnp.sum(parts_ref[...], 0)
    tiles, drives = [], [None] * TILES
    for tile in range(TILES):
        part = pltpu.roll(total, LANES - 32 * tile, 1) if tile else total
        if tile < 2:
            drives[tile] = pltpu.roll(part, 2 * RANK - 31, 1)
            drives[tile + 2] = pltpu.roll(part, 2 * RANK - 30, 1)
        tiles.append(part)
    lower = jnp.concatenate(tiles, 0)
    wide = lax.broadcasted_iota(jnp.int32, (RANK, LANES), 1)
    deep = lax.broadcasted_iota(jnp.int32, (RANK, LANES), 0)
    mirrored = jnp.concatenate([lower, jnp.zeros((LANES - RANK, LANES), jnp.float32)], 0).T[0:RANK, :]
    work = jnp.where(wide > deep, mirrored, lower)
    work = jnp.where(wide < RANK, work, 0.0) + jnp.where((wide == deep) | (wide == deep + RANK), 1.0, 0.0)
    work = jnp.where(wide == 2 * RANK, jnp.concatenate(drives, 0), work)
    for first in range(0, RANK, WIDTH):
        columns = [jnp.broadcast_to(work[:, k : k + 1], (RANK, LANES)) for k in range(first, first + WIDTH)]
        rows = [work[k : k + 1, :] for k in range(first, first + WIDTH)]
        for j in range(WIDTH):
            k = first + j
            inverse = 1.0 / columns[j][k : k + 1, :]
            scaled_row = rows[j] * inverse
            for i in range(j + 1, WIDTH):
                ratio = columns[j][first + i : first + i + 1, :] * inverse
                rows[i] = rows[i] - ratio * rows[j]
                columns[i] = columns[i] - columns[j] * ratio
            work = work - jnp.where(deep > k, columns[j], 0.0) * scaled_row
    pivots = jnp.sum(jnp.where(wide == deep, work, 0.0), 1, keepdims=True)
    work = work * lax.rsqrt(pivots)
    shift = jnp.sum(work * work[:, 2 * RANK : 2 * RANK + 1], 0, keepdims=True)
    mixed = jnp.concatenate([work, jnp.broadcast_to(shift, (8, LANES))], 0)[:, RANK : 2 * RANK]
    high = mixed.astype(jnp.bfloat16)
    rest = mixed - high.astype(jnp.float32)
    middle = rest.astype(jnp.bfloat16)
    low = (rest - middle.astype(jnp.float32)).astype(jnp.bfloat16)
    left = jnp.concatenate([high, high, high, middle, middle, low], 1)
    split = split_ref[...]
    fine = jnp.concatenate([split, split[0 : 2 * RANK], split[0:RANK]], 0)
    out = jnp.dot(left, fine, preferred_element_type=jnp.float32)
    for plane in range(PLANES):
        cols = slice(plane * LANES, (plane + 1) * LANES)
        for tile in range(TILES):
            factor_ref[pl.ds(8 * tile * PLANES + plane, 8, stride=PLANES), :] = out[8 * tile : 8 * tile + 8, cols]
        update_ref[plane : plane + 1, :] = mean_ref[plane : plane + 1, :] + out[RANK : RANK + 1, cols]


VMEM = pl.BlockSpec(memory_space=pltpu.VMEM)
SMEM = pl.BlockSpec(memory_space=pltpu.SMEM)


def f32(*shape):
    return jax.ShapeDtypeStruct(shape, jnp.float32)


def chip(*shape):
    return pltpu.VMEM(shape, jnp.float32)


def on_chip(value):
    return pltpu.with_memory_space_constraint(value, pltpu.VMEM)


def shift_by(value, axis, step, periodic):
    count = lax.axis_size(axis)
    pairs = [(i, (i + step) % count) for i in range(count) if periodic or 0 <= i + step < count]
    return lax.ppermute(value, axis, pairs)


def sum_over(value, axis):
    count = lax.axis_size(axis)
    sent = jnp.broadcast_to(value[None], (count, *value.shape))
    return lax.all_to_all(sent, axis, 0, 0)


def per_device(
    background_expectation, factor, average_thickness, obs_cells, obs_count, obs_values, obs_error
):
    assert factor.shape == (RANK, 3, ROWS, LANES)
    block, edges = pl.pallas_call(
        pack_kernel,
        out_shape=(chip(ROWS * PER_ROW * 8, LANES), chip(ROWS * 16, LANES)),
        in_specs=[VMEM] * 3,
        out_specs=(VMEM, VMEM),
        name="pack",
    )(factor.reshape(RANK * PLANES, LANES), background_expectation.reshape(PLANES, LANES), average_thickness)
    block = on_chip(block)
    from_west = shift_by(edges, "lon", 1, True)
    from_east = shift_by(edges, "lon", -1, True)
    north = on_chip(shift_by(block, "lat", 1, False))
    south = on_chip(shift_by(block, "lat", -1, False))
    east_lane = (lax.broadcasted_iota(jnp.int32, (ROWS * 16, LANES), 1) & 8) == 0
    halo = jnp.where(east_lane, from_east, from_west)
    north_halo = on_chip(shift_by(halo, "lat", 1, False))
    south_halo = on_chip(shift_by(halo, "lat", -1, False))
    slots = obs_cells.shape[0]
    inner, weights = pl.pallas_call(
        inner_kernel,
        out_shape=(chip(RANK * PLANES, LANES), chip(2 * ROWS, LANES)),
        in_specs=[SMEM] + [VMEM] * 6,
        out_specs=(VMEM, VMEM),
        scratch_shapes=[
            pltpu.VMEM((2, 3, 3 * ROWS, 8, LANES), jnp.float32),
            pltpu.VMEM((3 * ROWS, 8, LANES), jnp.float32),
        ],
        name="inner",
    )(
        obs_count, block, north, south,
        obs_cells.reshape(1, slots), obs_values.reshape(1, slots), obs_error.reshape(1, slots),
    )
    split, mean, gram = pl.pallas_call(
        side_kernel,
        out_shape=(
            pltpu.VMEM((3 * RANK, PLANES * LANES), jnp.bfloat16),
            chip(PLANES, LANES),
            chip(8, LANES),
        ),
        in_specs=[VMEM] * 8,
        out_specs=(VMEM,) * 3,
        scratch_shapes=[
            pltpu.VMEM((3, 3, 3 * ROWS, 8, LANES), jnp.float32),
            pltpu.VMEM((3, 3 * ROWS, 8, LANES), jnp.float32),
            pltpu.VMEM((RANK, ROWS * LANES), jnp.float32),
            pltpu.VMEM((RANK + 8, ROWS * LANES), jnp.float32),
        ],
        name="side",
    )(block, north, south, on_chip(halo), north_halo, south_halo, on_chip(inner), on_chip(weights))
    gram = jnp.sum(sum_over(gram, "lat"), 0)
    parts = sum_over(gram, "lon")
    update, analysis = pl.pallas_call(
        analysis_kernel,
        out_shape=(f32(PLANES, LANES), f32(RANK * PLANES, LANES)),
        in_specs=[VMEM] * 3,
        out_specs=(VMEM, VMEM),
        name="analysis",
    )(on_chip(parts), on_chip(split), on_chip(mean))
    return update.reshape(background_expectation.shape), analysis.reshape(factor.shape)


def solution(mesh):
    return jax.shard_map(
        per_device,
        mesh=mesh,
        in_specs=(
            P(None, "lat", "lon"),
            P(None, None, "lat", "lon"),
            P("lat", "lon"),
            P(("lat", "lon")),
            P(("lat", "lon")),
            P(("lat", "lon")),
            P(("lat", "lon")),
        ),
        out_specs=(P(None, "lat", "lon"), P(None, None, "lat", "lon")),
        check_vma=False,
    )
```

time: 76.8 us -> 69.7 us (0.908)
  Pallas kernels: 14.4 us -> 7.41 us
  local copies, waits for them, and re-layouts: 1.94 us -> 0.02 us
  waiting for transfers between devices: 0.02 us -> 1.69 us
    pallas_call x3, Pallas kernels: 9.37 us -> 5 us  [the longest x1 2.28 us: per_device(): pl.pallas_call(inner_kernel, out_shape=(chip(RANK * PLANES, LANES), chip(...]
    pallas_call x1, Pallas kernels: 5.01 us -> 2.41 us  [per_device(): pl.pallas_call(analysis_kernel, out_shape=(f32(PLANES, LANES), f32(RANK *...]
    unnamed x11 -> x0, local copies, waits for them, and re-layouts: 1.84 us -> none
    ppermute x6, waiting for transfers between devices: 0.02 us -> 1.69 us  [shift_by(): return lax.ppermute(value, axis, pairs)]
  transfers between devices with their start and end apart: 6 -> 6, of which waited for: 0 -> 1; matrix products, arithmetic and copies ran while one was open for 0% -> 0% of each run, Pallas kernels for 1% -> 3%
where the time goes in v3:
time: 69.7 us; the launch traced here: 69.3 us
  blocking collectives  31.9 us (46%)
  starting transfers between devices  26.8 us (38%)
  Pallas kernels  7.41 us (11%)
  waiting for transfers between devices  1.69 us (2%)
  between operations  1.38 us (2%)
    all_to_all x2, blocking collectives, sum_over(): return lax.all_to_all(sent, axis, 0, 0)  31.9 us
    ppermute x6, starting transfers between devices, shift_by(): return lax.ppermute(value, axis, pairs)  26.8 us
    pallas_call x1, Pallas kernels, per_device(): pl.pallas_call(analysis_kernel, out_shape=(f32(PLANES, LANES), f32(RANK *...  2.41 us
    pallas_call x1, Pallas kernels, per_device(): pl.pallas_call(inner_kernel, out_shape=(chip(RANK * PLANES, LANES), chip(...  2.28 us
    ppermute x6, waiting for transfers between devices, shift_by(): return lax.ppermute(value, axis, pairs)  1.69 us
  transfers between devices with their start and end apart: 6, of which 1 were waited for; matrix products, arithmetic and copies ran while one was open for 0% of the time, Pallas kernels for 3%

profile of v3, /device:TPU:1, one launch (start us, length us, event | category | flops | bytes accessed | tf_op | source)
XLA Modules:
  0.0 69.3 jit_solution(1377925673916576677)
XLA Ops:
  0.6 1.3 %pack.1 = (f32[1088,128]{1,0:T(8,128)S(1)}, f32[128,128]{1,0:T(8,128)S(1)}) custom-call(f32[768,128]{1,0:T(8,128)} %bitcast.7, f32[24,128]{1,0:T(8,128)} %bitcast.8, f32[8,128]{1,0:T(8,128)} %depth_ref.1), custom_call_target="tpu_custom_call" | custom-call | tf_op jit(solution)/shard_map/pack/pallas_call | solution.py:323
  2.0 8.7 %collective-permute-start.1 = (f32[1088,128]{1,0:T(8,128)S(1)}, f32[1088,128]{1,0:T(8,128)S(1)}, u32[]{:S(2)}, u32[]{:S(2)}) collective-permute-start(f32[1088,128]{1,0:T(8,128)S(1)} %get-tuple-element.11.own_ref), channel_id=1, source_target_pairs={{32,0},{64,32},{96,64},{128,96},{160,128},{192,160},{224,192},{256... | collective-permute-start | bytes 1671176 | tf_op jit(solution)/shard_map/ppermute | solution.py:310
  10.7 1.9 %collective-permute-start = (f32[1088,128]{1,0:T(8,128)S(1)}, f32[1088,128]{1,0:T(8,128)S(1)}, u32[]{:S(2)}, u32[]{:S(2)}) collective-permute-start(f32[1088,128]{1,0:T(8,128)S(1)} %get-tuple-element.11.own_ref), channel_id=1, source_target_pairs={{0,32},{32,64},{64,96},{96,128},{128,160},{160,192},{192,224},{224... | collective-permute-start | bytes 1671176 | tf_op jit(solution)/shard_map/ppermute | solution.py:310
  12.6 1.9 %collective-permute-start.3 = (f32[128,128]{1,0:T(8,128)S(1)}, f32[128,128]{1,0:T(8,128)S(1)}, u32[]{:S(2)}, u32[]{:S(2)}) collective-permute-start(f32[128,128]{1,0:T(8,128)S(1)} %get-tuple-element.12), channel_id=1, source_target_pairs={{0,1},{1,2},{2,3},{3,4},{4,5},{5,6},{6,7},{7,8},{8,9},{9,10},{10,1... | collective-permute-start | bytes 196616 | tf_op jit(solution)/shard_map/ppermute | solution.py:310
  14.6 8.7 %collective-permute-start.2 = (f32[128,128]{1,0:T(8,128)S(1)}, f32[128,128]{1,0:T(8,128)S(1)}, u32[]{:S(2)}, u32[]{:S(2)}) collective-permute-start(f32[128,128]{1,0:T(8,128)S(1)} %get-tuple-element.12), channel_id=1, source_target_pairs={{0,31},{1,0},{2,1},{3,2},{4,3},{5,4},{6,5},{7,6},{8,7},{9,8},{10,9... | collective-permute-start | bytes 196616 | tf_op jit(solution)/shard_map/ppermute | solution.py:310
  23.3 0.0 collective-permute-done.3
  23.3 1.7 %collective-permute-done.2 = f32[128,128]{1,0:T(8,128)S(1)} collective-permute-done((f32[128,128]{1,0:T(8,128)S(1)}, f32[128,128]{1,0:T(8,128)S(1)}, u32[]{:S(2)}, u32[]{:S(2)}) %collective-permute-start.2) | collective-permute-done | bytes 65568 | tf_op jit(solution)/shard_map/ppermute | solution.py:310
  25.0 2.1 %collective-permute-start.5 = (f32[128,128]{1,0:T(8,128)S(1)}, f32[128,128]{1,0:T(8,128)S(1)}, u32[]{:S(2)}, u32[]{:S(2)}) collective-permute-start(f32[128,128]{1,0:T(8,128)S(1)} %broadcast_select_fusion.halo_ref), channel_id=1, source_target_pairs={{32,0},{64,32},{96,64},{128,96},{160,128},{192,160},{224,192},{256... | collective-permute-start | bytes 196616 | tf_op jit(solution)/shard_map/ppermute | solution.py:310
  27.1 3.5 %collective-permute-start.4 = (f32[128,128]{1,0:T(8,128)S(1)}, f32[128,128]{1,0:T(8,128)S(1)}, u32[]{:S(2)}, u32[]{:S(2)}) collective-permute-start(f32[128,128]{1,0:T(8,128)S(1)} %broadcast_select_fusion.halo_ref), channel_id=1, source_target_pairs={{0,32},{32,64},{64,96},{96,128},{128,160},{160,192},{192,224},{224... | collective-permute-start | bytes 196616 | tf_op jit(solution)/shard_map/ppermute | solution.py:310
  31.2 0.0 collective-permute-done.1.south_ref
  31.2 0.0 collective-permute-done.north_ref
  31.2 2.3 %inner.1 = (f32[768,128]{1,0:T(8,128)S(1)}, f32[16,128]{1,0:T(8,128)S(1)}) custom-call(s32[1]{0:T(128)S(6)} %copy.9.count_ref, f32[1088,128]{1,0:T(8,128)S(1)} %get-tuple-element.11.own_ref, f32[1088,128]{1,0:T(8,128)S(1)} %collective-permute-done.north_ref, f32[1088,128]{1,0:T(8,128)S(1)} %collective-permute-done.1.south_ref, s32[1,256]{1,0:T(1,128)} %bitcast.9, ...), custom_call_target="tpu_custom_call" | custom-call | tf_op jit(solution)/shard_map/inner/pallas_call | solution.py:340
  33.5 0.0 collective-permute-done.5.south_halo_ref
  33.5 0.0 collective-permute-done.4.north_halo_ref
  33.5 1.4 %side.1 = (bf16[96,3072]{1,0:T(8,128)(2,1)S(1)}, f32[24,128]{1,0:T(8,128)S(1)}, f32[8,128]{1,0:T(8,128)S(1)}) custom-call(f32[1088,128]{1,0:T(8,128)S(1)} %get-tuple-element.11.own_ref, f32[1088,128]{1,0:T(8,128)S(1)} %collective-permute-done.north_ref, f32[1088,128]{1,0:T(8,128)S(1)} %collective-permute-done.1.south_ref, ...), custom_call_target="tpu_custom_call" | custom-call | tf_op jit(solution)/shard_map/side/pallas_call | solution.py:354
  34.9 16.2 %all_to_all.10 = f32[16,8,128]{2,1,0:T(8,128)S(1)} all-to-all(f32[16,8,128]{2,1,0:T(8,128)S(1)} %broadcast_in_dim.4), channel_id=1, replica_groups=mesh['lat'=16,'lon'=32] {'lat'}, dimensions={0} | all-to-all | bytes 131072 | tf_op jit(solution)/shard_map/all_to_all | solution.py:316
  51.2 15.7 %all_to_all.11.parts_ref = f32[32,8,128]{2,1,0:T(8,128)S(1)} all-to-all(f32[32,8,128]{2,1,0:T(8,128)S(1)} %broadcast_in_dim.5), channel_id=1, replica_groups=mesh['lat'=16,'lon'=32] {'lon'}, dimensions={0} | all-to-all | bytes 262144 | tf_op jit(solution)/shard_map/all_to_all | solution.py:316
  66.9 2.4 %analysis.1 = (f32[24,128]{1,0:T(8,128)}, f32[768,128]{1,0:T(8,128)}) custom-call(f32[32,8,128]{2,1,0:T(8,128)S(1)} %all_to_all.11.parts_ref, bf16[96,3072]{1,0:T(8,128)(2,1)S(1)} %get-tuple-element.16.split_ref, f32[24,128]{1,0:T(8,128)S(1)} %get-tuple-element.17.mean_ref), custom_call_target="tpu_custom_call" | custom-call | tf_op jit(solution)/shard_map/analysis/pallas_call | solution.py:373
  (5 shorter events, 0.1 us)
Async XLA Ops:
  2.0 29.3 %collective-permute-start.1 = (f32[1088,128]{1,0:T(8,128)S(1)}, f32[1088,128]{1,0:T(8,128)S(1)}, u32[]{:S(2)}, u32[]{:S(2)}) collective-permute-start(f32[1088,128]{1,0:T(8,128)S(1)} %get-tuple-element.11.own_ref), channel_id=1, source_target_pairs={{32,0},{64,32},{96,64},{128,96},{160,128},{192,160},{224,192},{256... | collective-permute-start | bytes 1671176 | tf_op jit(solution)/shard_map/ppermute | solution.py:310
  10.7 20.5 %collective-permute-start = (f32[1088,128]{1,0:T(8,128)S(1)}, f32[1088,128]{1,0:T(8,128)S(1)}, u32[]{:S(2)}, u32[]{:S(2)}) collective-permute-start(f32[1088,128]{1,0:T(8,128)S(1)} %get-tuple-element.11.own_ref), channel_id=1, source_target_pairs={{0,32},{32,64},{64,96},{96,128},{128,160},{160,192},{192,224},{224... | collective-permute-start | bytes 1671176 | tf_op jit(solution)/shard_map/ppermute | solution.py:310
  12.6 10.7 %collective-permute-start.3 = (f32[128,128]{1,0:T(8,128)S(1)}, f32[128,128]{1,0:T(8,128)S(1)}, u32[]{:S(2)}, u32[]{:S(2)}) collective-permute-start(f32[128,128]{1,0:T(8,128)S(1)} %get-tuple-element.12), channel_id=1, source_target_pairs={{0,1},{1,2},{2,3},{3,4},{4,5},{5,6},{6,7},{7,8},{8,9},{9,10},{10,1... | collective-permute-start | bytes 196616 | tf_op jit(solution)/shard_map/ppermute | solution.py:310
  14.6 10.4 %collective-permute-start.2 = (f32[128,128]{1,0:T(8,128)S(1)}, f32[128,128]{1,0:T(8,128)S(1)}, u32[]{:S(2)}, u32[]{:S(2)}) collective-permute-start(f32[128,128]{1,0:T(8,128)S(1)} %get-tuple-element.12), channel_id=1, source_target_pairs={{0,31},{1,0},{2,1},{3,2},{4,3},{5,4},{6,5},{7,6},{8,7},{9,8},{10,9... | collective-permute-start | bytes 196616 | tf_op jit(solution)/shard_map/ppermute | solution.py:310
  25.0 8.5 %collective-permute-start.5 = (f32[128,128]{1,0:T(8,128)S(1)}, f32[128,128]{1,0:T(8,128)S(1)}, u32[]{:S(2)}, u32[]{:S(2)}) collective-permute-start(f32[128,128]{1,0:T(8,128)S(1)} %broadcast_select_fusion.halo_ref), channel_id=1, source_target_pairs={{32,0},{64,32},{96,64},{128,96},{160,128},{192,160},{224,192},{256... | collective-permute-start | bytes 196616 | tf_op jit(solution)/shard_map/ppermute | solution.py:310
  27.1 6.4 %collective-permute-start.4 = (f32[128,128]{1,0:T(8,128)S(1)}, f32[128,128]{1,0:T(8,128)S(1)}, u32[]{:S(2)}, u32[]{:S(2)}) collective-permute-start(f32[128,128]{1,0:T(8,128)S(1)} %broadcast_select_fusion.halo_ref), channel_id=1, source_target_pairs={{0,32},{32,64},{64,96},{96,128},{128,160},{160,192},{192,224},{224... | collective-permute-start | bytes 196616 | tf_op jit(solution)/shard_map/ppermute | solution.py:310

commit v4 on v3

--- a/solution.py
+++ b/solution.py
@@ -1,11 +1,10 @@
-import functools
-
 import jax
 import jax.numpy as jnp
 from jax import lax
 from jax.experimental import pallas as pl
 from jax.experimental.pallas import tpu as pltpu
 from jax.sharding import PartitionSpec as P
+
 
 STEPS = 4
 TIME_STEP = 0.9
@@ -79,6 +78,11 @@
     return north, south
 
 
+def by_side(near, far):
+    odd = lax.rem(lax.axis_index("lat"), 2) == 1
+    return jnp.where(odd, near, far), jnp.where(odd, far, near)
+
+
 def lon_difference(value):
     return pltpu.roll(value, LANES - 1, 1) - pltpu.roll(value, 1, 1)
 
@@ -120,25 +124,26 @@
 
 
 def inner_kernel(
-    count_ref, own_ref, north_ref, south_ref, cells_ref, values_ref, error_ref, out_ref, weight_ref, state, depth
+    count_ref, own_ref, near_ref, far_ref, cells_ref, values_ref, error_ref, out_ref, weight_ref, state, depth
 ):
-    blocks = (north_ref, own_ref, south_ref)
-    for block, ref in enumerate(blocks):
-        for row in range(ROWS):
-            depth[ROWS * block + row] = PULL * jnp.broadcast_to(
-                ref[pl.ds((row * PER_ROW + SMALL) * 8 + 3, 1), :], (8, LANES)
-            )
+    def around(at):
+        north, south = by_side(near_ref[at, :], far_ref[at, :])
+        return enumerate((north, own_ref[at, :], south))
+
+    for row in range(ROWS):
+        for block, value in around(pl.ds((row * PER_ROW + SMALL) * 8 + 3, 1)):
+            depth[ROWS * block + row] = PULL * jnp.broadcast_to(value, (8, LANES))
     weight_ref[...] = observed(count_ref, cells_ref, values_ref, error_ref)
     row_pulls = pulls()
 
     def pair(which, carry):
         for half in range(2):
             tile = 2 * which + half
-            for block, ref in enumerate(blocks):
-                for field in range(3):
-                    for row in range(ROWS):
-                        at = pl.multiple_of((row * PER_ROW + MAIN + TILES * field + tile) * 8, 8)
-                        state[half, field, ROWS * block + row] = ref[pl.ds(at, 8), :]
+            for field in range(3):
+                for row in range(ROWS):
+                    at = pl.multiple_of((row * PER_ROW + MAIN + TILES * field + tile) * 8, 8)
+                    for block, value in around(pl.ds(at, 8)):
+                        state[half, field, ROWS * block + row] = value
         advance([(state.at[half], depth) for half in range(2)], row_pulls)
         for half in range(2):
             tile = 2 * which + half
@@ -152,19 +157,24 @@
 
 
 def side_kernel(
-    own_ref, north_ref, south_ref, halo_ref, north_halo_ref, south_halo_ref, inner_ref, weight_ref,
+    own_ref, near_ref, far_ref, halo_ref, near_halo_ref, far_halo_ref, inner_ref, weight_ref,
     split_ref, mean_out_ref, gram_ref, state, depth, heights, scaled,
 ):
     lane = lane_iota()
     low_lanes = (lane & 16) == 0
     sub = lax.broadcasted_iota(jnp.int32, (8, LANES), 0)
-    blocks = ((north_ref, north_halo_ref), (own_ref, halo_ref), (south_ref, south_halo_ref))
-    for block, (ref, halos) in enumerate(blocks):
-        for row in range(ROWS):
-            at = ROWS * block + row
-            for which in range(4):
-                side = ref[block_at(row, SIDE + which), :]
-                halo = halos[pl.ds(((row // 2) * 4 + which) * 8, 8), :]
+
+    def around(own, near, far, at):
+        north, south = by_side(near[at, :], far[at, :])
+        return north, own[at, :], south
+
+    for row in range(ROWS):
+        smalls = around(own_ref, near_ref, far_ref, block_at(row, SMALL))
+        for which in range(4):
+            sides = around(own_ref, near_ref, far_ref, block_at(row, SIDE + which))
+            halos = around(halo_ref, near_halo_ref, far_halo_ref, pl.ds(((row // 2) * 4 + which) * 8, 8))
+            for block, (small, side, halo) in enumerate(zip(smalls, sides, halos)):
+                at = ROWS * block + row
                 if row % 2:
                     halo = pltpu.roll(halo, LANES - 16, 1)
                 right = jnp.where(low_lanes, side, halo)
@@ -172,22 +182,23 @@
                 if which < 3:
                     state[0, which, at] = right
                     state[1, which, at] = left
-                else:
-                    small = ref[block_at(row, SMALL), :]
-                    for field in range(3):
-                        state[2, field, at] = jnp.where(
-                            sub == 0,
-                            jnp.broadcast_to(small[field : field + 1, :], (8, LANES)),
-                            jnp.where(
-                                sub == 1,
-                                jnp.broadcast_to(right[field : field + 1, :], (8, LANES)),
-                                jnp.broadcast_to(left[field : field + 1, :], (8, LANES)),
-                            ),
-                        )
-                    depth[0, at] = PULL * jnp.broadcast_to(right[3:4, :], (8, LANES))
-                    depth[1, at] = PULL * jnp.broadcast_to(left[3:4, :], (8, LANES))
-                    whole = PULL * jnp.broadcast_to(small[3:4, :], (8, LANES))
-                    depth[2, at] = jnp.where(sub == 0, whole, jnp.where(sub == 1, depth[0, at], depth[1, at]))
+                    continue
+                for field in range(3):
+                    state[2, field, at] = jnp.where(
+                        sub == 0,
+                        jnp.broadcast_to(small[field : field + 1, :], (8, LANES)),
+                        jnp.where(
+                            sub == 1,
+                            jnp.broadcast_to(right[field : field + 1, :], (8, LANES)),
+                            jnp.broadcast_to(left[field : field + 1, :], (8, LANES)),
+                        ),
+                    )
+                of_right = PULL * jnp.broadcast_to(right[3:4, :], (8, LANES))
+                of_left = PULL * jnp.broadcast_to(left[3:4, :], (8, LANES))
+                whole = PULL * jnp.broadcast_to(small[3:4, :], (8, LANES))
+                depth[0, at] = of_right
+                depth[1, at] = of_left
+                depth[2, at] = jnp.where(sub == 0, whole, jnp.where(sub == 1, of_right, of_left))
     advance([(state.at[which], depth.at[which]) for which in range(3)], pulls())
 
     from_right = (lane & 16) == 0
@@ -304,10 +315,12 @@
     return pltpu.with_memory_space_constraint(value, pltpu.VMEM)
 
 
-def shift_by(value, axis, step, periodic):
+def swapped(value, axis, offset, periodic):
     count = lax.axis_size(axis)
-    pairs = [(i, (i + step) % count) for i in range(count) if periodic or 0 <= i + step < count]
-    return lax.ppermute(value, axis, pairs)
+    pairs = [(i, i + 1) for i in range(offset, count - 1, 2)]
+    if offset and periodic:
+        pairs.append((count - 1, 0))
+    return lax.ppermute(value, axis, pairs + [(j, i) for i, j in pairs])
 
 
 def sum_over(value, axis):
@@ -328,14 +341,15 @@
         name="pack",
     )(factor.reshape(RANK * PLANES, LANES), background_expectation.reshape(PLANES, LANES), average_thickness)
     block = on_chip(block)
-    from_west = shift_by(edges, "lon", 1, True)
-    from_east = shift_by(edges, "lon", -1, True)
-    north = on_chip(shift_by(block, "lat", 1, False))
-    south = on_chip(shift_by(block, "lat", -1, False))
-    east_lane = (lax.broadcasted_iota(jnp.int32, (ROWS * 16, LANES), 1) & 8) == 0
-    halo = jnp.where(east_lane, from_east, from_west)
-    north_halo = on_chip(shift_by(halo, "lat", 1, False))
-    south_halo = on_chip(shift_by(halo, "lat", -1, False))
+    even_edges = swapped(edges, "lon", 0, True)
+    odd_edges = swapped(edges, "lon", 1, True)
+    far = on_chip(swapped(block, "lat", 1, False))
+    near = on_chip(swapped(block, "lat", 0, False))
+    eastern = (lax.broadcasted_iota(jnp.int32, (ROWS * 16, LANES), 1) & 8) // 8 != 1
+    from_even = eastern == (lax.rem(lax.axis_index("lon"), 2) == 0)
+    halo = jnp.where(from_even, even_edges, odd_edges)
+    far_halo = on_chip(swapped(halo, "lat", 1, False))
+    near_halo = on_chip(swapped(halo, "lat", 0, False))
     slots = obs_cells.shape[0]
     inner, weights = pl.pallas_call(
         inner_kernel,
@@ -348,7 +362,7 @@
         ],
         name="inner",
     )(
-        obs_count, block, north, south,
+        obs_count, block, near, far,
         obs_cells.reshape(1, slots), obs_values.reshape(1, slots), obs_error.reshape(1, slots),
     )
     split, mean, gram = pl.pallas_call(
@@ -367,7 +381,7 @@
             pltpu.VMEM((RANK + 8, ROWS * LANES), jnp.float32),
         ],
         name="side",
-    )(block, north, south, on_chip(halo), north_halo, south_halo, on_chip(inner), on_chip(weights))
+    )(block, near, far, on_chip(halo), near_halo, far_halo, on_chip(inner), on_chip(weights))
     gram = jnp.sum(sum_over(gram, "lat"), 0)
     parts = sum_over(gram, "lon")
     update, analysis = pl.pallas_call(

time: 69.7 us -> 66.1 us (0.948)
  blocking collectives: 31.9 us -> 25.6 us
  starting transfers between devices: 26.8 us -> 28.2 us
  waiting for transfers between devices: 1.69 us -> 3.06 us
    all_to_all x2, blocking collectives: 31.9 us -> 25.6 us  [sum_over(): return lax.all_to_all(sent, axis, 0, 0)]
    ppermute x6, starting transfers between devices: 26.8 us -> 28.2 us  [swapped(): return lax.ppermute(value, axis, pairs + [(j, i) for i, j in pairs])]
    ppermute x6, waiting for transfers between devices: 1.69 us -> 3.06 us  [swapped(): return lax.ppermute(value, axis, pairs + [(j, i) for i, j in pairs])]
where the time goes in v4:
time: 66.1 us; the launch traced here: 65.7 us
  starting transfers between devices  28.2 us (43%)
  blocking collectives  25.6 us (39%)
  Pallas kernels  7.45 us (11%)
  waiting for transfers between devices  3.06 us (5%)
  between operations  1.4 us (2%)
    ppermute x6, starting transfers between devices, swapped(): return lax.ppermute(value, axis, pairs + [(j, i) for i, j in pairs])  28.2 us
    all_to_all x2, blocking collectives, sum_over(): return lax.all_to_all(sent, axis, 0, 0)  25.6 us
    ppermute x6, waiting for transfers between devices, swapped(): return lax.ppermute(value, axis, pairs + [(j, i) for i, j in pairs])  3.06 us
    pallas_call x1, Pallas kernels, per_device(): pl.pallas_call(analysis_kernel, out_shape=(f32(PLANES, LANES), f32(RANK *...  2.41 us
    pallas_call x1, Pallas kernels, per_device(): pl.pallas_call(inner_kernel, out_shape=(chip(RANK * PLANES, LANES), chip(...  2.29 us
    pallas_call x1, Pallas kernels, per_device(): pl.pallas_call(side_kernel, out_shape=(pltpu.VMEM((3 * RANK, PLANES * LAN...  1.43 us
    pallas_call x1, Pallas kernels, per_device(): pl.pallas_call(pack_kernel, out_shape=(chip(ROWS * PER_ROW * 8, LANES), c...  1.32 us
  transfers between devices with their start and end apart: 6, of which 1 were waited for; matrix products, arithmetic and copies ran while one was open for 0% of the time, Pallas kernels for 3%

profile of v4, /device:TPU:1, one launch (start us, length us, event | category | flops | bytes accessed | tf_op | source)
XLA Modules:
  0.0 65.7 jit_solution(2185067868789036245)
XLA Ops:
  0.6 1.3 %pack.1 = (f32[1088,128]{1,0:T(8,128)S(1)}, f32[128,128]{1,0:T(8,128)S(1)}) custom-call(f32[768,128]{1,0:T(8,128)} %bitcast.7, f32[24,128]{1,0:T(8,128)} %bitcast.8, f32[8,128]{1,0:T(8,128)} %depth_ref.1), custom_call_target="tpu_custom_call" | custom-call | tf_op jit(solution)/shard_map/pack/pallas_call | solution.py:336
  2.0 4.6 %collective-permute-start.1 = (f32[1088,128]{1,0:T(8,128)S(1)}, f32[1088,128]{1,0:T(8,128)S(1)}, u32[]{:S(2)}, u32[]{:S(2)}) collective-permute-start(f32[1088,128]{1,0:T(8,128)S(1)} %get-tuple-element.11.own_ref), channel_id=1, source_target_pairs={{32,64},{96,128},{160,192},{224,256},{288,320},{352,384},{416,448}... | collective-permute-start | bytes 1671176 | tf_op jit(solution)/shard_map/ppermute | solution.py:323
  6.5 4.9 %collective-permute-start = (f32[1088,128]{1,0:T(8,128)S(1)}, f32[1088,128]{1,0:T(8,128)S(1)}, u32[]{:S(2)}, u32[]{:S(2)}) collective-permute-start(f32[1088,128]{1,0:T(8,128)S(1)} %get-tuple-element.11.own_ref), channel_id=1, source_target_pairs={{0,32},{64,96},{128,160},{192,224},{256,288},{320,352},{384,416},{... | collective-permute-start | bytes 1671176 | tf_op jit(solution)/shard_map/ppermute | solution.py:323
  11.4 9.9 %collective-permute-start.3 = (f32[128,128]{1,0:T(8,128)S(1)}, f32[128,128]{1,0:T(8,128)S(1)}, u32[]{:S(2)}, u32[]{:S(2)}) collective-permute-start(f32[128,128]{1,0:T(8,128)S(1)} %get-tuple-element.12), channel_id=1, source_target_pairs={{1,2},{3,4},{5,6},{7,8},{9,10},{11,12},{13,14},{15,16},{17,18},{19... | collective-permute-start | bytes 196616 | tf_op jit(solution)/shard_map/ppermute | solution.py:323
  21.3 1.9 %collective-permute-start.2 = (f32[128,128]{1,0:T(8,128)S(1)}, f32[128,128]{1,0:T(8,128)S(1)}, u32[]{:S(2)}, u32[]{:S(2)}) collective-permute-start(f32[128,128]{1,0:T(8,128)S(1)} %get-tuple-element.12), channel_id=1, source_target_pairs={{0,1},{2,3},{4,5},{6,7},{8,9},{10,11},{12,13},{14,15},{16,17},{18,... | collective-permute-start | bytes 196616 | tf_op jit(solution)/shard_map/ppermute | solution.py:323
  23.3 0.0 collective-permute-done.3
  23.3 3.0 %collective-permute-done.2 = f32[128,128]{1,0:T(8,128)S(1)} collective-permute-done((f32[128,128]{1,0:T(8,128)S(1)}, f32[128,128]{1,0:T(8,128)S(1)}, u32[]{:S(2)}, u32[]{:S(2)}) %collective-permute-start.2) | collective-permute-done | bytes 65568 | tf_op jit(solution)/shard_map/ppermute | solution.py:323
  26.4 5.0 %collective-permute-start.5 = (f32[128,128]{1,0:T(8,128)S(1)}, f32[128,128]{1,0:T(8,128)S(1)}, u32[]{:S(2)}, u32[]{:S(2)}) collective-permute-start(f32[128,128]{1,0:T(8,128)S(1)} %fusion.1.halo_ref), channel_id=1, source_target_pairs={{32,64},{96,128},{160,192},{224,256},{288,320},{352,384},{416,448}... | collective-permute-start | bytes 196616 | tf_op jit(solution)/shard_map/ppermute | solution.py:323
  31.4 1.9 %collective-permute-start.4 = (f32[128,128]{1,0:T(8,128)S(1)}, f32[128,128]{1,0:T(8,128)S(1)}, u32[]{:S(2)}, u32[]{:S(2)}) collective-permute-start(f32[128,128]{1,0:T(8,128)S(1)} %fusion.1.halo_ref), channel_id=1, source_target_pairs={{0,32},{64,96},{128,160},{192,224},{256,288},{320,352},{384,416},{... | collective-permute-start | bytes 196616 | tf_op jit(solution)/shard_map/ppermute | solution.py:323
  34.0 0.0 collective-permute-done.1.far_ref
  34.0 0.0 collective-permute-done.near_ref
  34.0 2.3 %inner.1 = (f32[768,128]{1,0:T(8,128)S(1)}, f32[16,128]{1,0:T(8,128)S(1)}) custom-call(s32[1]{0:T(128)S(6)} %copy.9.count_ref, f32[1088,128]{1,0:T(8,128)S(1)} %get-tuple-element.11.own_ref, f32[1088,128]{1,0:T(8,128)S(1)} %collective-permute-done.near_ref, f32[1088,128]{1,0:T(8,128)S(1)} %collective-permute-done.1.far_ref, s32[1,256]{1,0:T(1,128)} %bitcast.9, ...), custom_call_target="tpu_custom_call" | custom-call | tf_op jit(solution)/shard_map/inner/pallas_call | solution.py:354
  36.3 0.0 collective-permute-done.5.far_halo_ref
  36.3 0.0 collective-permute-done.4.near_halo_ref
  36.3 1.4 %side.1 = (bf16[96,3072]{1,0:T(8,128)(2,1)S(1)}, f32[24,128]{1,0:T(8,128)S(1)}, f32[8,128]{1,0:T(8,128)S(1)}) custom-call(f32[1088,128]{1,0:T(8,128)S(1)} %get-tuple-element.11.own_ref, f32[1088,128]{1,0:T(8,128)S(1)} %collective-permute-done.near_ref, f32[1088,128]{1,0:T(8,128)S(1)} %collective-permute-done.1.far_ref, f32[128,128]{1,0:T(8,128)S(1)} %fusion.1.halo_ref, ...), custom_call_target="tpu_custom_call" | custom-call | tf_op jit(solution)/shard_map/side/pallas_call | solution.py:368
  37.7 13.4 %all_to_all.10 = f32[16,8,128]{2,1,0:T(8,128)S(1)} all-to-all(f32[16,8,128]{2,1,0:T(8,128)S(1)} %broadcast_in_dim.4), channel_id=1, replica_groups=mesh['lat'=16,'lon'=32] {'lat'}, dimensions={0} | all-to-all | bytes 131072 | tf_op jit(solution)/shard_map/all_to_all | solution.py:329
  51.2 12.1 %all_to_all.11.parts_ref = f32[32,8,128]{2,1,0:T(8,128)S(1)} all-to-all(f32[32,8,128]{2,1,0:T(8,128)S(1)} %broadcast_in_dim.5), channel_id=1, replica_groups=mesh['lat'=16,'lon'=32] {'lon'}, dimensions={0} | all-to-all | bytes 262144 | tf_op jit(solution)/shard_map/all_to_all | solution.py:329
  63.3 2.4 %analysis.1 = (f32[24,128]{1,0:T(8,128)}, f32[768,128]{1,0:T(8,128)}) custom-call(f32[32,8,128]{2,1,0:T(8,128)S(1)} %all_to_all.11.parts_ref, bf16[96,3072]{1,0:T(8,128)(2,1)S(1)} %get-tuple-element.16.split_ref, f32[24,128]{1,0:T(8,128)S(1)} %get-tuple-element.17.mean_ref), custom_call_target="tpu_custom_call" | custom-call | tf_op jit(solution)/shard_map/analysis/pallas_call | solution.py:387
  (6 shorter events, 0.1 us)
Async XLA Ops:
  2.0 32.0 %collective-permute-start.1 = (f32[1088,128]{1,0:T(8,128)S(1)}, f32[1088,128]{1,0:T(8,128)S(1)}, u32[]{:S(2)}, u32[]{:S(2)}) collective-permute-start(f32[1088,128]{1,0:T(8,128)S(1)} %get-tuple-element.11.own_ref), channel_id=1, source_target_pairs={{32,64},{96,128},{160,192},{224,256},{288,320},{352,384},{416,448}... | collective-permute-start | bytes 1671176 | tf_op jit(solution)/shard_map/ppermute | solution.py:323
  6.5 27.4 %collective-permute-start = (f32[1088,128]{1,0:T(8,128)S(1)}, f32[1088,128]{1,0:T(8,128)S(1)}, u32[]{:S(2)}, u32[]{:S(2)}) collective-permute-start(f32[1088,128]{1,0:T(8,128)S(1)} %get-tuple-element.11.own_ref), channel_id=1, source_target_pairs={{0,32},{64,96},{128,160},{192,224},{256,288},{320,352},{384,416},{... | collective-permute-start | bytes 1671176 | tf_op jit(solution)/shard_map/ppermute | solution.py:323
  11.4 11.9 %collective-permute-start.3 = (f32[128,128]{1,0:T(8,128)S(1)}, f32[128,128]{1,0:T(8,128)S(1)}, u32[]{:S(2)}, u32[]{:S(2)}) collective-permute-start(f32[128,128]{1,0:T(8,128)S(1)} %get-tuple-element.12), channel_id=1, source_target_pairs={{1,2},{3,4},{5,6},{7,8},{9,10},{11,12},{13,14},{15,16},{17,18},{19... | collective-permute-start | bytes 196616 | tf_op jit(solution)/shard_map/ppermute | solution.py:323
  21.3 5.0 %collective-permute-start.2 = (f32[128,128]{1,0:T(8,128)S(1)}, f32[128,128]{1,0:T(8,128)S(1)}, u32[]{:S(2)}, u32[]{:S(2)}) collective-permute-start(f32[128,128]{1,0:T(8,128)S(1)} %get-tuple-element.12), channel_id=1, source_target_pairs={{0,1},{2,3},{4,5},{6,7},{8,9},{10,11},{12,13},{14,15},{16,17},{18,... | collective-permute-start | bytes 196616 | tf_op jit(solution)/shard_map/ppermute | solution.py:323
  26.4 9.9 %collective-permute-start.5 = (f32[128,128]{1,0:T(8,128)S(1)}, f32[128,128]{1,0:T(8,128)S(1)}, u32[]{:S(2)}, u32[]{:S(2)}) collective-permute-start(f32[128,128]{1,0:T(8,128)S(1)} %fusion.1.halo_ref), channel_id=1, source_target_pairs={{32,64},{96,128},{160,192},{224,256},{288,320},{352,384},{416,448}... | collective-permute-start | bytes 196616 | tf_op jit(solution)/shard_map/ppermute | solution.py:323
  31.4 4.9 %collective-permute-start.4 = (f32[128,128]{1,0:T(8,128)S(1)}, f32[128,128]{1,0:T(8,128)S(1)}, u32[]{:S(2)}, u32[]{:S(2)}) collective-permute-start(f32[128,128]{1,0:T(8,128)S(1)} %fusion.1.halo_ref), channel_id=1, source_target_pairs={{0,32},{64,96},{128,160},{192,224},{256,288},{320,352},{384,416},{... | collective-permute-start | bytes 196616 | tf_op jit(solution)/shard_map/ppermute | solution.py:323

commit v5 on v4

--- a/solution.py
+++ b/solution.py
@@ -19,8 +19,9 @@
 GROUP = LANES // TILES
 MAIN, SMALL, SIDE = 0, 12, 13
 PER_ROW = 17
+MOVES = (0, 16, 8, 24)
 PULL = 0.5 * TIME_STEP
-WIDTH = 4
+WIDTH = 8
 HIGHEST = lax.Precision.HIGHEST
 NT = (((1,), (1,)), ((), ()))
 
@@ -37,11 +38,12 @@
     return pl.ds((row * PER_ROW + tile) * 8, 8)
 
 
-def pack_kernel(factor_ref, mean_ref, depth_ref, block_ref, edge_ref):
+def pack_kernel(factor_ref, mean_ref, depth_ref, block_ref, even_edge_ref, odd_edge_ref):
     lane = lane_iota()
     part = lane // GROUP
-    even = ((lane - 8) & 16) == 0
-    kept = {}
+    octet = (lane // 8) & 3
+    even = lax.rem(lax.axis_index("lon"), 2) == 0
+    eastward, westward = {}, {}
     for row in range(ROWS):
         small = jnp.concatenate(
             [mean_ref[f * ROWS + row : f * ROWS + row + 1, :] for f in range(3)]
@@ -63,11 +65,17 @@
         sides.append(jnp.where(part < 2, side, pltpu.roll(side, 2 * GROUP, 1)))
         for which, side in enumerate(sides):
             block_ref[block_at(row, SIDE + which), :] = side
-            if row % 2 == 0:
-                kept[which] = side
-            else:
-                at = pl.ds(((row // 2) * 4 + which) * 8, 8)
-                edge_ref[at, :] = jnp.where(even, kept[which], pltpu.roll(side, 16, 1))
+            move = MOVES[row % 4]
+            moved = pltpu.roll(side, move, 1) if move else side
+            if row % 4 == 0:
+                eastward[which] = westward[which] = moved
+                continue
+            eastward[which] = jnp.where(octet == (1 + move // 8) % 4, moved, eastward[which])
+            westward[which] = jnp.where(octet == (2 + move // 8) % 4, moved, westward[which])
+            if row % 4 == 3:
+                at = pl.ds(((row // 4) * 4 + which) * 8, 8)
+                even_edge_ref[at, :] = jnp.where(even, eastward[which], westward[which])
+                odd_edge_ref[at, :] = jnp.where(even, westward[which], eastward[which])
 
 
 def pulls():
@@ -105,9 +113,9 @@
                 n[row] = north - row_pull * (h[row + 1] - h[row - 1]) - ROTATION * east
 
 
-def observed(count_ref, cells_ref, values_ref, error_ref):
+def weight_kernel(count_ref, cells_ref, values_ref, error_ref, out_ref):
     slots = cells_ref.shape[1]
-    live = lax.broadcasted_iota(jnp.int32, (1, slots), 1) < count_ref[0]
+    live = lax.broadcasted_iota(jnp.int32, (1, slots), 1) < count_ref[...]
     weight = jnp.where(live, 1.0, 0.0) / error_ref[...]
     square = weight * weight
     cells = cells_ref[...]
@@ -118,14 +126,12 @@
         [jnp.where(in_row, square, 0.0), jnp.where(in_row, square * values_ref[...], 0.0)], 0
     )
     in_lane = lax.broadcasted_iota(jnp.int32, (LANES, slots), 0) == lane_of
-    return lax.dot_general(
+    out_ref[...] = lax.dot_general(
         spread, jnp.where(in_lane, 1.0, 0.0), NT, precision=HIGHEST, preferred_element_type=jnp.float32
     )
 
 
-def inner_kernel(
-    count_ref, own_ref, near_ref, far_ref, cells_ref, values_ref, error_ref, out_ref, weight_ref, state, depth
-):
+def inner_kernel(own_ref, near_ref, far_ref, out_ref, state, depth):
     def around(at):
         north, south = by_side(near_ref[at, :], far_ref[at, :])
         return enumerate((north, own_ref[at, :], south))
@@ -133,7 +139,6 @@
     for row in range(ROWS):
         for block, value in around(pl.ds((row * PER_ROW + SMALL) * 8 + 3, 1)):
             depth[ROWS * block + row] = PULL * jnp.broadcast_to(value, (8, LANES))
-    weight_ref[...] = observed(count_ref, cells_ref, values_ref, error_ref)
     row_pulls = pulls()
 
     def pair(which, carry):
@@ -175,8 +180,8 @@
             halos = around(halo_ref, near_halo_ref, far_halo_ref, pl.ds(((row // 2) * 4 + which) * 8, 8))
             for block, (small, side, halo) in enumerate(zip(smalls, sides, halos)):
                 at = ROWS * block + row
-                if row % 2:
-                    halo = pltpu.roll(halo, LANES - 16, 1)
+                if MOVES[row % 4]:
+                    halo = pltpu.roll(halo, LANES - MOVES[row % 4], 1)
                 right = jnp.where(low_lanes, side, halo)
                 left = jnp.where(low_lanes, halo, side)
                 if which < 3:
@@ -300,7 +305,7 @@
 
 
 VMEM = pl.BlockSpec(memory_space=pltpu.VMEM)
-SMEM = pl.BlockSpec(memory_space=pltpu.SMEM)
+SMALL_VMEM = pltpu.CompilerParams(vmem_limit_bytes=8 << 20)
 
 
 def f32(*shape):
@@ -333,38 +338,45 @@
     background_expectation, factor, average_thickness, obs_cells, obs_count, obs_values, obs_error
 ):
     assert factor.shape == (RANK, 3, ROWS, LANES)
-    block, edges = pl.pallas_call(
+    block, even_edges, odd_edges = pl.pallas_call(
         pack_kernel,
-        out_shape=(chip(ROWS * PER_ROW * 8, LANES), chip(ROWS * 16, LANES)),
+        out_shape=(chip(ROWS * PER_ROW * 8, LANES),) + (chip(ROWS * 8, LANES),) * 2,
         in_specs=[VMEM] * 3,
-        out_specs=(VMEM, VMEM),
-        name="pack",
+        out_specs=(VMEM,) * 3,
+        name="pack", compiler_params=SMALL_VMEM,
     )(factor.reshape(RANK * PLANES, LANES), background_expectation.reshape(PLANES, LANES), average_thickness)
     block = on_chip(block)
-    even_edges = swapped(edges, "lon", 0, True)
-    odd_edges = swapped(edges, "lon", 1, True)
+    even_edges = swapped(even_edges, "lon", 0, True)
+    odd_edges = swapped(odd_edges, "lon", 1, True)
     far = on_chip(swapped(block, "lat", 1, False))
     near = on_chip(swapped(block, "lat", 0, False))
-    eastern = (lax.broadcasted_iota(jnp.int32, (ROWS * 16, LANES), 1) & 8) // 8 != 1
+    slots = obs_cells.shape[0]
+    weights = pl.pallas_call(
+        weight_kernel, out_shape=chip(2 * ROWS, LANES), in_specs=[VMEM] * 4, out_specs=VMEM, name="weigh", compiler_params=SMALL_VMEM
+    )(
+        obs_count.reshape(1, 1), obs_cells.reshape(1, slots),
+        obs_values.reshape(1, slots), obs_error.reshape(1, slots),
+    )
+    shape = (ROWS // 4, 4 * 8, LANES)
+    eastern = (lax.broadcasted_iota(jnp.int32, shape, 2) & 8) // 8 != 1
     from_even = eastern == (lax.rem(lax.axis_index("lon"), 2) == 0)
-    halo = jnp.where(from_even, even_edges, odd_edges)
+    even_edges, odd_edges = even_edges.reshape(shape), odd_edges.reshape(shape)
+    halo = jnp.stack(
+        [jnp.where(from_even, even_edges, odd_edges), jnp.where(from_even, odd_edges, even_edges)], 1
+    ).reshape(ROWS * 16, LANES)
     far_halo = on_chip(swapped(halo, "lat", 1, False))
     near_halo = on_chip(swapped(halo, "lat", 0, False))
-    slots = obs_cells.shape[0]
-    inner, weights = pl.pallas_call(
+    inner = pl.pallas_call(
         inner_kernel,
-        out_shape=(chip(RANK * PLANES, LANES), chip(2 * ROWS, LANES)),
-        in_specs=[SMEM] + [VMEM] * 6,
-        out_specs=(VMEM, VMEM),
+        out_shape=chip(RANK * PLANES, LANES),
+        in_specs=[VMEM] * 3,
+        out_specs=VMEM,
         scratch_shapes=[
             pltpu.VMEM((2, 3, 3 * ROWS, 8, LANES), jnp.float32),
             pltpu.VMEM((3 * ROWS, 8, LANES), jnp.float32),
         ],
-        name="inner",
-    )(
-        obs_count, block, near, far,
-        obs_cells.reshape(1, slots), obs_values.reshape(1, slots), obs_error.reshape(1, slots),
-    )
+        name="inner", compiler_params=SMALL_VMEM,
+    )(block, near, far)
     split, mean, gram = pl.pallas_call(
         side_kernel,
         out_shape=(
@@ -380,7 +392,7 @@
             pltpu.VMEM((RANK, ROWS * LANES), jnp.float32),
             pltpu.VMEM((RANK + 8, ROWS * LANES), jnp.float32),
         ],
-        name="side",
+        name="side", compiler_params=SMALL_VMEM,
     )(block, near, far, on_chip(halo), near_halo, far_halo, on_chip(inner), on_chip(weights))
     gram = jnp.sum(sum_over(gram, "lat"), 0)
     parts = sum_over(gram, "lon")
@@ -389,7 +401,7 @@
         out_shape=(f32(PLANES, LANES), f32(RANK * PLANES, LANES)),
         in_specs=[VMEM] * 3,
         out_specs=(VMEM, VMEM),
-        name="analysis",
+        name="analysis", compiler_params=SMALL_VMEM,
     )(on_chip(parts), on_chip(split), on_chip(mean))
     return update.reshape(background_expectation.shape), analysis.reshape(factor.shape)
 

time: 66.1 us -> 69.2 us (1.047)
  blocking collectives: 25.6 us -> 29.1 us
  local copies, waits for them, and re-layouts: 0.02 us -> 3.07 us
  Pallas kernels: 7.45 us -> 5.5 us
  waiting for transfers between devices: 3.06 us -> 1.27 us
    all_to_all x2, blocking collectives: 25.6 us -> 29.1 us  [sum_over(): return lax.all_to_all(sent, axis, 0, 0)]
    unnamed x0 -> x12, local copies, waits for them, and re-layouts: none -> 3.05 us
    ppermute x6, waiting for transfers between devices: 3.06 us -> 1.27 us  [swapped(): return lax.ppermute(value, axis, pairs + [(j, i) for i, j in pairs])]
    pallas_call x2 -> x3, Pallas kernels: 3.61 us -> 1.93 us  [the longest x1 1.35 us: per_device(): pl.pallas_call(inner_kernel, out_shape=chip(RANK * PLANES, LANES), in_spe...]
  transfers between devices with their start and end apart: 6 -> 6, of which waited for: 1 -> 1; matrix products, arithmetic and copies ran while one was open for 0% -> 0% of each run, Pallas kernels for 3% -> 2%
where the time goes in v5:
time: 69.2 us; the launch traced here: 68.7 us
  blocking collectives  29.1 us (42%)
  starting transfers between devices  28.2 us (41%)
  Pallas kernels  5.5 us (8%)
  local copies, waits for them, and re-layouts  3.07 us (4%)
  between operations  1.46 us (2%)
  waiting for transfers between devices  1.27 us (2%)
    all_to_all x2, blocking collectives, sum_over(): return lax.all_to_all(sent, axis, 0, 0)  29.1 us
    ppermute x6, starting transfers between devices, swapped(): return lax.ppermute(value, axis, pairs + [(j, i) for i, j in pairs])  28.2 us
    unnamed x12, local copies, waits for them, and re-layouts  3.05 us
    pallas_call x1, Pallas kernels, per_device(): pl.pallas_call(analysis_kernel, out_shape=(f32(PLANES, LANES), f32(RANK *...  2.12 us
    pallas_call x1, Pallas kernels, per_device(): pl.pallas_call(side_kernel, out_shape=(pltpu.VMEM((3 * RANK, PLANES * LAN...  1.45 us
  transfers between devices with their start and end apart: 6, of which 1 were waited for; matrix products, arithmetic and copies ran while one was open for 0% of the time, Pallas kernels for 2%

profile of v5, /device:TPU:1, one launch (start us, length us, event | category | flops | bytes accessed | tf_op | source)
XLA Modules:
  0.0 68.7 jit_solution(2806161053638488915)
XLA Ops:
  0.6 0.0 copy-start
  0.6 1.0 %copy-done = f32[32,3,8,128]{3,2,1,0:T(8,128)S(1)} copy-done((f32[32,3,8,128]{3,2,1,0:T(8,128)S(1)}, f32[32,3,8,128]{3,2,1,0:T(8,128)}, u32[]{:S(2)}) %copy-start) | copy-done | bytes 393240
  1.6 0.0 copy-start.1
  1.6 0.7 %copy-done.1 = f32[3,8,128]{2,1,0:T(8,128)S(1)} copy-done((f32[3,8,128]{2,1,0:T(8,128)S(1)}, f32[3,8,128]{2,1,0:T(8,128)}, u32[]{:S(2)}) %copy-start.1) | copy-done | bytes 12312
  2.3 0.0 copy-start.2
  2.3 0.7 copy-done.2
  3.0 0.3 pack.1
  3.3 4.6 %collective-permute-start.1 = (f32[1088,128]{1,0:T(8,128)S(1)}, f32[1088,128]{1,0:T(8,128)S(1)}, u32[]{:S(2)}, u32[]{:S(2)}) collective-permute-start(f32[1088,128]{1,0:T(8,128)S(1)} %get-tuple-element.10.own_ref), channel_id=1, source_target_pairs={{32,64},{96,128},{160,192},{224,256},{288,320},{352,384},{416,448}... | collective-permute-start | bytes 1671176 | tf_op jit(solution)/shard_map/ppermute | solution.py:328
  7.9 4.9 %collective-permute-start = (f32[1088,128]{1,0:T(8,128)S(1)}, f32[1088,128]{1,0:T(8,128)S(1)}, u32[]{:S(2)}, u32[]{:S(2)}) collective-permute-start(f32[1088,128]{1,0:T(8,128)S(1)} %get-tuple-element.10.own_ref), channel_id=1, source_target_pairs={{0,32},{64,96},{128,160},{192,224},{256,288},{320,352},{384,416},{... | collective-permute-start | bytes 1671176 | tf_op jit(solution)/shard_map/ppermute | solution.py:328
  12.8 1.9 %collective-permute-start.2 = (f32[64,128]{1,0:T(8,128)S(1)}, f32[64,128]{1,0:T(8,128)S(1)}, u32[]{:S(2)}, u32[]{:S(2)}) collective-permute-start(f32[64,128]{1,0:T(8,128)S(1)} %get-tuple-element.11), channel_id=1, source_target_pairs={{0,1},{2,3},{4,5},{6,7},{8,9},{10,11},{12,13},{14,15},{16,17},{18,... | collective-permute-start | bytes 98312 | tf_op jit(solution)/shard_map/ppermute | solution.py:328
  14.7 10.2 %collective-permute-start.3 = (f32[64,128]{1,0:T(8,128)S(1)}, f32[64,128]{1,0:T(8,128)S(1)}, u32[]{:S(2)}, u32[]{:S(2)}) collective-permute-start(f32[64,128]{1,0:T(8,128)S(1)} %get-tuple-element.12), channel_id=1, source_target_pairs={{1,2},{3,4},{5,6},{7,8},{9,10},{11,12},{13,14},{15,16},{17,18},{19... | collective-permute-start | bytes 98312 | tf_op jit(solution)/shard_map/ppermute | solution.py:328
  24.9 0.0 collective-permute-done.2
  25.0 1.3 %collective-permute-done.3 = f32[64,128]{1,0:T(8,128)S(1)} collective-permute-done((f32[64,128]{1,0:T(8,128)S(1)}, f32[64,128]{1,0:T(8,128)S(1)}, u32[]{:S(2)}, u32[]{:S(2)}) %collective-permute-start.3) | collective-permute-done | bytes 32800 | tf_op jit(solution)/shard_map/ppermute | solution.py:328
  26.2 4.7 %collective-permute-start.5 = (f32[128,128]{1,0:T(8,128)S(1)}, f32[128,128]{1,0:T(8,128)S(1)}, u32[]{:S(2)}, u32[]{:S(2)}) collective-permute-start(f32[128,128]{1,0:T(8,128)S(1)} %bitcast.17), channel_id=1, source_target_pairs={{32,64},{96,128},{160,192},{224,256},{288,320},{352,384},{416,448}... | collective-permute-start | bytes 196616 | tf_op jit(solution)/shard_map/ppermute | solution.py:328
  31.0 1.9 %collective-permute-start.4 = (f32[128,128]{1,0:T(8,128)S(1)}, f32[128,128]{1,0:T(8,128)S(1)}, u32[]{:S(2)}, u32[]{:S(2)}) collective-permute-start(f32[128,128]{1,0:T(8,128)S(1)} %bitcast.18), channel_id=1, source_target_pairs={{0,32},{64,96},{128,160},{192,224},{256,288},{320,352},{384,416},{... | collective-permute-start | bytes 196616 | tf_op jit(solution)/shard_map/ppermute | solution.py:328
  32.9 0.0 copy-start.4
  32.9 0.0 copy-start.5
  33.6 0.0 copy-start.3
  33.6 0.0 copy-done.4
  33.6 0.0 copy-done.5
  33.6 0.7 copy-done.3
  34.3 0.3 weigh.1.weight_ref
  34.5 0.0 collective-permute-done.1.far_ref
  34.5 0.0 collective-permute-done.near_ref
  34.6 1.4 %inner.1.inner_ref = f32[768,128]{1,0:T(8,128)S(1)} custom-call(f32[1088,128]{1,0:T(8,128)S(1)} %get-tuple-element.10.own_ref, f32[1088,128]{1,0:T(8,128)S(1)} %collective-permute-done.near_ref, f32[1088,128]{1,0:T(8,128)S(1)} %collective-permute-done.1.far_ref), custom_call_target="tpu_custom_call" | custom-call | tf_op jit(solution)/shard_map/inner/pallas_call | solution.py:369
  35.9 0.0 collective-permute-done.5.far_halo_ref
  35.9 0.0 collective-permute-done.4.near_halo_ref
  35.9 1.4 %side.1 = (bf16[96,3072]{1,0:T(8,128)(2,1)S(1)}, f32[24,128]{1,0:T(8,128)S(1)}, f32[8,128]{1,0:T(8,128)S(1)}) custom-call(f32[1088,128]{1,0:T(8,128)S(1)} %get-tuple-element.10.own_ref, f32[1088,128]{1,0:T(8,128)S(1)} %collective-permute-done.near_ref, f32[1088,128]{1,0:T(8,128)S(1)} %collective-permute-done.1.far_ref, f32[128,128]{1,0:T(8,128)S(1)} %bitcast.19, ...), custom_call_target="tpu_custom_call" | custom-call | tf_op jit(solution)/shard_map/side/pallas_call | solution.py:380
  37.4 13.7 %all_to_all.10 = f32[16,8,128]{2,1,0:T(8,128)S(1)} all-to-all(f32[16,8,128]{2,1,0:T(8,128)S(1)} %broadcast_in_dim.4), channel_id=1, replica_groups=mesh['lat'=16,'lon'=32] {'lat'}, dimensions={0} | all-to-all | bytes 131072 | tf_op jit(solution)/shard_map/all_to_all | solution.py:334
  51.2 15.4 %all_to_all.11.parts_ref = f32[32,8,128]{2,1,0:T(8,128)S(1)} all-to-all(f32[32,8,128]{2,1,0:T(8,128)S(1)} %broadcast_in_dim.5), channel_id=1, replica_groups=mesh['lat'=16,'lon'=32] {'lon'}, dimensions={0} | all-to-all | bytes 262144 | tf_op jit(solution)/shard_map/all_to_all | solution.py:334
  66.5 2.1 %analysis.1 = (f32[24,128]{1,0:T(8,128)}, f32[768,128]{1,0:T(8,128)}) custom-call(f32[32,8,128]{2,1,0:T(8,128)S(1)} %all_to_all.11.parts_ref, bf16[96,3072]{1,0:T(8,128)(2,1)S(1)} %get-tuple-element.14.split_ref, f32[24,128]{1,0:T(8,128)S(1)} %get-tuple-element.15.mean_ref), custom_call_target="tpu_custom_call" | custom-call | tf_op jit(solution)/shard_map/analysis/pallas_call | solution.py:399
  (7 shorter events, 0.1 us)
Async XLA Ops:
  0.6 1.0 %copy-start = (f32[32,3,8,128]{3,2,1,0:T(8,128)S(1)}, f32[32,3,8,128]{3,2,1,0:T(8,128)}, u32[]{:S(2)}) copy-start(f32[32,3,8,128]{3,2,1,0:T(8,128)} %param.8) | copy-start | bytes 1179652
  1.6 0.7 %copy-start.1 = (f32[3,8,128]{2,1,0:T(8,128)S(1)}, f32[3,8,128]{2,1,0:T(8,128)}, u32[]{:S(2)}) copy-start(f32[3,8,128]{2,1,0:T(8,128)} %param.7) | copy-start | bytes 36868
  2.3 0.7 %copy-start.2 = (f32[8,128]{1,0:T(8,128)S(1)}, f32[8,128]{1,0:T(8,128)}, u32[]{:S(2)}) copy-start(f32[8,128]{1,0:T(8,128)} %depth_ref.1) | copy-start | bytes 12292
  3.3 31.2 %collective-permute-start.1 = (f32[1088,128]{1,0:T(8,128)S(1)}, f32[1088,128]{1,0:T(8,128)S(1)}, u32[]{:S(2)}, u32[]{:S(2)}) collective-permute-start(f32[1088,128]{1,0:T(8,128)S(1)} %get-tuple-element.10.own_ref), channel_id=1, source_target_pairs={{32,64},{96,128},{160,192},{224,256},{288,320},{352,384},{416,448}... | collective-permute-start | bytes 1671176 | tf_op jit(solution)/shard_map/ppermute | solution.py:328
  7.9 26.6 %collective-permute-start = (f32[1088,128]{1,0:T(8,128)S(1)}, f32[1088,128]{1,0:T(8,128)S(1)}, u32[]{:S(2)}, u32[]{:S(2)}) collective-permute-start(f32[1088,128]{1,0:T(8,128)S(1)} %get-tuple-element.10.own_ref), channel_id=1, source_target_pairs={{0,32},{64,96},{128,160},{192,224},{256,288},{320,352},{384,416},{... | collective-permute-start | bytes 1671176 | tf_op jit(solution)/shard_map/ppermute | solution.py:328
  12.8 12.2 %collective-permute-start.2 = (f32[64,128]{1,0:T(8,128)S(1)}, f32[64,128]{1,0:T(8,128)S(1)}, u32[]{:S(2)}, u32[]{:S(2)}) collective-permute-start(f32[64,128]{1,0:T(8,128)S(1)} %get-tuple-element.11), channel_id=1, source_target_pairs={{0,1},{2,3},{4,5},{6,7},{8,9},{10,11},{12,13},{14,15},{16,17},{18,... | collective-permute-start | bytes 98312 | tf_op jit(solution)/shard_map/ppermute | solution.py:328
  14.7 11.5 %collective-permute-start.3 = (f32[64,128]{1,0:T(8,128)S(1)}, f32[64,128]{1,0:T(8,128)S(1)}, u32[]{:S(2)}, u32[]{:S(2)}) collective-permute-start(f32[64,128]{1,0:T(8,128)S(1)} %get-tuple-element.12), channel_id=1, source_target_pairs={{1,2},{3,4},{5,6},{7,8},{9,10},{11,12},{13,14},{15,16},{17,18},{19... | collective-permute-start | bytes 98312 | tf_op jit(solution)/shard_map/ppermute | solution.py:328
  26.2 9.7 %collective-permute-start.5 = (f32[128,128]{1,0:T(8,128)S(1)}, f32[128,128]{1,0:T(8,128)S(1)}, u32[]{:S(2)}, u32[]{:S(2)}) collective-permute-start(f32[128,128]{1,0:T(8,128)S(1)} %bitcast.17), channel_id=1, source_target_pairs={{32,64},{96,128},{160,192},{224,256},{288,320},{352,384},{416,448}... | collective-permute-start | bytes 196616 | tf_op jit(solution)/shard_map/ppermute | solution.py:328
  31.0 4.9 %collective-permute-start.4 = (f32[128,128]{1,0:T(8,128)S(1)}, f32[128,128]{1,0:T(8,128)S(1)}, u32[]{:S(2)}, u32[]{:S(2)}) collective-permute-start(f32[128,128]{1,0:T(8,128)S(1)} %bitcast.18), channel_id=1, source_target_pairs={{0,32},{64,96},{128,160},{192,224},{256,288},{320,352},{384,416},{... | collective-permute-start | bytes 196616 | tf_op jit(solution)/shard_map/ppermute | solution.py:328
  32.9 0.7 %copy-start.4 = (f32[256]{0:T(256)S(1)}, f32[256]{0:T(256)}, u32[]{:S(2)}) copy-start(f32[256]{0:T(256)} %param.12) | copy-start | bytes 3076
  32.9 0.7 %copy-start.5 = (f32[256]{0:T(256)S(1)}, f32[256]{0:T(256)}, u32[]{:S(2)}) copy-start(f32[256]{0:T(256)} %param.13) | copy-start | bytes 3076
  33.6 0.7 copy-start.3

commit v6 on v5

--- a/solution.py
+++ b/solution.py
@@ -38,10 +38,32 @@
     return pl.ds((row * PER_ROW + tile) * 8, 8)
 
 
-def pack_kernel(factor_ref, mean_ref, depth_ref, block_ref, even_edge_ref, odd_edge_ref):
+def observed(count_ref, cells_ref, values_ref, error_ref):
+    slots = cells_ref.shape[1]
+    live = lax.broadcasted_iota(jnp.int32, (1, slots), 1) < count_ref[...]
+    weight = jnp.where(live, 1.0, 0.0) / error_ref[...]
+    square = weight * weight
+    cells = cells_ref[...]
+    row_of = cells // LANES
+    lane_of = cells - row_of * LANES
+    in_row = lax.broadcasted_iota(jnp.int32, (ROWS, slots), 0) == row_of
+    spread = jnp.concatenate(
+        [jnp.where(in_row, square, 0.0), jnp.where(in_row, square * values_ref[...], 0.0)], 0
+    )
+    in_lane = lax.broadcasted_iota(jnp.int32, (LANES, slots), 0) == lane_of
+    return lax.dot_general(
+        spread, jnp.where(in_lane, 1.0, 0.0), NT, precision=HIGHEST, preferred_element_type=jnp.float32
+    )
+
+
+def pack_kernel(
+    factor_ref, mean_ref, depth_ref, count_ref, cells_ref, values_ref, error_ref,
+    block_ref, even_edge_ref, odd_edge_ref, weight_ref,
+):
     lane = lane_iota()
     part = lane // GROUP
     octet = (lane // 8) & 3
+    weight_ref[...] = observed(count_ref, cells_ref, values_ref, error_ref)
     even = lax.rem(lax.axis_index("lon"), 2) == 0
     eastward, westward = {}, {}
     for row in range(ROWS):
@@ -111,24 +133,6 @@
                 east, north = e[row], n[row]
                 e[row] = east - PULL * lon_difference(h[row]) + ROTATION * north
                 n[row] = north - row_pull * (h[row + 1] - h[row - 1]) - ROTATION * east
-
-
-def weight_kernel(count_ref, cells_ref, values_ref, error_ref, out_ref):
-    slots = cells_ref.shape[1]
-    live = lax.broadcasted_iota(jnp.int32, (1, slots), 1) < count_ref[...]
-    weight = jnp.where(live, 1.0, 0.0) / error_ref[...]
-    square = weight * weight
-    cells = cells_ref[...]
-    row_of = cells // LANES
-    lane_of = cells - row_of * LANES
-    in_row = lax.broadcasted_iota(jnp.int32, (ROWS, slots), 0) == row_of
-    spread = jnp.concatenate(
-        [jnp.where(in_row, square, 0.0), jnp.where(in_row, square * values_ref[...], 0.0)], 0
-    )
-    in_lane = lax.broadcasted_iota(jnp.int32, (LANES, slots), 0) == lane_of
-    out_ref[...] = lax.dot_general(
-        spread, jnp.where(in_lane, 1.0, 0.0), NT, precision=HIGHEST, preferred_element_type=jnp.float32
-    )
 
 
 def inner_kernel(own_ref, near_ref, far_ref, out_ref, state, depth):
@@ -338,25 +342,22 @@
     background_expectation, factor, average_thickness, obs_cells, obs_count, obs_values, obs_error
 ):
     assert factor.shape == (RANK, 3, ROWS, LANES)
-    block, even_edges, odd_edges = pl.pallas_call(
+    slots = obs_cells.shape[0]
+    block, even_edges, odd_edges, weights = pl.pallas_call(
         pack_kernel,
-        out_shape=(chip(ROWS * PER_ROW * 8, LANES),) + (chip(ROWS * 8, LANES),) * 2,
-        in_specs=[VMEM] * 3,
-        out_specs=(VMEM,) * 3,
-        name="pack", compiler_params=SMALL_VMEM,
-    )(factor.reshape(RANK * PLANES, LANES), background_expectation.reshape(PLANES, LANES), average_thickness)
+        out_shape=(chip(ROWS * PER_ROW * 8, LANES),) + (chip(ROWS * 8, LANES),) * 2 + (chip(2 * ROWS, LANES),),
+        in_specs=[VMEM] * 7,
+        out_specs=(VMEM,) * 4,
+        name="pack",
+    )(
+        factor.reshape(RANK * PLANES, LANES), background_expectation.reshape(PLANES, LANES), average_thickness,
+        obs_count.reshape(1, 1), obs_cells.reshape(1, slots), obs_values.reshape(1, slots), obs_error.reshape(1, slots),
+    )
     block = on_chip(block)
     even_edges = swapped(even_edges, "lon", 0, True)
     odd_edges = swapped(odd_edges, "lon", 1, True)
     far = on_chip(swapped(block, "lat", 1, False))
     near = on_chip(swapped(block, "lat", 0, False))
-    slots = obs_cells.shape[0]
-    weights = pl.pallas_call(
-        weight_kernel, out_shape=chip(2 * ROWS, LANES), in_specs=[VMEM] * 4, out_specs=VMEM, name="weigh", compiler_params=SMALL_VMEM
-    )(
-        obs_count.reshape(1, 1), obs_cells.reshape(1, slots),
-        obs_values.reshape(1, slots), obs_error.reshape(1, slots),
-    )
     shape = (ROWS // 4, 4 * 8, LANES)
     eastern = (lax.broadcasted_iota(jnp.int32, shape, 2) & 8) // 8 != 1
     from_even = eastern == (lax.rem(lax.axis_index("lon"), 2) == 0)

time: 69.2 us -> 67.4 us (0.974)
  local copies, waits for them, and re-layouts: 3.07 us -> 0.02 us
  Pallas kernels: 5.5 us -> 6.29 us
  blocking collectives: 29.1 us -> 29.8 us
    unnamed x12 -> x0, local copies, waits for them, and re-layouts: 3.05 us -> none
    pallas_call x1, Pallas kernels: 0.32 us -> 1.37 us  [per_device(): pl.pallas_call(pack_kernel, out_shape=(chip(ROWS * PER_ROW * 8, LANES),)...]
    all_to_all x2, blocking collectives: 29.1 us -> 29.8 us  [sum_over(): return lax.all_to_all(sent, axis, 0, 0)]
where the time goes in v6:
time: 67.4 us; the launch traced here: 67.1 us
  blocking collectives  29.8 us (44%)
  starting transfers between devices  28.2 us (42%)
  Pallas kernels  6.29 us (9%)
  between operations  1.41 us (2%)
  waiting for transfers between devices  1.26 us (2%)
    all_to_all x2, blocking collectives, sum_over(): return lax.all_to_all(sent, axis, 0, 0)  29.8 us
    ppermute x6, starting transfers between devices, swapped(): return lax.ppermute(value, axis, pairs + [(j, i) for i, j in pairs])  28.2 us
    pallas_call x1, Pallas kernels, per_device(): pl.pallas_call(analysis_kernel, out_shape=(f32(PLANES, LANES), f32(RANK *...  2.12 us
    pallas_call x1, Pallas kernels, per_device(): pl.pallas_call(side_kernel, out_shape=(pltpu.VMEM((3 * RANK, PLANES * LAN...  1.45 us
    pallas_call x1, Pallas kernels, per_device(): pl.pallas_call(pack_kernel, out_shape=(chip(ROWS * PER_ROW * 8, LANES),)...  1.37 us
    pallas_call x1, Pallas kernels, per_device(): pl.pallas_call(inner_kernel, out_shape=chip(RANK * PLANES, LANES), in_spe...  1.35 us
  transfers between devices with their start and end apart: 6, of which 1 were waited for; matrix products, arithmetic and copies ran while one was open for 0% of the time, Pallas kernels for 2%

profile of v6, /device:TPU:1, one launch (start us, length us, event | category | flops | bytes accessed | tf_op | source)
XLA Modules:
  0.0 67.1 jit_solution(10202173180048564803)
XLA Ops:
  1.3 1.4 %pack.1 = (f32[1088,128]{1,0:T(8,128)S(1)}, f32[64,128]{1,0:T(8,128)S(1)}, f32[64,128]{1,0:T(8,128)S(1)}, f32[16,128]{1,0:T(8,128)S(1)}) custom-call(f32[768,128]{1,0:T(8,128)} %bitcast.19, f32[24,128]{1,0:T(8,128)} %bitcast.22, f32[8,128]{1,0:T(8,128)} %depth_ref.1, s32[1,1]{1,0:T(1,128)} %bitcast.15.count_ref, s32[1,256]{1,0:T(1,128)} %bitcast.23, ...), custom_call_target="tpu_custom_call" | custom-call | tf_op jit(solution)/shard_map/pack/pallas_call | solution.py:346
  2.7 4.6 %collective-permute-start.1 = (f32[1088,128]{1,0:T(8,128)S(1)}, f32[1088,128]{1,0:T(8,128)S(1)}, u32[]{:S(2)}, u32[]{:S(2)}) collective-permute-start(f32[1088,128]{1,0:T(8,128)S(1)} %get-tuple-element.11.own_ref), channel_id=1, source_target_pairs={{32,64},{96,128},{160,192},{224,256},{288,320},{352,384},{416,448}... | collective-permute-start | bytes 1671176 | tf_op jit(solution)/shard_map/ppermute | solution.py:332
  7.2 4.9 %collective-permute-start = (f32[1088,128]{1,0:T(8,128)S(1)}, f32[1088,128]{1,0:T(8,128)S(1)}, u32[]{:S(2)}, u32[]{:S(2)}) collective-permute-start(f32[1088,128]{1,0:T(8,128)S(1)} %get-tuple-element.11.own_ref), channel_id=1, source_target_pairs={{0,32},{64,96},{128,160},{192,224},{256,288},{320,352},{384,416},{... | collective-permute-start | bytes 1671176 | tf_op jit(solution)/shard_map/ppermute | solution.py:332
  12.1 1.9 %collective-permute-start.2 = (f32[64,128]{1,0:T(8,128)S(1)}, f32[64,128]{1,0:T(8,128)S(1)}, u32[]{:S(2)}, u32[]{:S(2)}) collective-permute-start(f32[64,128]{1,0:T(8,128)S(1)} %get-tuple-element.12), channel_id=1, source_target_pairs={{0,1},{2,3},{4,5},{6,7},{8,9},{10,11},{12,13},{14,15},{16,17},{18,... | collective-permute-start | bytes 98312 | tf_op jit(solution)/shard_map/ppermute | solution.py:332
  14.0 10.2 %collective-permute-start.3 = (f32[64,128]{1,0:T(8,128)S(1)}, f32[64,128]{1,0:T(8,128)S(1)}, u32[]{:S(2)}, u32[]{:S(2)}) collective-permute-start(f32[64,128]{1,0:T(8,128)S(1)} %get-tuple-element.13), channel_id=1, source_target_pairs={{1,2},{3,4},{5,6},{7,8},{9,10},{11,12},{13,14},{15,16},{17,18},{19... | collective-permute-start | bytes 98312 | tf_op jit(solution)/shard_map/ppermute | solution.py:332
  24.3 0.0 collective-permute-done.2
  24.3 1.3 %collective-permute-done.3 = f32[64,128]{1,0:T(8,128)S(1)} collective-permute-done((f32[64,128]{1,0:T(8,128)S(1)}, f32[64,128]{1,0:T(8,128)S(1)}, u32[]{:S(2)}, u32[]{:S(2)}) %collective-permute-start.3) | collective-permute-done | bytes 32800 | tf_op jit(solution)/shard_map/ppermute | solution.py:332
  25.6 4.7 %collective-permute-start.5 = (f32[128,128]{1,0:T(8,128)S(1)}, f32[128,128]{1,0:T(8,128)S(1)}, u32[]{:S(2)}, u32[]{:S(2)}) collective-permute-start(f32[128,128]{1,0:T(8,128)S(1)} %bitcast.16), channel_id=1, source_target_pairs={{32,64},{96,128},{160,192},{224,256},{288,320},{352,384},{416,448}... | collective-permute-start | bytes 196616 | tf_op jit(solution)/shard_map/ppermute | solution.py:332
  30.3 1.9 %collective-permute-start.4 = (f32[128,128]{1,0:T(8,128)S(1)}, f32[128,128]{1,0:T(8,128)S(1)}, u32[]{:S(2)}, u32[]{:S(2)}) collective-permute-start(f32[128,128]{1,0:T(8,128)S(1)} %bitcast.17), channel_id=1, source_target_pairs={{0,32},{64,96},{128,160},{192,224},{256,288},{320,352},{384,416},{... | collective-permute-start | bytes 196616 | tf_op jit(solution)/shard_map/ppermute | solution.py:332
  32.2 0.0 collective-permute-done.1.far_ref
  32.2 0.0 collective-permute-done.near_ref
  32.2 1.4 %inner.1.inner_ref = f32[768,128]{1,0:T(8,128)S(1)} custom-call(f32[1088,128]{1,0:T(8,128)S(1)} %get-tuple-element.11.own_ref, f32[1088,128]{1,0:T(8,128)S(1)} %collective-permute-done.near_ref, f32[1088,128]{1,0:T(8,128)S(1)} %collective-permute-done.1.far_ref), custom_call_target="tpu_custom_call" | custom-call | tf_op jit(solution)/shard_map/inner/pallas_call | solution.py:370
  33.6 0.0 collective-permute-done.5.far_halo_ref
  33.6 0.0 collective-permute-done.4.near_halo_ref
  33.6 1.4 %side.1 = (bf16[96,3072]{1,0:T(8,128)(2,1)S(1)}, f32[24,128]{1,0:T(8,128)S(1)}, f32[8,128]{1,0:T(8,128)S(1)}) custom-call(f32[1088,128]{1,0:T(8,128)S(1)} %get-tuple-element.11.own_ref, f32[1088,128]{1,0:T(8,128)S(1)} %collective-permute-done.near_ref, f32[1088,128]{1,0:T(8,128)S(1)} %collective-permute-done.1.far_ref, f32[128,128]{1,0:T(8,128)S(1)} %bitcast.18, ...), custom_call_target="tpu_custom_call" | custom-call | tf_op jit(solution)/shard_map/side/pallas_call | solution.py:381
  35.1 14.1 %all_to_all.10 = f32[16,8,128]{2,1,0:T(8,128)S(1)} all-to-all(f32[16,8,128]{2,1,0:T(8,128)S(1)} %broadcast_in_dim.4), channel_id=1, replica_groups=mesh['lat'=16,'lon'=32] {'lat'}, dimensions={0} | all-to-all | bytes 131072 | tf_op jit(solution)/shard_map/all_to_all | solution.py:338
  49.3 15.7 %all_to_all.11.parts_ref = f32[32,8,128]{2,1,0:T(8,128)S(1)} all-to-all(f32[32,8,128]{2,1,0:T(8,128)S(1)} %broadcast_in_dim.5), channel_id=1, replica_groups=mesh['lat'=16,'lon'=32] {'lon'}, dimensions={0} | all-to-all | bytes 262144 | tf_op jit(solution)/shard_map/all_to_all | solution.py:338
  64.9 2.1 %analysis.1 = (f32[24,128]{1,0:T(8,128)}, f32[768,128]{1,0:T(8,128)}) custom-call(f32[32,8,128]{2,1,0:T(8,128)S(1)} %all_to_all.11.parts_ref, bf16[96,3072]{1,0:T(8,128)(2,1)S(1)} %get-tuple-element.16.split_ref, f32[24,128]{1,0:T(8,128)S(1)} %get-tuple-element.17.mean_ref), custom_call_target="tpu_custom_call" | custom-call | tf_op jit(solution)/shard_map/analysis/pallas_call | solution.py:400
  (7 shorter events, 0.1 us)
Async XLA Ops:
  2.7 29.6 %collective-permute-start.1 = (f32[1088,128]{1,0:T(8,128)S(1)}, f32[1088,128]{1,0:T(8,128)S(1)}, u32[]{:S(2)}, u32[]{:S(2)}) collective-permute-start(f32[1088,128]{1,0:T(8,128)S(1)} %get-tuple-element.11.own_ref), channel_id=1, source_target_pairs={{32,64},{96,128},{160,192},{224,256},{288,320},{352,384},{416,448}... | collective-permute-start | bytes 1671176 | tf_op jit(solution)/shard_map/ppermute | solution.py:332
  7.2 25.0 %collective-permute-start = (f32[1088,128]{1,0:T(8,128)S(1)}, f32[1088,128]{1,0:T(8,128)S(1)}, u32[]{:S(2)}, u32[]{:S(2)}) collective-permute-start(f32[1088,128]{1,0:T(8,128)S(1)} %get-tuple-element.11.own_ref), channel_id=1, source_target_pairs={{0,32},{64,96},{128,160},{192,224},{256,288},{320,352},{384,416},{... | collective-permute-start | bytes 1671176 | tf_op jit(solution)/shard_map/ppermute | solution.py:332
  12.1 12.2 %collective-permute-start.2 = (f32[64,128]{1,0:T(8,128)S(1)}, f32[64,128]{1,0:T(8,128)S(1)}, u32[]{:S(2)}, u32[]{:S(2)}) collective-permute-start(f32[64,128]{1,0:T(8,128)S(1)} %get-tuple-element.12), channel_id=1, source_target_pairs={{0,1},{2,3},{4,5},{6,7},{8,9},{10,11},{12,13},{14,15},{16,17},{18,... | collective-permute-start | bytes 98312 | tf_op jit(solution)/shard_map/ppermute | solution.py:332
  14.0 11.5 %collective-permute-start.3 = (f32[64,128]{1,0:T(8,128)S(1)}, f32[64,128]{1,0:T(8,128)S(1)}, u32[]{:S(2)}, u32[]{:S(2)}) collective-permute-start(f32[64,128]{1,0:T(8,128)S(1)} %get-tuple-element.13), channel_id=1, source_target_pairs={{1,2},{3,4},{5,6},{7,8},{9,10},{11,12},{13,14},{15,16},{17,18},{19... | collective-permute-start | bytes 98312 | tf_op jit(solution)/shard_map/ppermute | solution.py:332
  25.6 8.1 %collective-permute-start.5 = (f32[128,128]{1,0:T(8,128)S(1)}, f32[128,128]{1,0:T(8,128)S(1)}, u32[]{:S(2)}, u32[]{:S(2)}) collective-permute-start(f32[128,128]{1,0:T(8,128)S(1)} %bitcast.16), channel_id=1, source_target_pairs={{32,64},{96,128},{160,192},{224,256},{288,320},{352,384},{416,448}... | collective-permute-start | bytes 196616 | tf_op jit(solution)/shard_map/ppermute | solution.py:332
  30.3 3.3 %collective-permute-start.4 = (f32[128,128]{1,0:T(8,128)S(1)}, f32[128,128]{1,0:T(8,128)S(1)}, u32[]{:S(2)}, u32[]{:S(2)}) collective-permute-start(f32[128,128]{1,0:T(8,128)S(1)} %bitcast.17), channel_id=1, source_target_pairs={{0,32},{64,96},{128,160},{192,224},{256,288},{320,352},{384,416},{... | collective-permute-start | bytes 196616 | tf_op jit(solution)/shard_map/ppermute | solution.py:332

commit v7 on v6

--- a/solution.py
+++ b/solution.py
@@ -17,8 +17,8 @@
 TILES = RANK // 8
 PLANES = 3 * ROWS
 GROUP = LANES // TILES
-MAIN, SMALL, SIDE = 0, 12, 13
-PER_ROW = 17
+MAIN, SMALL = 0, 12
+PER_ROW = 13
 MOVES = (0, 16, 8, 24)
 PULL = 0.5 * TIME_STEP
 WIDTH = 8
@@ -56,12 +56,24 @@
     )
 
 
+def side_tile(values):
+    part = lane_iota() // GROUP
+    if len(values) == 1:
+        side = pltpu.roll(values[0], 16, 1)
+        side = jnp.where(part == 0, side, pltpu.roll(side, GROUP, 1))
+        return jnp.where(part < 2, side, pltpu.roll(side, 2 * GROUP, 1))
+    side = None
+    for tile, value in enumerate(values):
+        moved = pltpu.roll(value, 16 + GROUP * tile, 1)
+        side = moved if side is None else jnp.where(part == tile, moved, side)
+    return side
+
+
 def pack_kernel(
     factor_ref, mean_ref, depth_ref, count_ref, cells_ref, values_ref, error_ref,
-    block_ref, even_edge_ref, odd_edge_ref, weight_ref,
+    block_ref, side_ref, even_edge_ref, odd_edge_ref, weight_ref,
 ):
     lane = lane_iota()
-    part = lane // GROUP
     octet = (lane // 8) & 3
     weight_ref[...] = observed(count_ref, cells_ref, values_ref, error_ref)
     even = lax.rem(lax.axis_index("lon"), 2) == 0
@@ -75,18 +87,13 @@
         block_ref[block_at(row, SMALL), :] = small
         sides = []
         for field in range(3):
-            side = None
-            for tile in range(TILES):
-                value = factor_ref[member_rows(field, row, tile), :]
+            values = [factor_ref[member_rows(field, row, tile), :] for tile in range(TILES)]
+            for tile, value in enumerate(values):
                 block_ref[block_at(row, MAIN + TILES * field + tile), :] = value
-                moved = pltpu.roll(value, 16 + GROUP * tile, 1)
-                side = moved if side is None else jnp.where(part == tile, moved, side)
-            sides.append(side)
-        side = pltpu.roll(small, 16, 1)
-        side = jnp.where(part == 0, side, pltpu.roll(side, GROUP, 1))
-        sides.append(jnp.where(part < 2, side, pltpu.roll(side, 2 * GROUP, 1)))
+            sides.append(side_tile(values))
+        sides.append(side_tile([small]))
         for which, side in enumerate(sides):
-            block_ref[block_at(row, SIDE + which), :] = side
+            side_ref[pl.ds((row * 4 + which) * 8, 8), :] = side
             move = MOVES[row % 4]
             moved = pltpu.roll(side, move, 1) if move else side
             if row % 4 == 0:
@@ -166,7 +173,7 @@
 
 
 def side_kernel(
-    own_ref, near_ref, far_ref, halo_ref, near_halo_ref, far_halo_ref, inner_ref, weight_ref,
+    own_ref, side_ref, near_ref, far_ref, halo_ref, near_halo_ref, far_halo_ref, inner_ref, weight_ref,
     split_ref, mean_out_ref, gram_ref, state, depth, heights, scaled,
 ):
     lane = lane_iota()
@@ -180,7 +187,10 @@
     for row in range(ROWS):
         smalls = around(own_ref, near_ref, far_ref, block_at(row, SMALL))
         for which in range(4):
-            sides = around(own_ref, near_ref, far_ref, block_at(row, SIDE + which))
+            tiles = [SMALL] if which == 3 else range(TILES * which, TILES * (which + 1))
+            pairs = [by_side(near_ref[block_at(row, t), :], far_ref[block_at(row, t), :]) for t in tiles]
+            north, south = (side_tile(values) for values in zip(*pairs))
+            sides = (north, side_ref[pl.ds((row * 4 + which) * 8, 8), :], south)
             halos = around(halo_ref, near_halo_ref, far_halo_ref, pl.ds(((row // 2) * 4 + which) * 8, 8))
             for block, (small, side, halo) in enumerate(zip(smalls, sides, halos)):
                 at = ROWS * block + row
@@ -343,11 +353,17 @@
 ):
     assert factor.shape == (RANK, 3, ROWS, LANES)
     slots = obs_cells.shape[0]
-    block, even_edges, odd_edges, weights = pl.pallas_call(
+    block, sides, even_edges, odd_edges, weights = pl.pallas_call(
         pack_kernel,
-        out_shape=(chip(ROWS * PER_ROW * 8, LANES),) + (chip(ROWS * 8, LANES),) * 2 + (chip(2 * ROWS, LANES),),
+        out_shape=(
+            chip(ROWS * PER_ROW * 8, LANES),
+            chip(ROWS * 4 * 8, LANES),
+            chip(ROWS * 8, LANES),
+            chip(ROWS * 8, LANES),
+            chip(2 * ROWS, LANES),
+        ),
         in_specs=[VMEM] * 7,
-        out_specs=(VMEM,) * 4,
+        out_specs=(VMEM,) * 5,
         name="pack",
     )(
         factor.reshape(RANK * PLANES, LANES), background_expectation.reshape(PLANES, LANES), average_thickness,
@@ -385,7 +401,7 @@
             chip(PLANES, LANES),
             chip(8, LANES),
         ),
-        in_specs=[VMEM] * 8,
+        in_specs=[VMEM] * 9,
         out_specs=(VMEM,) * 3,
         scratch_shapes=[
             pltpu.VMEM((3, 3, 3 * ROWS, 8, LANES), jnp.float32),
@@ -394,7 +410,7 @@
             pltpu.VMEM((RANK + 8, ROWS * LANES), jnp.float32),
         ],
         name="side", compiler_params=SMALL_VMEM,
-    )(block, near, far, on_chip(halo), near_halo, far_halo, on_chip(inner), on_chip(weights))
+    )(block, on_chip(sides), near, far, on_chip(halo), near_halo, far_halo, on_chip(inner), on_chip(weights))
     gram = jnp.sum(sum_over(gram, "lat"), 0)
     parts = sum_over(gram, "lon")
     update, analysis = pl.pallas_call(

time: 67.4 us -> 68.6 us (1.018)
  Pallas kernels: 6.29 us -> 7.5 us
    pallas_call x1, Pallas kernels: 1.45 us -> 2.65 us  [per_device(): pl.pallas_call(side_kernel, out_shape=(pltpu.VMEM((3 * RANK, PLANES * LAN...]
where the time goes in v7:
time: 68.6 us; the launch traced here: 68.3 us
  blocking collectives  29.8 us (43%)
  starting transfers between devices  28.2 us (41%)
  Pallas kernels  7.5 us (11%)
  between operations  1.43 us (2%)
  waiting for transfers between devices  1.26 us (2%)
    all_to_all x2, blocking collectives, sum_over(): return lax.all_to_all(sent, axis, 0, 0)  29.8 us
    ppermute x6, starting transfers between devices, swapped(): return lax.ppermute(value, axis, pairs + [(j, i) for i, j in pairs])  28.2 us
    pallas_call x1, Pallas kernels, per_device(): pl.pallas_call(side_kernel, out_shape=(pltpu.VMEM((3 * RANK, PLANES * LAN...  2.65 us
    pallas_call x1, Pallas kernels, per_device(): pl.pallas_call(analysis_kernel, out_shape=(f32(PLANES, LANES), f32(RANK *...  2.12 us
    pallas_call x1, Pallas kernels, per_device(): pl.pallas_call(pack_kernel, out_shape=(chip(ROWS * PER_ROW * 8, LANES), c...  1.37 us
  transfers between devices with their start and end apart: 6, of which 1 were waited for; matrix products, arithmetic and copies ran while one was open for 0% of the time, Pallas kernels for 2%

profile of v7, /device:TPU:1, one launch (start us, length us, event | category | flops | bytes accessed | tf_op | source)
XLA Modules:
  0.0 68.3 jit_solution(13174771595611789141)
XLA Ops:
  1.3 1.4 %pack.1 = (f32[832,128]{1,0:T(8,128)S(1)}, f32[256,128]{1,0:T(8,128)S(1)}, f32[64,128]{1,0:T(8,128)S(1)}, f32[64,128]{1,0:T(8,128)S(1)}, f32[16,128]{1,0:T(8,128)S(1)}) custom-call(f32[768,128]{1,0:T(8,128)} %bitcast.19, f32[24,128]{1,0:T(8,128)} %bitcast.22, f32[8,128]{1,0:T(8,128)} %depth_ref.1, s32[1,1]{1,0:T(1,128)} %bitcast.15.count_ref, ...), custom_call_target="tpu_custom_call" | custom-call | tf_op jit(solution)/shard_map/pack/pallas_call | solution.py:356
  2.7 4.6 %collective-permute-start.1 = (f32[832,128]{1,0:T(8,128)S(1)}, f32[832,128]{1,0:T(8,128)S(1)}, u32[]{:S(2)}, u32[]{:S(2)}) collective-permute-start(f32[832,128]{1,0:T(8,128)S(1)} %get-tuple-element.12.own_ref), channel_id=1, source_target_pairs={{32,64},{96,128},{160,192},{224,256},{288,320},{352,384},{416,448}... | collective-permute-start | bytes 1277960 | tf_op jit(solution)/shard_map/ppermute | solution.py:342
  7.2 4.9 %collective-permute-start = (f32[832,128]{1,0:T(8,128)S(1)}, f32[832,128]{1,0:T(8,128)S(1)}, u32[]{:S(2)}, u32[]{:S(2)}) collective-permute-start(f32[832,128]{1,0:T(8,128)S(1)} %get-tuple-element.12.own_ref), channel_id=1, source_target_pairs={{0,32},{64,96},{128,160},{192,224},{256,288},{320,352},{384,416},{... | collective-permute-start | bytes 1277960 | tf_op jit(solution)/shard_map/ppermute | solution.py:342
  12.1 1.9 %collective-permute-start.2 = (f32[64,128]{1,0:T(8,128)S(1)}, f32[64,128]{1,0:T(8,128)S(1)}, u32[]{:S(2)}, u32[]{:S(2)}) collective-permute-start(f32[64,128]{1,0:T(8,128)S(1)} %get-tuple-element.14), channel_id=1, source_target_pairs={{0,1},{2,3},{4,5},{6,7},{8,9},{10,11},{12,13},{14,15},{16,17},{18,... | collective-permute-start | bytes 98312 | tf_op jit(solution)/shard_map/ppermute | solution.py:342
  14.0 10.2 %collective-permute-start.3 = (f32[64,128]{1,0:T(8,128)S(1)}, f32[64,128]{1,0:T(8,128)S(1)}, u32[]{:S(2)}, u32[]{:S(2)}) collective-permute-start(f32[64,128]{1,0:T(8,128)S(1)} %get-tuple-element.15), channel_id=1, source_target_pairs={{1,2},{3,4},{5,6},{7,8},{9,10},{11,12},{13,14},{15,16},{17,18},{19... | collective-permute-start | bytes 98312 | tf_op jit(solution)/shard_map/ppermute | solution.py:342
  24.3 0.0 collective-permute-done.2
  24.3 1.3 %collective-permute-done.3 = f32[64,128]{1,0:T(8,128)S(1)} collective-permute-done((f32[64,128]{1,0:T(8,128)S(1)}, f32[64,128]{1,0:T(8,128)S(1)}, u32[]{:S(2)}, u32[]{:S(2)}) %collective-permute-start.3) | collective-permute-done | bytes 32800 | tf_op jit(solution)/shard_map/ppermute | solution.py:342
  25.6 4.7 %collective-permute-start.5 = (f32[128,128]{1,0:T(8,128)S(1)}, f32[128,128]{1,0:T(8,128)S(1)}, u32[]{:S(2)}, u32[]{:S(2)}) collective-permute-start(f32[128,128]{1,0:T(8,128)S(1)} %bitcast.16), channel_id=1, source_target_pairs={{32,64},{96,128},{160,192},{224,256},{288,320},{352,384},{416,448}... | collective-permute-start | bytes 196616 | tf_op jit(solution)/shard_map/ppermute | solution.py:342
  30.3 1.9 %collective-permute-start.4 = (f32[128,128]{1,0:T(8,128)S(1)}, f32[128,128]{1,0:T(8,128)S(1)}, u32[]{:S(2)}, u32[]{:S(2)}) collective-permute-start(f32[128,128]{1,0:T(8,128)S(1)} %bitcast.17), channel_id=1, source_target_pairs={{0,32},{64,96},{128,160},{192,224},{256,288},{320,352},{384,416},{... | collective-permute-start | bytes 196616 | tf_op jit(solution)/shard_map/ppermute | solution.py:342
  32.2 0.0 collective-permute-done.1.far_ref
  32.2 0.0 collective-permute-done.near_ref
  32.2 1.4 %inner.1.inner_ref = f32[768,128]{1,0:T(8,128)S(1)} custom-call(f32[832,128]{1,0:T(8,128)S(1)} %get-tuple-element.12.own_ref, f32[832,128]{1,0:T(8,128)S(1)} %collective-permute-done.near_ref, f32[832,128]{1,0:T(8,128)S(1)} %collective-permute-done.1.far_ref), custom_call_target="tpu_custom_call" | custom-call | tf_op jit(solution)/shard_map/inner/pallas_call | solution.py:386
  33.6 0.0 collective-permute-done.5.far_halo_ref
  33.6 0.0 collective-permute-done.4.near_halo_ref
  33.6 2.6 %side.1 = (bf16[96,3072]{1,0:T(8,128)(2,1)S(1)}, f32[24,128]{1,0:T(8,128)S(1)}, f32[8,128]{1,0:T(8,128)S(1)}) custom-call(f32[832,128]{1,0:T(8,128)S(1)} %get-tuple-element.12.own_ref, f32[256,128]{1,0:T(8,128)S(1)} %get-tuple-element.13.side_ref, f32[832,128]{1,0:T(8,128)S(1)} %collective-permute-done.near_ref, ...), custom_call_target="tpu_custom_call" | custom-call | tf_op jit(solution)/shard_map/side/pallas_call | solution.py:397
  36.3 14.1 %all_to_all.10 = f32[16,8,128]{2,1,0:T(8,128)S(1)} all-to-all(f32[16,8,128]{2,1,0:T(8,128)S(1)} %broadcast_in_dim.4), channel_id=1, replica_groups=mesh['lat'=16,'lon'=32] {'lat'}, dimensions={0} | all-to-all | bytes 131072 | tf_op jit(solution)/shard_map/all_to_all | solution.py:348
  50.5 15.7 %all_to_all.11.parts_ref = f32[32,8,128]{2,1,0:T(8,128)S(1)} all-to-all(f32[32,8,128]{2,1,0:T(8,128)S(1)} %broadcast_in_dim.5), channel_id=1, replica_groups=mesh['lat'=16,'lon'=32] {'lon'}, dimensions={0} | all-to-all | bytes 262144 | tf_op jit(solution)/shard_map/all_to_all | solution.py:348
  66.2 2.1 %analysis.1 = (f32[24,128]{1,0:T(8,128)}, f32[768,128]{1,0:T(8,128)}) custom-call(f32[32,8,128]{2,1,0:T(8,128)S(1)} %all_to_all.11.parts_ref, bf16[96,3072]{1,0:T(8,128)(2,1)S(1)} %get-tuple-element.18.split_ref, f32[24,128]{1,0:T(8,128)S(1)} %get-tuple-element.19.mean_ref), custom_call_target="tpu_custom_call" | custom-call | tf_op jit(solution)/shard_map/analysis/pallas_call | solution.py:416
  (7 shorter events, 0.1 us)
Async XLA Ops:
  2.7 29.6 %collective-permute-start.1 = (f32[832,128]{1,0:T(8,128)S(1)}, f32[832,128]{1,0:T(8,128)S(1)}, u32[]{:S(2)}, u32[]{:S(2)}) collective-permute-start(f32[832,128]{1,0:T(8,128)S(1)} %get-tuple-element.12.own_ref), channel_id=1, source_target_pairs={{32,64},{96,128},{160,192},{224,256},{288,320},{352,384},{416,448}... | collective-permute-start | bytes 1277960 | tf_op jit(solution)/shard_map/ppermute | solution.py:342
  7.2 25.0 %collective-permute-start = (f32[832,128]{1,0:T(8,128)S(1)}, f32[832,128]{1,0:T(8,128)S(1)}, u32[]{:S(2)}, u32[]{:S(2)}) collective-permute-start(f32[832,128]{1,0:T(8,128)S(1)} %get-tuple-element.12.own_ref), channel_id=1, source_target_pairs={{0,32},{64,96},{128,160},{192,224},{256,288},{320,352},{384,416},{... | collective-permute-start | bytes 1277960 | tf_op jit(solution)/shard_map/ppermute | solution.py:342
  12.1 12.2 %collective-permute-start.2 = (f32[64,128]{1,0:T(8,128)S(1)}, f32[64,128]{1,0:T(8,128)S(1)}, u32[]{:S(2)}, u32[]{:S(2)}) collective-permute-start(f32[64,128]{1,0:T(8,128)S(1)} %get-tuple-element.14), channel_id=1, source_target_pairs={{0,1},{2,3},{4,5},{6,7},{8,9},{10,11},{12,13},{14,15},{16,17},{18,... | collective-permute-start | bytes 98312 | tf_op jit(solution)/shard_map/ppermute | solution.py:342
  14.0 11.5 %collective-permute-start.3 = (f32[64,128]{1,0:T(8,128)S(1)}, f32[64,128]{1,0:T(8,128)S(1)}, u32[]{:S(2)}, u32[]{:S(2)}) collective-permute-start(f32[64,128]{1,0:T(8,128)S(1)} %get-tuple-element.15), channel_id=1, source_target_pairs={{1,2},{3,4},{5,6},{7,8},{9,10},{11,12},{13,14},{15,16},{17,18},{19... | collective-permute-start | bytes 98312 | tf_op jit(solution)/shard_map/ppermute | solution.py:342
  25.6 8.1 %collective-permute-start.5 = (f32[128,128]{1,0:T(8,128)S(1)}, f32[128,128]{1,0:T(8,128)S(1)}, u32[]{:S(2)}, u32[]{:S(2)}) collective-permute-start(f32[128,128]{1,0:T(8,128)S(1)} %bitcast.16), channel_id=1, source_target_pairs={{32,64},{96,128},{160,192},{224,256},{288,320},{352,384},{416,448}... | collective-permute-start | bytes 196616 | tf_op jit(solution)/shard_map/ppermute | solution.py:342
  30.3 3.3 %collective-permute-start.4 = (f32[128,128]{1,0:T(8,128)S(1)}, f32[128,128]{1,0:T(8,128)S(1)}, u32[]{:S(2)}, u32[]{:S(2)}) collective-permute-start(f32[128,128]{1,0:T(8,128)S(1)} %bitcast.17), channel_id=1, source_target_pairs={{0,32},{64,96},{128,160},{192,224},{256,288},{320,352},{384,416},{... | collective-permute-start | bytes 196616 | tf_op jit(solution)/shard_map/ppermute | solution.py:342

commit v8 on v6

--- a/solution.py
+++ b/solution.py
@@ -19,6 +19,7 @@
 GROUP = LANES // TILES
 MAIN, SMALL, SIDE = 0, 12, 13
 PER_ROW = 17
+BLOCK = ROWS * PER_ROW * 8
 MOVES = (0, 16, 8, 24)
 PULL = 0.5 * TIME_STEP
 WIDTH = 8
@@ -38,7 +39,7 @@
     return pl.ds((row * PER_ROW + tile) * 8, 8)
 
 
-def observed(count_ref, cells_ref, values_ref, error_ref):
+def weight_kernel(count_ref, cells_ref, values_ref, error_ref, out_ref):
     slots = cells_ref.shape[1]
     live = lax.broadcasted_iota(jnp.int32, (1, slots), 1) < count_ref[...]
     weight = jnp.where(live, 1.0, 0.0) / error_ref[...]
@@ -51,19 +52,26 @@
         [jnp.where(in_row, square, 0.0), jnp.where(in_row, square * values_ref[...], 0.0)], 0
     )
     in_lane = lax.broadcasted_iota(jnp.int32, (LANES, slots), 0) == lane_of
-    return lax.dot_general(
+    out_ref[...] = lax.dot_general(
         spread, jnp.where(in_lane, 1.0, 0.0), NT, precision=HIGHEST, preferred_element_type=jnp.float32
     )
 
 
 def pack_kernel(
-    factor_ref, mean_ref, depth_ref, count_ref, cells_ref, values_ref, error_ref,
-    block_ref, even_edge_ref, odd_edge_ref, weight_ref,
+    factor_ref, mean_ref, depth_ref, cells_ref, values_ref, error_ref,
+    block_ref, near_block_ref, even_edge_ref, odd_edge_ref, cells_out_ref, values_out_ref, error_out_ref,
 ):
     lane = lane_iota()
     part = lane // GROUP
     octet = (lane // 8) & 3
-    weight_ref[...] = observed(count_ref, cells_ref, values_ref, error_ref)
+    cells_out_ref[...] = cells_ref[...]
+    values_out_ref[...] = values_ref[...]
+    error_out_ref[...] = error_ref[...]
+
+    def keep(row, tile, value):
+        block_ref[block_at(row, tile), :] = value
+        near_block_ref[block_at(row, tile), :] = value
+
     even = lax.rem(lax.axis_index("lon"), 2) == 0
     eastward, westward = {}, {}
     for row in range(ROWS):
@@ -72,13 +80,13 @@
             + [depth_ref[row : row + 1, :]] * 5,
             0,
         )
-        block_ref[block_at(row, SMALL), :] = small
+        keep(row, SMALL, small)
         sides = []
         for field in range(3):
             side = None
             for tile in range(TILES):
                 value = factor_ref[member_rows(field, row, tile), :]
-                block_ref[block_at(row, MAIN + TILES * field + tile), :] = value
+                keep(row, MAIN + TILES * field + tile, value)
                 moved = pltpu.roll(value, 16 + GROUP * tile, 1)
                 side = moved if side is None else jnp.where(part == tile, moved, side)
             sides.append(side)
@@ -86,7 +94,7 @@
         side = jnp.where(part == 0, side, pltpu.roll(side, GROUP, 1))
         sides.append(jnp.where(part < 2, side, pltpu.roll(side, 2 * GROUP, 1)))
         for which, side in enumerate(sides):
-            block_ref[block_at(row, SIDE + which), :] = side
+            keep(row, SIDE + which, side)
             move = MOVES[row % 4]
             moved = pltpu.roll(side, move, 1) if move else side
             if row % 4 == 0:
@@ -166,22 +174,22 @@
 
 
 def side_kernel(
-    own_ref, near_ref, far_ref, halo_ref, near_halo_ref, far_halo_ref, inner_ref, weight_ref,
+    own_ref, near_ref, far_ref, halo_ref, far_halo_ref, inner_ref, weight_ref,
     split_ref, mean_out_ref, gram_ref, state, depth, heights, scaled,
 ):
     lane = lane_iota()
     low_lanes = (lane & 16) == 0
     sub = lax.broadcasted_iota(jnp.int32, (8, LANES), 0)
 
-    def around(own, near, far, at):
-        north, south = by_side(near[at, :], far[at, :])
+    def around(own, near, far, at, below=0):
+        north, south = by_side(near[pl.ds(below + at.start, 8), :], far[at, :])
         return north, own[at, :], south
 
     for row in range(ROWS):
         smalls = around(own_ref, near_ref, far_ref, block_at(row, SMALL))
         for which in range(4):
             sides = around(own_ref, near_ref, far_ref, block_at(row, SIDE + which))
-            halos = around(halo_ref, near_halo_ref, far_halo_ref, pl.ds(((row // 2) * 4 + which) * 8, 8))
+            halos = around(halo_ref, near_ref, far_halo_ref, pl.ds(((row // 2) * 4 + which) * 8, 8), BLOCK)
             for block, (small, side, halo) in enumerate(zip(smalls, sides, halos)):
                 at = ROWS * block + row
                 if MOVES[row % 4]:
@@ -343,21 +351,31 @@
 ):
     assert factor.shape == (RANK, 3, ROWS, LANES)
     slots = obs_cells.shape[0]
-    block, even_edges, odd_edges, weights = pl.pallas_call(
+    block, near_block, even_edges, odd_edges, cells, values, error = pl.pallas_call(
         pack_kernel,
-        out_shape=(chip(ROWS * PER_ROW * 8, LANES),) + (chip(ROWS * 8, LANES),) * 2 + (chip(2 * ROWS, LANES),),
-        in_specs=[VMEM] * 7,
-        out_specs=(VMEM,) * 4,
+        out_shape=(
+            chip(BLOCK, LANES),
+            chip(BLOCK + ROWS * 16, LANES),
+            chip(ROWS * 8, LANES),
+            chip(ROWS * 8, LANES),
+            pltpu.VMEM((1, slots), jnp.int32),
+            chip(1, slots),
+            chip(1, slots),
+        ),
+        in_specs=[VMEM] * 6,
+        out_specs=(VMEM,) * 7,
         name="pack",
     )(
         factor.reshape(RANK * PLANES, LANES), background_expectation.reshape(PLANES, LANES), average_thickness,
-        obs_count.reshape(1, 1), obs_cells.reshape(1, slots), obs_values.reshape(1, slots), obs_error.reshape(1, slots),
+        obs_cells.reshape(1, slots), obs_values.reshape(1, slots), obs_error.reshape(1, slots),
     )
     block = on_chip(block)
-    even_edges = swapped(even_edges, "lon", 0, True)
     odd_edges = swapped(odd_edges, "lon", 1, True)
     far = on_chip(swapped(block, "lat", 1, False))
-    near = on_chip(swapped(block, "lat", 0, False))
+    even_edges = swapped(even_edges, "lon", 0, True)
+    weights = pl.pallas_call(
+        weight_kernel, out_shape=chip(2 * ROWS, LANES), in_specs=[VMEM] * 4, out_specs=VMEM, name="weigh"
+    )(obs_count.reshape(1, 1), on_chip(cells), on_chip(values), on_chip(error))
     shape = (ROWS // 4, 4 * 8, LANES)
     eastern = (lax.broadcasted_iota(jnp.int32, shape, 2) & 8) // 8 != 1
     from_even = eastern == (lax.rem(lax.axis_index("lon"), 2) == 0)
@@ -366,7 +384,8 @@
         [jnp.where(from_even, even_edges, odd_edges), jnp.where(from_even, odd_edges, even_edges)], 1
     ).reshape(ROWS * 16, LANES)
     far_halo = on_chip(swapped(halo, "lat", 1, False))
-    near_halo = on_chip(swapped(halo, "lat", 0, False))
+    near_block = lax.dynamic_update_slice(near_block, halo, (BLOCK, 0))
+    near = on_chip(swapped(near_block, "lat", 0, False))
     inner = pl.pallas_call(
         inner_kernel,
         out_shape=chip(RANK * PLANES, LANES),
@@ -385,7 +404,7 @@
             chip(PLANES, LANES),
             chip(8, LANES),
         ),
-        in_specs=[VMEM] * 8,
+        in_specs=[VMEM] * 7,
         out_specs=(VMEM,) * 3,
         scratch_shapes=[
             pltpu.VMEM((3, 3, 3 * ROWS, 8, LANES), jnp.float32),
@@ -394,7 +413,7 @@
             pltpu.VMEM((RANK + 8, ROWS * LANES), jnp.float32),
         ],
         name="side", compiler_params=SMALL_VMEM,
-    )(block, near, far, on_chip(halo), near_halo, far_halo, on_chip(inner), on_chip(weights))
+    )(block, near, far, on_chip(halo), far_halo, on_chip(inner), on_chip(weights))
     gram = jnp.sum(sum_over(gram, "lat"), 0)
     parts = sum_over(gram, "lon")
     update, analysis = pl.pallas_call(

time: 67.4 us -> 70.7 us (1.049)
  waiting for transfers between devices: 1.26 us -> 5.63 us
  starting transfers between devices: 28.2 us -> 25.2 us
  blocking collectives: 29.8 us -> 31.6 us
    ppermute x6 -> x5, waiting for transfers between devices: 1.26 us -> 5.63 us  [swapped(): return lax.ppermute(value, axis, pairs + [(j, i) for i, j in pairs])]
    ppermute x6 -> x5, starting transfers between devices: 28.2 us -> 25.2 us  [swapped(): return lax.ppermute(value, axis, pairs + [(j, i) for i, j in pairs])]
    all_to_all x2, blocking collectives: 29.8 us -> 31.6 us  [sum_over(): return lax.all_to_all(sent, axis, 0, 0)]
    pallas_call x1 -> x2, Pallas kernels: 1.37 us -> 1.62 us  [the longest x1 1.37 us: per_device(): pl.pallas_call(pack_kernel, out_shape=(chip(BLOCK, LANES), chip(BLOCK + R...]
  transfers between devices with their start and end apart: 6 -> 5, of which waited for: 1 -> 2; matrix products, arithmetic and copies ran while one was open for 0% -> 0% of each run, Pallas kernels for 2% -> 2%
where the time goes in v8:
time: 70.7 us; the launch traced here: 70.4 us
  blocking collectives  31.6 us (45%)
  starting transfers between devices  25.2 us (36%)
  Pallas kernels  6.56 us (9%)
  waiting for transfers between devices  5.63 us (8%)
  between operations  1.39 us (2%)
    all_to_all x2, blocking collectives, sum_over(): return lax.all_to_all(sent, axis, 0, 0)  31.6 us
    ppermute x5, starting transfers between devices, swapped(): return lax.ppermute(value, axis, pairs + [(j, i) for i, j in pairs])  25.2 us
    ppermute x5, waiting for transfers between devices, swapped(): return lax.ppermute(value, axis, pairs + [(j, i) for i, j in pairs])  5.63 us
    pallas_call x1, Pallas kernels, per_device(): pl.pallas_call(analysis_kernel, out_shape=(f32(PLANES, LANES), f32(RANK *...  2.12 us
    pallas_call x1, Pallas kernels, per_device(): pl.pallas_call(side_kernel, out_shape=(pltpu.VMEM((3 * RANK, PLANES * LAN...  1.46 us
  transfers between devices with their start and end apart: 5, of which 2 were waited for; matrix products, arithmetic and copies ran while one was open for 0% of the time, Pallas kernels for 2%

profile of v8, /device:TPU:1, one launch (start us, length us, event | category | flops | bytes accessed | tf_op | source)
XLA Modules:
  0.0 70.4 jit_solution(10615451820336725932)
XLA Ops:
  0.6 1.4 %pack.1 = (f32[1088,128]{1,0:T(8,128)S(1)}, f32[1216,128]{1,0:T(8,128)S(1)}, f32[64,128]{1,0:T(8,128)S(1)}, f32[64,128]{1,0:T(8,128)S(1)}, s32[1,256]{1,0:T(1,12...) custom-call(f32[768,128]{1,0:T(8,128)} %bitcast.19, f32[24,128]{1,0:T(8,128)} %bitcast.22, f32[8,128]{1,0:T(8,128)} %depth_ref.1, ...), custom_call_target="tpu_custom_call" | custom-call | tf_op jit(solution)/shard_map/pack/pallas_call | solution.py:354
  2.0 4.8 %collective-permute-start = (f32[64,128]{1,0:T(8,128)S(1)}, f32[64,128]{1,0:T(8,128)S(1)}, u32[]{:S(2)}, u32[]{:S(2)}) collective-permute-start(f32[64,128]{1,0:T(8,128)S(1)} %get-tuple-element.16), channel_id=1, source_target_pairs={{0,1},{2,3},{4,5},{6,7},{8,9},{10,11},{12,13},{14,15},{16,17},{18,... | collective-permute-start | bytes 98312 | tf_op jit(solution)/shard_map/ppermute | solution.py:340
  6.8 11.0 %collective-permute-start.1 = (f32[64,128]{1,0:T(8,128)S(1)}, f32[64,128]{1,0:T(8,128)S(1)}, u32[]{:S(2)}, u32[]{:S(2)}) collective-permute-start(f32[64,128]{1,0:T(8,128)S(1)} %get-tuple-element.17), channel_id=1, source_target_pairs={{1,2},{3,4},{5,6},{7,8},{9,10},{11,12},{13,14},{15,16},{17,18},{19... | collective-permute-start | bytes 98312 | tf_op jit(solution)/shard_map/ppermute | solution.py:340
  17.9 0.0 collective-permute-done
  17.9 1.3 %collective-permute-done.1 = f32[64,128]{1,0:T(8,128)S(1)} collective-permute-done((f32[64,128]{1,0:T(8,128)S(1)}, f32[64,128]{1,0:T(8,128)S(1)}, u32[]{:S(2)}, u32[]{:S(2)}) %collective-permute-start.1) | collective-permute-done | bytes 32800 | tf_op jit(solution)/shard_map/ppermute | solution.py:340
  19.2 3.7 %collective-permute-start.2 = (f32[1216,128]{1,0:T(8,128)S(1)}, f32[1216,128]{1,0:T(8,128)S(1)}, u32[]{:S(2)}, u32[]{:S(2)}) collective-permute-start(f32[1216,128]{1,0:T(8,128)S(1)} %constant_dynamic-update-slice_fusion), channel_id=1, source_target_pairs={{0,32},{64,96},{128,160},{192,224},{256,288},{320,352},{384,416},{... | collective-permute-start | bytes 1867784 | tf_op jit(solution)/shard_map/ppermute | solution.py:340
  23.0 3.1 %collective-permute-start.3 = (f32[1088,128]{1,0:T(8,128)S(1)}, f32[1088,128]{1,0:T(8,128)S(1)}, u32[]{:S(2)}, u32[]{:S(2)}) collective-permute-start(f32[1088,128]{1,0:T(8,128)S(1)} %get-tuple-element.14.own_ref), channel_id=1, source_target_pairs={{32,64},{96,128},{160,192},{224,256},{288,320},{352,384},{416,448}... | collective-permute-start | bytes 1671176 | tf_op jit(solution)/shard_map/ppermute | solution.py:340
  26.1 2.5 %collective-permute-start.4 = (f32[128,128]{1,0:T(8,128)S(1)}, f32[128,128]{1,0:T(8,128)S(1)}, u32[]{:S(2)}, u32[]{:S(2)}) collective-permute-start(f32[128,128]{1,0:T(8,128)S(1)} %bitcast.17), channel_id=1, source_target_pairs={{32,64},{96,128},{160,192},{224,256},{288,320},{352,384},{416,448}... | collective-permute-start | bytes 196616 | tf_op jit(solution)/shard_map/ppermute | solution.py:340
  29.2 0.3 weigh.1.weight_ref
  29.4 4.4 %collective-permute-done.3.far_ref = f32[1088,128]{1,0:T(8,128)S(1)} collective-permute-done((f32[1088,128]{1,0:T(8,128)S(1)}, f32[1088,128]{1,0:T(8,128)S(1)}, u32[]{:S(2)}, u32[]{:S(2)}) %collective-permute-start.3) | collective-permute-done | bytes 557088 | tf_op jit(solution)/shard_map/ppermute | solution.py:340
  33.8 0.0 collective-permute-done.2.near_ref
  33.8 1.4 %inner.1.inner_ref = f32[768,128]{1,0:T(8,128)S(1)} custom-call(f32[1088,128]{1,0:T(8,128)S(1)} %get-tuple-element.14.own_ref, f32[1216,128]{1,0:T(8,128)S(1)} %collective-permute-done.2.near_ref, f32[1088,128]{1,0:T(8,128)S(1)} %collective-permute-done.3.far_ref), custom_call_target="tpu_custom_call" | custom-call | tf_op jit(solution)/shard_map/inner/pallas_call | solution.py:389
  35.2 0.0 collective-permute-done.4.far_halo_ref
  35.2 1.5 %side.1 = (bf16[96,3072]{1,0:T(8,128)(2,1)S(1)}, f32[24,128]{1,0:T(8,128)S(1)}, f32[8,128]{1,0:T(8,128)S(1)}) custom-call(f32[1088,128]{1,0:T(8,128)S(1)} %get-tuple-element.14.own_ref, f32[1216,128]{1,0:T(8,128)S(1)} %collective-permute-done.2.near_ref, f32[1088,128]{1,0:T(8,128)S(1)} %collective-permute-done.3.far_ref, f32[128,128]{1,0:T(8,128)S(1)} %bitcast.18, ...), custom_call_target="tpu_custom_call" | custom-call | tf_op jit(solution)/shard_map/side/pallas_call | solution.py:400
  36.7 15.9 %all_to_all.10 = f32[16,8,128]{2,1,0:T(8,128)S(1)} all-to-all(f32[16,8,128]{2,1,0:T(8,128)S(1)} %broadcast_in_dim.4), channel_id=1, replica_groups=mesh['lat'=16,'lon'=32] {'lat'}, dimensions={0} | all-to-all | bytes 131072 | tf_op jit(solution)/shard_map/all_to_all | solution.py:346
  52.6 15.7 %all_to_all.11.parts_ref = f32[32,8,128]{2,1,0:T(8,128)S(1)} all-to-all(f32[32,8,128]{2,1,0:T(8,128)S(1)} %broadcast_in_dim.5), channel_id=1, replica_groups=mesh['lat'=16,'lon'=32] {'lon'}, dimensions={0} | all-to-all | bytes 262144 | tf_op jit(solution)/shard_map/all_to_all | solution.py:346
  68.3 2.1 %analysis.1 = (f32[24,128]{1,0:T(8,128)}, f32[768,128]{1,0:T(8,128)}) custom-call(f32[32,8,128]{2,1,0:T(8,128)S(1)} %all_to_all.11.parts_ref, bf16[96,3072]{1,0:T(8,128)(2,1)S(1)} %get-tuple-element.22.split_ref, f32[24,128]{1,0:T(8,128)S(1)} %get-tuple-element.23.mean_ref), custom_call_target="tpu_custom_call" | custom-call | tf_op jit(solution)/shard_map/analysis/pallas_call | solution.py:419
  (8 shorter events, 0.1 us)
Async XLA Ops:
  2.0 15.9 %collective-permute-start = (f32[64,128]{1,0:T(8,128)S(1)}, f32[64,128]{1,0:T(8,128)S(1)}, u32[]{:S(2)}, u32[]{:S(2)}) collective-permute-start(f32[64,128]{1,0:T(8,128)S(1)} %get-tuple-element.16), channel_id=1, source_target_pairs={{0,1},{2,3},{4,5},{6,7},{8,9},{10,11},{12,13},{14,15},{16,17},{18,... | collective-permute-start | bytes 98312 | tf_op jit(solution)/shard_map/ppermute | solution.py:340
  6.8 12.3 %collective-permute-start.1 = (f32[64,128]{1,0:T(8,128)S(1)}, f32[64,128]{1,0:T(8,128)S(1)}, u32[]{:S(2)}, u32[]{:S(2)}) collective-permute-start(f32[64,128]{1,0:T(8,128)S(1)} %get-tuple-element.17), channel_id=1, source_target_pairs={{1,2},{3,4},{5,6},{7,8},{9,10},{11,12},{13,14},{15,16},{17,18},{19... | collective-permute-start | bytes 98312 | tf_op jit(solution)/shard_map/ppermute | solution.py:340
  19.2 14.6 %collective-permute-start.2 = (f32[1216,128]{1,0:T(8,128)S(1)}, f32[1216,128]{1,0:T(8,128)S(1)}, u32[]{:S(2)}, u32[]{:S(2)}) collective-permute-start(f32[1216,128]{1,0:T(8,128)S(1)} %constant_dynamic-update-slice_fusion), channel_id=1, source_target_pairs={{0,32},{64,96},{128,160},{192,224},{256,288},{320,352},{384,416},{... | collective-permute-start | bytes 1867784 | tf_op jit(solution)/shard_map/ppermute | solution.py:340
  23.0 10.9 %collective-permute-start.3 = (f32[1088,128]{1,0:T(8,128)S(1)}, f32[1088,128]{1,0:T(8,128)S(1)}, u32[]{:S(2)}, u32[]{:S(2)}) collective-permute-start(f32[1088,128]{1,0:T(8,128)S(1)} %get-tuple-element.14.own_ref), channel_id=1, source_target_pairs={{32,64},{96,128},{160,192},{224,256},{288,320},{352,384},{416,448}... | collective-permute-start | bytes 1671176 | tf_op jit(solution)/shard_map/ppermute | solution.py:340
  26.1 9.1 %collective-permute-start.4 = (f32[128,128]{1,0:T(8,128)S(1)}, f32[128,128]{1,0:T(8,128)S(1)}, u32[]{:S(2)}, u32[]{:S(2)}) collective-permute-start(f32[128,128]{1,0:T(8,128)S(1)} %bitcast.17), channel_id=1, source_target_pairs={{32,64},{96,128},{160,192},{224,256},{288,320},{352,384},{416,448}... | collective-permute-start | bytes 196616 | tf_op jit(solution)/shard_map/ppermute | solution.py:340

commit v9 on v8

--- a/solution.py
+++ b/solution.py
@@ -59,7 +59,7 @@
 
 def pack_kernel(
     factor_ref, mean_ref, depth_ref, cells_ref, values_ref, error_ref,
-    block_ref, near_block_ref, even_edge_ref, odd_edge_ref, cells_out_ref, values_out_ref, error_out_ref,
+    block_ref, even_edge_ref, odd_edge_ref, cells_out_ref, values_out_ref, error_out_ref,
 ):
     lane = lane_iota()
     part = lane // GROUP
@@ -67,11 +67,6 @@
     cells_out_ref[...] = cells_ref[...]
     values_out_ref[...] = values_ref[...]
     error_out_ref[...] = error_ref[...]
-
-    def keep(row, tile, value):
-        block_ref[block_at(row, tile), :] = value
-        near_block_ref[block_at(row, tile), :] = value
-
     even = lax.rem(lax.axis_index("lon"), 2) == 0
     eastward, westward = {}, {}
     for row in range(ROWS):
@@ -80,13 +75,13 @@
             + [depth_ref[row : row + 1, :]] * 5,
             0,
         )
-        keep(row, SMALL, small)
+        block_ref[block_at(row, SMALL), :] = small
         sides = []
         for field in range(3):
             side = None
             for tile in range(TILES):
                 value = factor_ref[member_rows(field, row, tile), :]
-                keep(row, MAIN + TILES * field + tile, value)
+                block_ref[block_at(row, MAIN + TILES * field + tile), :] = value
                 moved = pltpu.roll(value, 16 + GROUP * tile, 1)
                 side = moved if side is None else jnp.where(part == tile, moved, side)
             sides.append(side)
@@ -94,7 +89,7 @@
         side = jnp.where(part == 0, side, pltpu.roll(side, GROUP, 1))
         sides.append(jnp.where(part < 2, side, pltpu.roll(side, 2 * GROUP, 1)))
         for which, side in enumerate(sides):
-            keep(row, SIDE + which, side)
+            block_ref[block_at(row, SIDE + which), :] = side
             move = MOVES[row % 4]
             moved = pltpu.roll(side, move, 1) if move else side
             if row % 4 == 0:
@@ -174,22 +169,22 @@
 
 
 def side_kernel(
-    own_ref, near_ref, far_ref, halo_ref, far_halo_ref, inner_ref, weight_ref,
+    own_ref, near_ref, far_ref, halo_ref, near_halo_ref, far_halo_ref, inner_ref, weight_ref,
     split_ref, mean_out_ref, gram_ref, state, depth, heights, scaled,
 ):
     lane = lane_iota()
     low_lanes = (lane & 16) == 0
     sub = lax.broadcasted_iota(jnp.int32, (8, LANES), 0)
 
-    def around(own, near, far, at, below=0):
-        north, south = by_side(near[pl.ds(below + at.start, 8), :], far[at, :])
+    def around(own, near, far, at):
+        north, south = by_side(near[at, :], far[at, :])
         return north, own[at, :], south
 
     for row in range(ROWS):
         smalls = around(own_ref, near_ref, far_ref, block_at(row, SMALL))
         for which in range(4):
             sides = around(own_ref, near_ref, far_ref, block_at(row, SIDE + which))
-            halos = around(halo_ref, near_ref, far_halo_ref, pl.ds(((row // 2) * 4 + which) * 8, 8), BLOCK)
+            halos = around(halo_ref, near_halo_ref, far_halo_ref, pl.ds(((row // 2) * 4 + which) * 8, 8))
             for block, (small, side, halo) in enumerate(zip(smalls, sides, halos)):
                 at = ROWS * block + row
                 if MOVES[row % 4]:
@@ -351,11 +346,10 @@
 ):
     assert factor.shape == (RANK, 3, ROWS, LANES)
     slots = obs_cells.shape[0]
-    block, near_block, even_edges, odd_edges, cells, values, error = pl.pallas_call(
+    block, even_edges, odd_edges, cells, values, error = pl.pallas_call(
         pack_kernel,
         out_shape=(
             chip(BLOCK, LANES),
-            chip(BLOCK + ROWS * 16, LANES),
             chip(ROWS * 8, LANES),
             chip(ROWS * 8, LANES),
             pltpu.VMEM((1, slots), jnp.int32),
@@ -363,7 +357,7 @@
             chip(1, slots),
         ),
         in_specs=[VMEM] * 6,
-        out_specs=(VMEM,) * 7,
+        out_specs=(VMEM,) * 6,
         name="pack",
     )(
         factor.reshape(RANK * PLANES, LANES), background_expectation.reshape(PLANES, LANES), average_thickness,
@@ -373,6 +367,7 @@
     odd_edges = swapped(odd_edges, "lon", 1, True)
     far = on_chip(swapped(block, "lat", 1, False))
     even_edges = swapped(even_edges, "lon", 0, True)
+    near = on_chip(swapped(block, "lat", 0, False))
     weights = pl.pallas_call(
         weight_kernel, out_shape=chip(2 * ROWS, LANES), in_specs=[VMEM] * 4, out_specs=VMEM, name="weigh"
     )(obs_count.reshape(1, 1), on_chip(cells), on_chip(values), on_chip(error))
@@ -384,8 +379,7 @@
         [jnp.where(from_even, even_edges, odd_edges), jnp.where(from_even, odd_edges, even_edges)], 1
     ).reshape(ROWS * 16, LANES)
     far_halo = on_chip(swapped(halo, "lat", 1, False))
-    near_block = lax.dynamic_update_slice(near_block, halo, (BLOCK, 0))
-    near = on_chip(swapped(near_block, "lat", 0, False))
+    near_halo = on_chip(swapped(halo, "lat", 0, False))
     inner = pl.pallas_call(
         inner_kernel,
         out_shape=chip(RANK * PLANES, LANES),
@@ -404,7 +398,7 @@
             chip(PLANES, LANES),
             chip(8, LANES),
         ),
-        in_specs=[VMEM] * 7,
+        in_specs=[VMEM] * 8,
         out_specs=(VMEM,) * 3,
         scratch_shapes=[
             pltpu.VMEM((3, 3, 3 * ROWS, 8, LANES), jnp.float32),
@@ -413,7 +407,7 @@
             pltpu.VMEM((RANK + 8, ROWS * LANES), jnp.float32),
         ],
         name="side", compiler_params=SMALL_VMEM,
-    )(block, near, far, on_chip(halo), far_halo, on_chip(inner), on_chip(weights))
+    )(block, near, far, on_chip(halo), near_halo, far_halo, on_chip(inner), on_chip(weights))
     gram = jnp.sum(sum_over(gram, "lat"), 0)
     parts = sum_over(gram, "lon")
     update, analysis = pl.pallas_call(

time: 70.7 us -> 67 us (0.948)
  waiting for transfers between devices: 5.63 us -> 1.27 us
  starting transfers between devices: 25.2 us -> 28.2 us
  blocking collectives: 31.6 us -> 29.1 us
    ppermute x5 -> x6, waiting for transfers between devices: 5.63 us -> 1.27 us  [swapped(): return lax.ppermute(value, axis, pairs + [(j, i) for i, j in pairs])]
    ppermute x5 -> x6, starting transfers between devices: 25.2 us -> 28.2 us  [swapped(): return lax.ppermute(value, axis, pairs + [(j, i) for i, j in pairs])]
    all_to_all x2, blocking collectives: 31.6 us -> 29.1 us  [sum_over(): return lax.all_to_all(sent, axis, 0, 0)]
  transfers between devices with their start and end apart: 5 -> 6, of which waited for: 2 -> 1; matrix products, arithmetic and copies ran while one was open for 0% -> 0% of each run, Pallas kernels for 2% -> 2%
where the time goes in v9:
time: 67 us; the launch traced here: 66.6 us
  blocking collectives  29.1 us (43%)
  starting transfers between devices  28.2 us (42%)
  Pallas kernels  6.55 us (10%)
  between operations  1.41 us (2%)
  waiting for transfers between devices  1.27 us (2%)
    all_to_all x2, blocking collectives, sum_over(): return lax.all_to_all(sent, axis, 0, 0)  29.1 us
    ppermute x6, starting transfers between devices, swapped(): return lax.ppermute(value, axis, pairs + [(j, i) for i, j in pairs])  28.2 us
    pallas_call x1, Pallas kernels, per_device(): pl.pallas_call(analysis_kernel, out_shape=(f32(PLANES, LANES), f32(RANK *...  2.12 us
    pallas_call x1, Pallas kernels, per_device(): pl.pallas_call(side_kernel, out_shape=(pltpu.VMEM((3 * RANK, PLANES * LAN...  1.46 us
    pallas_call x1, Pallas kernels, per_device(): pl.pallas_call(pack_kernel, out_shape=(chip(BLOCK, LANES), chip(ROWS * 8,...  1.36 us
    pallas_call x1, Pallas kernels, per_device(): pl.pallas_call(inner_kernel, out_shape=chip(RANK * PLANES, LANES), in_spe...  1.36 us
  transfers between devices with their start and end apart: 6, of which 1 were waited for; matrix products, arithmetic and copies ran while one was open for 0% of the time, Pallas kernels for 2%

profile of v9, /device:TPU:1, one launch (start us, length us, event | category | flops | bytes accessed | tf_op | source)
XLA Modules:
  0.0 66.6 jit_solution(15481358033401341030)
XLA Ops:
  0.6 1.4 %pack.1 = (f32[1088,128]{1,0:T(8,128)S(1)}, f32[64,128]{1,0:T(8,128)S(1)}, f32[64,128]{1,0:T(8,128)S(1)}, s32[1,256]{1,0:T(1,128)S(1)}, f32[1,256]{1,0:T(1,128)S(1)}, /*index=5*/f32[1,256]{1,0:T(1,128)S(1)}) custom-call(f32[768,128]{1,0:T(8,128)} %bitcast.19, f32[24,128]{1,0:T(8,128)} %bitcast.22, f32[8,128]{1,0:T(8,128)} %depth_ref.1, s32[1,256]{1,0:T(1,128)} %bitcast.23, ...), custom_call_target="tpu_custom_call" | custom-call | tf_op jit(solution)/shard_map/pack/pallas_call | solution.py:349
  2.0 4.6 %collective-permute-start.1 = (f32[1088,128]{1,0:T(8,128)S(1)}, f32[1088,128]{1,0:T(8,128)S(1)}, u32[]{:S(2)}, u32[]{:S(2)}) collective-permute-start(f32[1088,128]{1,0:T(8,128)S(1)} %get-tuple-element.13.own_ref), channel_id=1, source_target_pairs={{32,64},{96,128},{160,192},{224,256},{288,320},{352,384},{416,448}... | collective-permute-start | bytes 1671176 | tf_op jit(solution)/shard_map/ppermute | solution.py:335
  6.6 4.9 %collective-permute-start = (f32[1088,128]{1,0:T(8,128)S(1)}, f32[1088,128]{1,0:T(8,128)S(1)}, u32[]{:S(2)}, u32[]{:S(2)}) collective-permute-start(f32[1088,128]{1,0:T(8,128)S(1)} %get-tuple-element.13.own_ref), channel_id=1, source_target_pairs={{0,32},{64,96},{128,160},{192,224},{256,288},{320,352},{384,416},{... | collective-permute-start | bytes 1671176 | tf_op jit(solution)/shard_map/ppermute | solution.py:335
  11.5 1.9 %collective-permute-start.2 = (f32[64,128]{1,0:T(8,128)S(1)}, f32[64,128]{1,0:T(8,128)S(1)}, u32[]{:S(2)}, u32[]{:S(2)}) collective-permute-start(f32[64,128]{1,0:T(8,128)S(1)} %get-tuple-element.14), channel_id=1, source_target_pairs={{0,1},{2,3},{4,5},{6,7},{8,9},{10,11},{12,13},{14,15},{16,17},{18,... | collective-permute-start | bytes 98312 | tf_op jit(solution)/shard_map/ppermute | solution.py:335
  13.4 10.2 %collective-permute-start.3 = (f32[64,128]{1,0:T(8,128)S(1)}, f32[64,128]{1,0:T(8,128)S(1)}, u32[]{:S(2)}, u32[]{:S(2)}) collective-permute-start(f32[64,128]{1,0:T(8,128)S(1)} %get-tuple-element.15), channel_id=1, source_target_pairs={{1,2},{3,4},{5,6},{7,8},{9,10},{11,12},{13,14},{15,16},{17,18},{19... | collective-permute-start | bytes 98312 | tf_op jit(solution)/shard_map/ppermute | solution.py:335
  23.6 0.0 collective-permute-done.2
  23.6 1.3 %collective-permute-done.3 = f32[64,128]{1,0:T(8,128)S(1)} collective-permute-done((f32[64,128]{1,0:T(8,128)S(1)}, f32[64,128]{1,0:T(8,128)S(1)}, u32[]{:S(2)}, u32[]{:S(2)}) %collective-permute-start.3) | collective-permute-done | bytes 32800 | tf_op jit(solution)/shard_map/ppermute | solution.py:335
  24.9 4.7 %collective-permute-start.5 = (f32[128,128]{1,0:T(8,128)S(1)}, f32[128,128]{1,0:T(8,128)S(1)}, u32[]{:S(2)}, u32[]{:S(2)}) collective-permute-start(f32[128,128]{1,0:T(8,128)S(1)} %bitcast.16), channel_id=1, source_target_pairs={{32,64},{96,128},{160,192},{224,256},{288,320},{352,384},{416,448}... | collective-permute-start | bytes 196616 | tf_op jit(solution)/shard_map/ppermute | solution.py:335
  29.6 1.9 %collective-permute-start.4 = (f32[128,128]{1,0:T(8,128)S(1)}, f32[128,128]{1,0:T(8,128)S(1)}, u32[]{:S(2)}, u32[]{:S(2)}) collective-permute-start(f32[128,128]{1,0:T(8,128)S(1)} %bitcast.17), channel_id=1, source_target_pairs={{0,32},{64,96},{128,160},{192,224},{256,288},{320,352},{384,416},{... | collective-permute-start | bytes 196616 | tf_op jit(solution)/shard_map/ppermute | solution.py:335
  32.2 0.3 weigh.1.weight_ref
  32.5 0.0 collective-permute-done.1.far_ref
  32.5 0.0 collective-permute-done.near_ref
  32.5 1.4 %inner.1.inner_ref = f32[768,128]{1,0:T(8,128)S(1)} custom-call(f32[1088,128]{1,0:T(8,128)S(1)} %get-tuple-element.13.own_ref, f32[1088,128]{1,0:T(8,128)S(1)} %collective-permute-done.near_ref, f32[1088,128]{1,0:T(8,128)S(1)} %collective-permute-done.1.far_ref), custom_call_target="tpu_custom_call" | custom-call | tf_op jit(solution)/shard_map/inner/pallas_call | solution.py:383
  33.9 0.0 collective-permute-done.5.far_halo_ref
  33.9 0.0 collective-permute-done.4.near_halo_ref
  33.9 1.5 %side.1 = (bf16[96,3072]{1,0:T(8,128)(2,1)S(1)}, f32[24,128]{1,0:T(8,128)S(1)}, f32[8,128]{1,0:T(8,128)S(1)}) custom-call(f32[1088,128]{1,0:T(8,128)S(1)} %get-tuple-element.13.own_ref, f32[1088,128]{1,0:T(8,128)S(1)} %collective-permute-done.near_ref, f32[1088,128]{1,0:T(8,128)S(1)} %collective-permute-done.1.far_ref, f32[128,128]{1,0:T(8,128)S(1)} %bitcast.18, ...), custom_call_target="tpu_custom_call" | custom-call | tf_op jit(solution)/shard_map/side/pallas_call | solution.py:394
  35.4 13.7 %all_to_all.10 = f32[16,8,128]{2,1,0:T(8,128)S(1)} all-to-all(f32[16,8,128]{2,1,0:T(8,128)S(1)} %broadcast_in_dim.4), channel_id=1, replica_groups=mesh['lat'=16,'lon'=32] {'lat'}, dimensions={0} | all-to-all | bytes 131072 | tf_op jit(solution)/shard_map/all_to_all | solution.py:341
  49.1 15.4 %all_to_all.11.parts_ref = f32[32,8,128]{2,1,0:T(8,128)S(1)} all-to-all(f32[32,8,128]{2,1,0:T(8,128)S(1)} %broadcast_in_dim.5), channel_id=1, replica_groups=mesh['lat'=16,'lon'=32] {'lon'}, dimensions={0} | all-to-all | bytes 262144 | tf_op jit(solution)/shard_map/all_to_all | solution.py:341
  64.5 2.1 %analysis.1 = (f32[24,128]{1,0:T(8,128)}, f32[768,128]{1,0:T(8,128)}) custom-call(f32[32,8,128]{2,1,0:T(8,128)S(1)} %all_to_all.11.parts_ref, bf16[96,3072]{1,0:T(8,128)(2,1)S(1)} %get-tuple-element.20.split_ref, f32[24,128]{1,0:T(8,128)S(1)} %get-tuple-element.21.mean_ref), custom_call_target="tpu_custom_call" | custom-call | tf_op jit(solution)/shard_map/analysis/pallas_call | solution.py:413
  (7 shorter events, 0.1 us)
Async XLA Ops:
  2.0 30.5 %collective-permute-start.1 = (f32[1088,128]{1,0:T(8,128)S(1)}, f32[1088,128]{1,0:T(8,128)S(1)}, u32[]{:S(2)}, u32[]{:S(2)}) collective-permute-start(f32[1088,128]{1,0:T(8,128)S(1)} %get-tuple-element.13.own_ref), channel_id=1, source_target_pairs={{32,64},{96,128},{160,192},{224,256},{288,320},{352,384},{416,448}... | collective-permute-start | bytes 1671176 | tf_op jit(solution)/shard_map/ppermute | solution.py:335
  6.6 25.9 %collective-permute-start = (f32[1088,128]{1,0:T(8,128)S(1)}, f32[1088,128]{1,0:T(8,128)S(1)}, u32[]{:S(2)}, u32[]{:S(2)}) collective-permute-start(f32[1088,128]{1,0:T(8,128)S(1)} %get-tuple-element.13.own_ref), channel_id=1, source_target_pairs={{0,32},{64,96},{128,160},{192,224},{256,288},{320,352},{384,416},{... | collective-permute-start | bytes 1671176 | tf_op jit(solution)/shard_map/ppermute | solution.py:335
  11.5 12.2 %collective-permute-start.2 = (f32[64,128]{1,0:T(8,128)S(1)}, f32[64,128]{1,0:T(8,128)S(1)}, u32[]{:S(2)}, u32[]{:S(2)}) collective-permute-start(f32[64,128]{1,0:T(8,128)S(1)} %get-tuple-element.14), channel_id=1, source_target_pairs={{0,1},{2,3},{4,5},{6,7},{8,9},{10,11},{12,13},{14,15},{16,17},{18,... | collective-permute-start | bytes 98312 | tf_op jit(solution)/shard_map/ppermute | solution.py:335
  13.4 11.5 %collective-permute-start.3 = (f32[64,128]{1,0:T(8,128)S(1)}, f32[64,128]{1,0:T(8,128)S(1)}, u32[]{:S(2)}, u32[]{:S(2)}) collective-permute-start(f32[64,128]{1,0:T(8,128)S(1)} %get-tuple-element.15), channel_id=1, source_target_pairs={{1,2},{3,4},{5,6},{7,8},{9,10},{11,12},{13,14},{15,16},{17,18},{19... | collective-permute-start | bytes 98312 | tf_op jit(solution)/shard_map/ppermute | solution.py:335
  24.9 9.0 %collective-permute-start.5 = (f32[128,128]{1,0:T(8,128)S(1)}, f32[128,128]{1,0:T(8,128)S(1)}, u32[]{:S(2)}, u32[]{:S(2)}) collective-permute-start(f32[128,128]{1,0:T(8,128)S(1)} %bitcast.16), channel_id=1, source_target_pairs={{32,64},{96,128},{160,192},{224,256},{288,320},{352,384},{416,448}... | collective-permute-start | bytes 196616 | tf_op jit(solution)/shard_map/ppermute | solution.py:335
  29.6 4.2 %collective-permute-start.4 = (f32[128,128]{1,0:T(8,128)S(1)}, f32[128,128]{1,0:T(8,128)S(1)}, u32[]{:S(2)}, u32[]{:S(2)}) collective-permute-start(f32[128,128]{1,0:T(8,128)S(1)} %bitcast.17), channel_id=1, source_target_pairs={{0,32},{64,96},{128,160},{192,224},{256,288},{320,352},{384,416},{... | collective-permute-start | bytes 196616 | tf_op jit(solution)/shard_map/ppermute | solution.py:335
